TPU v7x, 128 devices: a whole 4x4x4 slice. The times are simulated.
128 devices in a mesh: grp: 4 (over z_lo, core), cell: 32 (over y, z_hi, x).
Axes of the slice: x: 4, y: 4, z: 4 (z_hi: 2, z_lo: 2; z = z_hi * 2 + z_lo), core: 2. Of those that a mesh axis runs over, the one named last changes fastest.
Arguments:
- theta: float32 [128, 256, 2048], P('grp', 'cell'), may hold values from 0.5 to 1.5
- density: float32 [128, 256, 2048], P('grp', 'cell'), may hold values from 0.05 to 0.8
- footprint: int32 [65536, 8], P('cell'), may hold values from 0 to 524287, as said below
- perturbed: float32 [128, 65536], P(None, 'cell'), may hold values from 0 to 6.4
- noise_var: float32 [65536], P('cell'), may hold values from 0.1 to 1
Outputs:
- theta_new: float32 [128, 256, 2048], P('grp', 'cell')
- predicted: float32 [128, 65536], P(None, 'cell')
Inputs may be any that keep to these rules, and one draw needn't show every extreme that they name: `footprint`: each sensor's 8 cells form a patch of 2 neighbouring grid rows by 4 neighbouring columns, listed row by row; for the sensors numbered d * 2048 to (d + 1) * 2048 - 1 the patch's upper row is among grid rows d * 8 to (d + 1) * 8 - 1.
All inputs are finite; a program needn't handle non-finite values.
Results may differ from a plain program's by a relative error of at most 0.000082.
Values sent between devices are 32-bit elements; how exact they have to be, the bound alone decides.
No kernel may reach another device: no remote copies, remote signals or barrier semaphores. Data moves between devices by JAX's collectives and lax.ppermute only.
A program may use at most 128 MiB of HBM per device.

v0:
```python
import jax
import jax.numpy as jnp
from jax import lax
from jax.sharding import PartitionSpec as P

STEPS = 2


def with_halo(block, sides, width):
    for axis, dim in sides:
        count = lax.axis_size(axis)
        forward = [(i, i + 1) for i in range(count - 1)]
        backward = [(target, source) for source, target in forward]
        low = lax.ppermute(
            lax.slice_in_dim(block, block.shape[dim] - width, None, axis=dim), axis, forward
        )
        high = lax.ppermute(lax.slice_in_dim(block, 0, width, axis=dim), axis, backward)
        block = jnp.concatenate([low, block, high], axis=dim)
    return block


def from_behind(value, axis, steps):
    count = lax.axis_size(axis)
    initial, last = (max(0, -steps), min(count, count - steps))
    return lax.ppermute(value, axis, [(source, source + steps) for source in range(initial, last)])


def advance(rho, speed_pad):
    edged = with_halo(rho, (("cell", 1),), 1)
    padded = jnp.pad(edged, ((0, 0), (0, 0), (1, 1)))
    flux_pad = speed_pad * padded * (1.0 - padded)
    center = flux_pad[:, 1:-1, 1:-1]
    flux = 2.0 * center - flux_pad[:, :-2, 1:-1] - flux_pad[:, 1:-1, :-2]
    spread = (
        padded[:, 2:, 1:-1]
        + padded[:, :-2, 1:-1]
        + padded[:, 1:-1, 2:]
        + padded[:, 1:-1, :-2]
        - 4.0 * rho
    )
    return rho - 0.2 * flux + 0.1 * spread


def masked_counts(flat, local, slab):
    inside = (local >= 0) & (local < slab)
    values = jnp.take(flat, jnp.clip(local, 0, slab - 1), axis=1)
    return jnp.sum(jnp.where(inside[None], values, 0.0), axis=2)


def body(theta, density, footprint, perturbed, noise_var):
    members, rows, columns = theta.shape
    total_members = members * lax.axis_size("grp")
    above = from_behind(theta[:, -1:, :], "cell", 1)
    speed_edged = jnp.concatenate([above, theta, jnp.zeros_like(above)], axis=1)
    speed_pad = jnp.pad(speed_edged, ((0, 0), (0, 0), (1, 1)))
    rho = density
    for step in range(STEPS):
        rho = advance(rho, speed_pad)
    slab = rows * columns
    flat = rho.reshape(members, slab)
    position = lax.axis_index("cell")
    local = footprint - position * slab
    own_counts = masked_counts(flat, local, slab)
    prior = from_behind(footprint, "cell", 1)
    prior_local = prior - position * slab
    prior_local = jnp.where(position > 0, prior_local, -1)
    prior_counts = masked_counts(flat, prior_local, slab)
    received = from_behind(prior_counts, "cell", -1)
    mine = own_counts + received
    predicted = lax.all_gather(mine, "grp", axis=0, tiled=True)
    anomaly = predicted - jnp.mean(predicted, axis=0)
    weighted = anomaly / noise_var
    gram_p = jnp.dot(
        weighted, anomaly.T, precision=lax.Precision.HIGHEST, preferred_element_type=jnp.float32
    )
    gram_q = jnp.dot(
        weighted,
        (perturbed - predicted).T,
        precision=lax.Precision.HIGHEST,
        preferred_element_type=jnp.float32,
    )
    gram_p, gram_q = lax.psum((gram_p, gram_q), "cell")
    system = (total_members - 1.0) * jnp.eye(total_members, dtype=jnp.float32) + gram_p
    factor = jnp.linalg.cholesky(system)
    mixing = jax.scipy.linalg.cho_solve((factor, True), gram_q)
    first = lax.axis_index("grp") * members
    own_columns = lax.dynamic_slice_in_dim(mixing, first, members, 1)
    piece = lax.all_gather(theta, "grp", axis=0, tiled=True)
    acc = jnp.zeros_like(theta)
    acc = acc + jnp.einsum("ij,ixy->jxy", own_columns, piece, precision=lax.Precision.HIGHEST)
    acc, running = (acc, jnp.sum(piece, axis=0))
    center_field = running / total_members
    update = acc - jnp.sum(own_columns, axis=0)[:, None, None] * center_field[None]
    return (theta + update, predicted)


def solution(mesh):
    return jax.shard_map(
        body,
        mesh=mesh,
        in_specs=(
            P("grp", "cell", None),
            P("grp", "cell", None),
            P("cell", None),
            P(None, "cell"),
            P("cell"),
        ),
        out_specs=(P("grp", "cell", None), P(None, "cell")),
        check_vma=False,
    )
```

profile of v0, /device:TPU:22, one launch (start us, length us, event | category | flops | bytes accessed | tf_op | source)
XLA Modules:
  0.0 681.3 jit_solution(4605378840053234020)
XLA Ops:
  7.2 2.8 copy.92
  11.4 5.7 collective-permute-start
  17.1 2.8 copy.79
  20.8 3.4 collective-permute-start.1
  26.6 7.0 %collective-permute-start.5 = (s32[2048,8]{0,1:T(8,128)}, s32[2048,8]{0,1:T(8,128)}, u32[]{:S(2)}, u32[]{:S(2)}) collective-permute-start(s32[2048,8]{0,1:T(8,128)} %param.9), channel_id=1, source_target_pairs={{0,1},{1,2},{2,3},{3,4},{4,5},{5,6},{6,7},{7,8},{8,9},{9,10},{10,1... | collective-permute-start | bytes 196616 | tf_op jit(solution)/shard_map/ppermute | solution.py:25
  44.3 2.5 subtract_multiply_fusion.1
  46.7 2.7 fusion.12
  49.5 5.6 collective-permute-start.3
  59.0 8.0 %collective-permute-done.4 = f32[32,1,2048]{2,0,1:T(8,128)S(1)} collective-permute-done((f32[32,1,2048]{2,0,1:T(8,128)S(1)}, f32[32,1,2048]{2,0,1:T(8,128)S(1)}, u32[]{:S(2)}, u32[]{:S(2)}) %collective-permute-start.4) | collective-permute-done | bytes 262176 | tf_op jit(solution)/shard_map/ppermute | solution.py:17
  68.5 2.8 fusion.6
  71.3 6.3 copy.83
  77.6 57.7 %gather_fusion.1 = f32[16384,32]{1,0:T(8,128)} fusion(f32[32,16384]{0,1:T(8,128)} %bitcast.35, s32[16384]{0:T(1024)S(1)} %broadcast_clamp_fusion), kind=kCustom, calls=%fused_computation.1.clone | custom fusion | bytes 4259840 | tf_op jit(solution)/shard_map/jit(_take)/gather | solution.py:46
  135.3 12.6 %fusion = f32[32,2048]{0,1:T(8,128)S(1)} fusion(f32[16384,32]{1,0:T(8,128)} %gather_fusion.1, pred[2048,8]{1,0:T(8,128)(4,1)S(1)} %copy.86, pred[2048,8]{1,0:T(8,128)(4,1)S(1)} %copy.85), kind=kLoop, calls=%fused_computation.3 | loop fusion | flops 1507328 | bytes 2392064 | tf_op jit(solution)/shard_map/reduce_sum | solution.py:47
  150.3 57.7 %gather_fusion = f32[16384,32]{1,0:T(8,128)} fusion(f32[32,16384]{0,1:T(8,128)} %bitcast.36, s32[16384]{0:T(1024)S(1)} %broadcast_clamp_fusion.1), kind=kCustom, calls=%fused_computation.clone | custom fusion | bytes 4259840 | tf_op jit(solution)/shard_map/jit(_take)/gather | solution.py:46
  208.1 12.6 %fusion.1 = f32[32,2048]{0,1:T(8,128)S(1)} fusion(f32[16384,32]{1,0:T(8,128)} %gather_fusion, pred[2048,8]{1,0:T(8,128)(4,1)S(1)} %copy-done.4, pred[2048,8]{1,0:T(8,128)(4,1)S(1)} %copy-done.3), kind=kLoop, calls=%fused_computation.6 | loop fusion | flops 1507328 | bytes 2392064 | tf_op jit(solution)/shard_map/reduce_sum | solution.py:47
  221.8 23.3 %all-gather.3.cloned.1.call-done = f32[128,2048]{1,0:T(8,128)} async-done(((f32[32,2048]{1,0:T(8,128)}), f32[128,2048]{1,0:T(8,128)}) %all-gather.3.cloned.1.call-update) | async-done | bytes 1048592 | tf_op jit(solution)/shard_map/all_gather | solution.py:70
  246.5 3.4 fusion.18
  252.4 312.9 %all-reduce.6.cloned.1.call-done = (f32[128,128]{1,0:T(8,128)}, f32[128,128]{1,0:T(8,128)}) async-done(((f32[128,128]{1,0:T(8,128)}, f32[128,128]{1,0:T(8,128)}), (f32[128,128]{1,0:T(8,128)}, f32[128,128]{1,0:T(8,128)})) %all-reduce.6.cloned.1.call-update) | async-done | bytes 131088 | tf_op jit(solution)/shard_map/psum | solution.py:82
  567.1 11.7 %cholesky.16 = f32[128,128]{1,0:T(8,128)S(1)} custom-call(f32[128,128]{1,0:T(8,128)S(1)} %fusion.29), custom_call_target="Cholesky" | custom-call | tf_op jit(solution)/shard_map/jit(cholesky)/cholesky | solution.py:84
  580.2 9.8 %custom-call.10 = f32[1,128,128]{1,2,0:T(8,128)S(1)} custom-call(f32[1,128,128]{2,1,0:T(8,128)S(1)} %fusion.24), custom_call_target="InvertDiagBlocksLowerTriangular" | custom-call | tf_op jit(solution)/shard_map/jit(_cho_solve)/triangular_solve | solution.py:85
  591.6 68.1 %all-gather.5.cloned.1.call-done = f32[128,8,2048]{2,0,1:T(8,128)} async-done(((f32[32,8,2048]{2,0,1:T(8,128)}), f32[128,8,2048]{2,0,1:T(8,128)}) %all-gather.5.cloned.1.call-update) | async-done | bytes 8388624 | tf_op jit(solution)/shard_map/all_gather | solution.py:88
  659.6 4.1 reduce_sum.49
  663.8 7.5 %fusion.3 = f32[32,8,2048]{2,0,1:T(8,128)S(1)} fusion(f32[128,8,2048]{2,0,1:T(8,128)} %all-gather.5.cloned.1.call-done, f32[8,2048]{1,0:T(8,128)S(1)} %broadcast_multiply_fusion, f32[32]{0:T(128)S(1)} %dynamic-slice_reduce_fusion, f32[128,128]{0,1:T(8,128)S(1)} %fusion.25, s32[]{:T(128)S(6)} %select_n.34, f32[32,8,2048]{2,1,0:T(8,128)S(1)} %copy-done.1), kind=kOutput, calls=%fused_computation.18 | convolution fusion | flops 806879232 | bytes 12665348 | tf_op jit(solution)/shard_map/ij,ixy->jxy/dot_general | solution.py:90
  671.3 2.5 copy.93
  (64 shorter events, 33.6 us)
Async XLA Ops:
  7.2 238.0 %all-gather.3.cloned.1.call-start = ((), (), s32[]{:S(2)}) async-start(), calls=%async_computation | async-start | bytes 1310720 | tf_op jit(solution)/shard_map/all_gather | solution.py:70
  10.0 1.4 copy-start
  11.4 30.7 %collective-permute-start = (f32[32,1,2048]{2,0,1:T(8,128)}, f32[32,1,2048]{2,0,1:T(8,128)}, u32[]{:S(2)}, u32[]{:S(2)}) collective-permute-start(f32[32,1,2048]{2,0,1:T(8,128)} %slice.106), channel_id=1, source_target_pairs={{0,1},{1,2},{2,3},{3,4},{4,5},{5,6},{6,7},{7,8},{8,9},{9,10},{10,1... | collective-permute-start | bytes 786440 | tf_op jit(solution)/shard_map/ppermute | solution.py:25
  20.8 23.5 %collective-permute-start.1 = (f32[32,1,2048]{2,0,1:T(8,128)}, f32[32,1,2048]{2,0,1:T(8,128)S(1)}, u32[]{:S(2)}, u32[]{:S(2)}) collective-permute-start(f32[32,1,2048]{2,0,1:T(8,128)} %get-tuple-element.25), channel_id=1, source_target_pairs={{0,1},{1,2},{2,3},{3,4},{4,5},{5,6},{6,7},{7,8},{8,9},{9,10},{10,1... | collective-permute-start | bytes 786440 | tf_op jit(solution)/shard_map/ppermute | solution.py:14
  24.2 20.1 %collective-permute-start.2 = (f32[32,1,2048]{2,0,1:T(8,128)}, f32[32,1,2048]{2,0,1:T(8,128)}, u32[]{:S(2)}, u32[]{:S(2)}) collective-permute-start(f32[32,1,2048]{2,0,1:T(8,128)} %get-tuple-element.26), channel_id=1, source_target_pairs={{1,0},{2,1},{3,2},{4,3},{5,4},{6,5},{7,6},{8,7},{9,8},{10,9},{11,1... | collective-permute-start | bytes 786440 | tf_op jit(solution)/shard_map/ppermute | solution.py:17
  26.6 11.6 %collective-permute-start.5 = (s32[2048,8]{0,1:T(8,128)}, s32[2048,8]{0,1:T(8,128)}, u32[]{:S(2)}, u32[]{:S(2)}) collective-permute-start(s32[2048,8]{0,1:T(8,128)} %param.9), channel_id=1, source_target_pairs={{0,1},{1,2},{2,3},{3,4},{4,5},{5,6},{6,7},{7,8},{8,9},{9,10},{10,1... | collective-permute-start | bytes 196616 | tf_op jit(solution)/shard_map/ppermute | solution.py:25
  49.5 9.4 %collective-permute-start.3 = (f32[32,1,2048]{2,0,1:T(8,128)S(1)}, f32[32,1,2048]{2,0,1:T(8,128)S(1)}, u32[]{:S(2)}, u32[]{:S(2)}) collective-permute-start(f32[32,1,2048]{2,0,1:T(8,128)S(1)} %get-tuple-element.23), channel_id=1, source_target_pairs={{0,1},{1,2},{2,3},{3,4},{4,5},{5,6},{6,7},{7,8},{8,9},{9,10},{10,1... | collective-permute-start | bytes 786440 | tf_op jit(solution)/shard_map/ppermute | solution.py:14
  55.1 11.9 %collective-permute-start.4 = (f32[32,1,2048]{2,0,1:T(8,128)S(1)}, f32[32,1,2048]{2,0,1:T(8,128)S(1)}, u32[]{:S(2)}, u32[]{:S(2)}) collective-permute-start(f32[32,1,2048]{2,0,1:T(8,128)S(1)} %get-tuple-element.24), channel_id=1, source_target_pairs={{1,0},{2,1},{3,2},{4,3},{5,4},{6,5},{7,6},{8,7},{9,8},{10,9},{11,1... | collective-permute-start | bytes 786440 | tf_op jit(solution)/shard_map/ppermute | solution.py:17
  148.2 59.8 %copy-start.3 = (pred[2048,8]{1,0:T(8,128)(4,1)S(1)}, pred[2048,8]{1,0:T(8,128)(4,1)}, u32[]{:S(2)}) copy-start(pred[2048,8]{1,0:T(8,128)(4,1)} %copy.72) | copy-start | bytes 49156
  148.2 59.8 %copy-start.4 = (pred[2048,8]{1,0:T(8,128)(4,1)S(1)}, pred[2048,8]{1,0:T(8,128)(4,1)}, u32[]{:S(2)}) copy-start(pred[2048,8]{1,0:T(8,128)(4,1)} %copy.73) | copy-start | bytes 49156
  148.3 72.8 %collective-permute-start.6 = (f32[32,2048]{1,0:T(8,128)S(1)}, f32[32,2048]{1,0:T(8,128)S(1)}, u32[]{:S(2)}, u32[]{:S(2)}) collective-permute-start(f32[32,2048]{1,0:T(8,128)S(1)} %copy.88), channel_id=1, source_target_pairs={{1,0},{2,1},{3,2},{4,3},{5,4},{6,5},{7,6},{8,7},{9,8},{10,9},{11,1... | collective-permute-start | bytes 786440 | tf_op jit(solution)/shard_map/ppermute | solution.py:25
  220.7 25.8 %copy-start.6 = (f32[2048]{0:T(1024)S(1)}, f32[2048]{0:T(1024)}, u32[]{:S(2)}) copy-start(f32[2048]{0:T(1024)} %param.11) | copy-start | bytes 24580
  221.8 343.5 %all-reduce.6.cloned.1.call-start = ((), (), s32[]{:S(2)}) async-start(), calls=%async_computation.2 | async-start | bytes 262144 | tf_op jit(solution)/shard_map/psum | solution.py:82
  246.5 3.4 copy-start.2
  246.5 3.4 copy-start.5
  251.7 407.9 %all-gather.5.cloned.1.call-start = ((), (), s32[]{:S(2)}) async-start(), calls=%async_computation.1 | async-start | bytes 10485760 | tf_op jit(solution)/shard_map/all_gather | solution.py:88
  591.6 72.2 %copy-start.1 = (f32[32,8,2048]{2,1,0:T(8,128)S(1)}, f32[32,8,2048]{2,1,0:T(8,128)}, u32[]{:S(2)}) copy-start(f32[32,8,2048]{2,1,0:T(8,128)} %param.7) | copy-start | bytes 6291460
Sparse Core Ops, SparseCore 0:
  221.9 23.2 all-gather.2
  251.8 313.4 all-reduce.5
  567.6 92.0 all-gather.4
where the time goes:
time: 685 us; the launch traced here: 681 us
  waiting for transfers between devices  415 us (61%)
  local copies, waits for them, and re-layouts  140 us (20%)
  other arithmetic  70.1 us (10%)
  starting transfers between devices  28.6 us (4%)
  matrix products  14.1 us (2%)
  between operations  14.1 us (2%)
    psum x1, waiting for transfers between devices, body(): gram_p, gram_q = lax.psum((gram_p, gram_q), 'cell')  313 us
    gather x2, local copies, waits for them, and re-layouts, masked_counts(): values = jnp.take(flat, jnp.clip(local, 0, slab - 1), axis=1)  115 us
    all_gather x1, waiting for transfers between devices, body(): piece = lax.all_gather(theta, 'grp', axis=0, tiled=True)  68.1 us
    reduce_sum x2, other arithmetic, masked_counts(): return jnp.sum(jnp.where(inside[None], values, 0.0), axis=2)  25.2 us
    all_gather x1, waiting for transfers between devices, body(): predicted = lax.all_gather(mine, 'grp', axis=0, tiled=True)  23.3 us
    ppermute x3, starting transfers between devices, from_behind(): lax.ppermute(value, axis, [(source, source + steps) for source in range(i...  14.8 us
  transfers between devices with their start and end apart: 10, of which 5 were waited for; matrix products, arithmetic and copies ran while one was open for 16% of the time, Pallas kernels for 0%

commit v1 on v0

v1 whole, which is shorter than its diff:
```python
import functools

import jax
import jax.numpy as jnp
from jax import lax
from jax.experimental import pallas as pl
from jax.experimental.pallas import tpu as pltpu
from jax.sharding import PartitionSpec as P

LANES = 128
F32 = jnp.float32


def along(axis, shift):
    count = lax.axis_size(axis)
    return [(i, i + shift) for i in range(count) if 0 <= i + shift < count]


def swapped(axis, bit):
    return [(i, i ^ bit) for i in range(lax.axis_size(axis))]


def vmem_params():
    return pltpu.CompilerParams(vmem_limit_bytes=56 * 1024 * 1024)


def outflow(speed, rho):
    return 0.2 * (speed * rho * (1.0 - rho)) + 0.1 * rho


def from_left(x):
    lane = lax.broadcasted_iota(jnp.int32, x.shape, 1)
    return jnp.where(lane == 0, 0.0, pltpu.roll(x, 1, 1))


def from_right(x):
    last = x.shape[1] - 1
    lane = lax.broadcasted_iota(jnp.int32, x.shape, 1)
    return jnp.where(lane == last, 0.0, pltpu.roll(x, last, 1))


def without_above(rho, out, below):
    return 0.8 * rho - 2.0 * out + from_left(out) + 0.1 * (below + from_right(rho))


def box4(x):
    n = x.shape[1]
    pair = x + pltpu.roll(x, n - 1, 1)
    return pair + pltpu.roll(pair, n - 2, 1)


def load_columns(source, target, sems):
    copies = []
    for b in range(source.shape[1] // LANES):
        copy = pltpu.make_async_copy(source.at[:, pl.ds(b * LANES, LANES)], target.at[b], sems.at[b])
        copy.start()
        copies.append(copy)
    return copies


def prep_kernel(members, rows, theta, rho, theta_t, rho_t, down, top, theta_in, rho_in, sems):
    waits = load_columns(rho, rho_in, sems.at[0]), load_columns(theta, theta_in, sems.at[1])
    for b in range(theta_in.shape[0]):
        at = slice(b * LANES, (b + 1) * LANES)
        waits[0][b].wait()
        waits[1][b].wait()
        for r in range(rows):
            speed = theta_in[b, pl.ds(r, members, stride=rows), :]
            now = rho_in[b, pl.ds(r, members, stride=rows), :]
            theta_t[r, :, at] = speed
            rho_t[r, :, at] = now
            if r == 0:
                top[:, at] = now
            if r == rows - 1:
                down[:, at] = outflow(speed, now)


def step1_kernel(theta, rho, above, below, rho1, down, top, part):
    rows, members, _ = rho.shape

    def chunk(c, carry):
        at = pl.ds(c * 8, 8)
        up = above[at, :]
        kept = None
        for r in range(rows):
            now = rho[r, at, :]
            under = rho[r + 1, at, :] if r + 1 < rows else below[at, :]
            speed = theta[r, at, :]
            out = outflow(speed, now)
            new = without_above(now, out, under) + up
            rho1[r, at, :] = new
            up = out
            if r == 0:
                top[at, :] = new
                kept = (new, outflow(speed, new))
            if r == 1:
                part[at, :] = without_above(kept[0], kept[1], new)
            if r == rows - 1:
                down[at, :] = outflow(speed, new)
        return carry

    lax.fori_loop(0, members // 8, chunk, 0)


def pick(table, first, count, pos_ref, start, out_ref):
    members = out_ref.shape[0]
    groups = pos_ref.shape[0]
    width = 4
    for g0 in range(0, groups, width):
        where = [jnp.broadcast_to(pos_ref[g : g + 1, :], (8, LANES)) for g in range(g0, g0 + width)]
        lane = [w & (LANES - 1) for w in where]
        block = [w >> 7 for w in where]
        init = tuple(
            start[m : m + 8, g * LANES : (g + 1) * LANES] if start is not None else jnp.zeros((8, LANES), F32)
            for g in range(g0, g0 + width)
            for m in range(0, members, 8)
        )

        def look(p, acc):
            rows = [table[p, m : m + 8, :] for m in range(0, members, 8)]
            new = []
            for k in range(width):
                hit = block[k] == p + first
                for i, row in enumerate(rows):
                    got = jnp.take_along_axis(row, lane[k], axis=1, mode="promise_in_bounds")
                    new.append(jnp.where(hit, got, acc[k * len(rows) + i]))
            return tuple(new)

        acc = lax.fori_loop(0, count, look, init, unroll=2)
        for k in range(width):
            for i in range(members // 8):
                g = g0 + k
                out_ref[i * 8 : i * 8 + 8, g * LANES : (g + 1) * LANES] = acc[k * (members // 8) + i]


def step2_kernel(theta, rho, above, below, pos, counts, rest, table):
    rows, members, columns = rho.shape
    blocks = columns // LANES

    def chunk(c, carry):
        at = pl.ds(c * 8, 8)
        up = above[at, :]
        last = None
        for r in range(rows):
            now = rho[r, at, :]
            under = rho[r + 1, at, :] if r + 1 < rows else below[at, :]
            out = outflow(theta[r, at, :], now)
            new = without_above(now, out, under) + up
            up = out
            if r > 0:
                sums = box4(last + new)
                for b in range(blocks):
                    table[(r - 1) * blocks + b, at, :] = sums[:, b * LANES : (b + 1) * LANES]
            if r == rows - 1:
                rest[at, :] = new + out
            last = new
        return carry

    lax.fori_loop(0, members // 8, chunk, 0)
    pick(table, 0, (rows - 1) * blocks, pos, None, counts)


def finish_kernel(first, rest, part, pos, counts, mine, table):
    members, columns = rest.shape
    blocks = columns // LANES
    for c in range(0, members, 8):
        sums = box4(rest[c : c + 8, :] + part[c : c + 8, :])
        for b in range(blocks):
            table[b, c : c + 8, :] = sums[:, b * LANES : (b + 1) * LANES]
    pick(table, first, blocks, pos, counts, mine)


def product_kernel(total, g_ref, own, core, chip, both, perturbed, noise, predicted, packed):
    members, sensors = own.shape
    g = g_ref[0]
    for step, piece in enumerate((own, core, chip, both)):
        predicted[pl.ds(pl.multiple_of((g ^ step) * members, members), members), :] = piece[...]
    width = 512
    acc = None
    for s in range(0, sensors, width):
        at = slice(s, s + width)
        all_counts = predicted[:, at]
        anomaly = all_counts - jnp.sum(all_counts, axis=0, keepdims=True) / total
        weighted = anomaly / noise[:, at]
        left = jnp.concatenate([anomaly, perturbed[:, at] - own[:, at]], axis=0)
        term = lax.dot_general(
            left, weighted, (((1,), (1,)), ((), ())), precision=lax.Precision.HIGHEST, preferred_element_type=F32
        )
        acc = term if acc is None else acc + term
    packed[...] = acc


def split(x):
    high = x.astype(jnp.bfloat16)
    return high, (x - high.astype(F32)).astype(jnp.bfloat16)


def update_kernel(rows, g_ref, mixing, own, core, chip, both, out, fields, new, sems, out_sems):
    members = own.shape[0] // rows
    g = g_ref[0]
    waits = [load_columns(piece, fields.at[k], sems.at[k]) for k, piece in enumerate((own, core, chip, both))]
    w = jnp.concatenate(
        [mixing[pl.ds(pl.multiple_of((g ^ step) * members, members), members), :] for step in range(4)], axis=0
    )
    wt = w.T
    wh, wl = split(wt)
    sent = []
    for b in range(new.shape[0]):
        for k in range(4):
            waits[k][b].wait()
        for r in range(rows):
            at = pl.ds(r, members, stride=rows)
            x = [fields[k, b, at, :] for k in range(4)]
            xh, xl = split(jnp.concatenate(x, axis=0))
            add = (
                jnp.dot(wh, xh, preferred_element_type=F32)
                + jnp.dot(wh, xl, preferred_element_type=F32)
                + jnp.dot(wl, xh, preferred_element_type=F32)
            )
            new[b, at, :] = x[0] + add
        copy = pltpu.make_async_copy(new.at[b], out.at[:, pl.ds(b * LANES, LANES)], out_sems.at[b])
        copy.start()
        sent.append(copy)
    for copy in sent:
        copy.wait()


def body(theta, density, footprint, perturbed, noise_var):
    members, rows, columns = theta.shape
    total = members * lax.axis_size("grp")
    sensors = footprint.shape[0]
    slab = rows * columns
    blocks = columns // LANES
    flat_theta = theta.reshape(members * rows, columns)
    flat_rho = density.reshape(members * rows, columns)
    g = lax.axis_index("grp").astype(jnp.int32).reshape(1)
    pos = (footprint[:, 0] - lax.axis_index("cell") * slab).reshape(sensors // LANES, LANES)

    row = jax.ShapeDtypeStruct((members, columns), F32)
    turned = jax.ShapeDtypeStruct((rows, members, columns), F32)
    anywhere = pl.BlockSpec(memory_space=pl.ANY)
    columns_of = pltpu.VMEM((blocks, members * rows, LANES), F32)
    theta_t, rho_t, down, top = pl.pallas_call(
        functools.partial(prep_kernel, members, rows),
        in_specs=[anywhere, anywhere],
        out_shape=[turned, turned, row, row],
        scratch_shapes=[columns_of, columns_of, pltpu.SemaphoreType.DMA((2, blocks))],
        name="prep",
        compiler_params=vmem_params(),
    )(flat_theta, flat_rho)

    above = lax.ppermute(down, "cell", along("cell", 1))
    below = lax.ppermute(top, "cell", along("cell", -1))
    rho1, down, top, part = pl.pallas_call(
        step1_kernel,
        out_shape=[turned, row, row, row],
        name="step1",
        compiler_params=vmem_params(),
    )(theta_t, rho_t, above, below)

    above = lax.ppermute(down, "cell", along("cell", 1))
    below = lax.ppermute(top, "cell", along("cell", -1))
    part = lax.ppermute(part, "cell", along("cell", -1))
    counts_shape = jax.ShapeDtypeStruct((members, sensors), F32)
    counts, rest = pl.pallas_call(
        step2_kernel,
        out_shape=[counts_shape, row],
        scratch_shapes=[pltpu.VMEM(((rows - 1) * blocks, members, LANES), F32)],
        name="step2",
        compiler_params=vmem_params(),
    )(theta_t, rho1, above, below, pos)
    own = pl.pallas_call(
        functools.partial(finish_kernel, (rows - 1) * blocks),
        out_shape=counts_shape,
        scratch_shapes=[pltpu.VMEM((blocks, members, LANES), F32)],
        name="finish",
        compiler_params=vmem_params(),
    )(rest, part, pos, counts)

    chip = lax.ppermute(own, "grp", swapped("grp", 2))
    core = lax.ppermute(own, "grp", swapped("grp", 1))
    both = lax.ppermute(chip, "grp", swapped("grp", 1))
    piece = pl.BlockSpec((members, sensors), lambda i, g: (0, 0))
    predicted, packed = pl.pallas_call(
        functools.partial(product_kernel, total),
        grid_spec=pltpu.PrefetchScalarGridSpec(
            num_scalar_prefetch=1,
            grid=(1,),
            in_specs=[piece] * 4
            + [
                pl.BlockSpec((members, sensors), lambda i, g: (g[0], 0)),
                pl.BlockSpec((1, sensors), lambda i, g: (0, 0)),
            ],
            out_specs=[
                pl.BlockSpec((total, sensors), lambda i, g: (0, 0)),
                pl.BlockSpec((total + members, total), lambda i, g: (0, 0)),
            ],
        ),
        out_shape=[
            jax.ShapeDtypeStruct((total, sensors), F32),
            jax.ShapeDtypeStruct((total + members, total), F32),
        ],
        name="product",
        compiler_params=vmem_params(),
    )(g, own, core, chip, both, perturbed, noise_var.reshape(1, sensors))

    bit = 1
    while bit < lax.axis_size("cell"):
        packed = packed + lax.ppermute(packed, "cell", swapped("cell", bit))
        bit *= 2
    system = (total - 1.0) * jnp.eye(total, dtype=F32) + packed[:total]
    factor = jnp.linalg.cholesky(system)
    mixing = jax.scipy.linalg.cho_solve((factor, True), packed[total:].T)
    mixing = mixing - jnp.mean(mixing, axis=0)

    chip_theta = lax.ppermute(flat_theta, "grp", swapped("grp", 2))
    core_theta = lax.ppermute(flat_theta, "grp", swapped("grp", 1))
    both_theta = lax.ppermute(chip_theta, "grp", swapped("grp", 1))
    new = pl.pallas_call(
        functools.partial(update_kernel, rows),
        in_specs=[pl.BlockSpec(memory_space=pltpu.SMEM), pl.BlockSpec(memory_space=pltpu.VMEM)] + [anywhere] * 4,
        out_specs=anywhere,
        out_shape=jax.ShapeDtypeStruct((members * rows, columns), F32),
        scratch_shapes=[
            pltpu.VMEM((4, blocks, members * rows, LANES), F32),
            columns_of,
            pltpu.SemaphoreType.DMA((4, blocks)),
            pltpu.SemaphoreType.DMA((blocks,)),
        ],
        name="update",
        compiler_params=vmem_params(),
    )(g, mixing, flat_theta, core_theta, chip_theta, both_theta)
    return (new.reshape(members, rows, columns), predicted)


def solution(mesh):
    return jax.shard_map(
        body,
        mesh=mesh,
        in_specs=(
            P("grp", "cell", None),
            P("grp", "cell", None),
            P("cell", None),
            P(None, "cell"),
            P("cell"),
        ),
        out_specs=(P("grp", "cell", None), P(None, "cell")),
        check_vma=False,
    )
```

time: 685 us -> 169 us (0.25)
  waiting for transfers between devices: 415 us -> 50.3 us
  local copies, waits for them, and re-layouts: 140 us -> 3.01 us
  Pallas kernels: 0 us -> 66 us
  other arithmetic: 70.1 us -> 25.9 us
  matrix products: 14.1 us -> 0.64 us
  between operations: 14.1 us -> 1.01 us
    psum x1 -> x0, waiting for transfers between devices: 313 us -> none  [body(): gram_p, gram_q = lax.psum((gram_p, gram_q), 'cell')]
    gather x2 -> x0, local copies, waits for them, and re-layouts: 115 us -> none  [masked_counts(): values = jnp.take(flat, jnp.clip(local, 0, slab - 1), axis=1)]
    all_gather x2 -> x0, waiting for transfers between devices: 91.4 us -> none  [the longest x1 68.1 us: body(): piece = lax.all_gather(theta, 'grp', axis=0, tiled=True)]
    pallas_call x0 -> x6, Pallas kernels: none -> 66 us  [the longest x1 35.5 us: body(): pl.pallas_call(step2_kernel, out_shape=[counts_shape, row], scratch_shape...]
    ppermute x7 -> x16, waiting for transfers between devices: 9.76 us -> 50.3 us  [the longest x5 23.5 us: body(): packed = packed + lax.ppermute(packed, 'cell', swapped('cell', bit))]
    reduce_sum x5 -> x0, other arithmetic: 30.8 us -> none  [the longest x2 25.2 us: masked_counts(): return jnp.sum(jnp.where(inside[None], values, 0.0), axis=2)]
    dot_general x3 -> x0, matrix products: 12.6 us -> none  [the longest x1 7.5 us: body(): jnp.einsum('ij,ixy->jxy', own_columns, piece, precision=lax.Precision.HIG...]
    unnamed x18, local copies, waits for them, and re-layouts: 9.78 us -> 2.82 us
  transfers between devices with their start and end apart: 10 -> 16, of which waited for: 5 -> 10; matrix products, arithmetic and copies ran while one was open for 16% -> 16% of each run, Pallas kernels for 0% -> 33%
where the time goes in v1:
time: 169 us
  Pallas kernels  66 us (39%)
  waiting for transfers between devices  50.3 us (30%)
  other arithmetic  25.9 us (15%)
  starting transfers between devices  21.8 us (13%)
  local copies, waits for them, and re-layouts  3.01 us (2%)
    pallas_call x1, Pallas kernels, body(): pl.pallas_call(step2_kernel, out_shape=[counts_shape, row], scratch_shape...  35.5 us
    ppermute x5, waiting for transfers between devices, body(): packed = packed + lax.ppermute(packed, 'cell', swapped('cell', bit))  23.5 us
    ppermute x2, waiting for transfers between devices, body(): below = lax.ppermute(top, 'cell', along('cell', -1))  15.1 us
    another operation x3, other arithmetic, body(): factor = jnp.linalg.cholesky(system)  12.4 us
    pallas_call x1, Pallas kernels, body(): pl.pallas_call(functools.partial(update_kernel, rows), in_specs=[pl.Block...  10.6 us
    another operation x2, other arithmetic, body(): mixing = jax.scipy.linalg.cho_solve((factor, True), packed[total:].T)  10.5 us
    ppermute x2, starting transfers between devices, body(): above = lax.ppermute(down, 'cell', along('cell', 1))  7.31 us
    ppermute x1, waiting for transfers between devices, body(): chip = lax.ppermute(own, 'grp', swapped('grp', 2))  6.58 us
  transfers between devices with their start and end apart: 16, of which 10 were waited for; matrix products, arithmetic and copies ran while one was open for 16% of the time, Pallas kernels for 33%

profile of v1, /device:TPU:22, one launch (start us, length us, event | category | flops | bytes accessed | tf_op | source)
XLA Modules:
  0.0 168.8 jit_solution(10398649510749758385)
XLA Ops:
  0.6 2.0 %collective-permute-start.14 = (f32[256,2048]{1,0:T(8,128)}, f32[256,2048]{1,0:T(8,128)}, u32[]{:S(2)}, u32[]{:S(2)}) collective-permute-start(f32[256,2048]{1,0:T(8,128)} %bitcast.20), channel_id=1, source_target_pairs={{0,64},{32,96},{64,0},{96,32},{1,65},{33,97},{65,1},{97,33},{2,66}... | collective-permute-start | bytes 6291464 | tf_op jit(solution)/shard_map/ppermute | solution.py:316
  2.6 5.0 %prep.1 = (f32[8,32,2048]{2,1,0:T(8,128)}, f32[8,32,2048]{2,1,0:T(8,128)}, f32[32,2048]{1,0:T(8,128)}, f32[32,2048]{1,0:T(8,128)}) custom-call(f32[256,2048]{1,0:T(8,128)} %bitcast.21, f32[256,2048]{1,0:T(8,128)} %bitcast.24), custom_call_target="tpu_custom_call" | custom-call | tf_op jit(solution)/shard_map/prep/pallas_call | solution.py:243
  7.6 5.4 %collective-permute-start = (f32[32,2048]{1,0:T(8,128)}, f32[32,2048]{1,0:T(8,128)S(1)}, u32[]{:S(2)}, u32[]{:S(2)}) collective-permute-start(f32[32,2048]{1,0:T(8,128)} %get-tuple-element.16), channel_id=1, source_target_pairs={{0,1},{1,2},{2,3},{3,4},{4,5},{5,6},{6,7},{7,8},{8,9},{9,10},{10,1... | collective-permute-start | bytes 786440 | tf_op jit(solution)/shard_map/ppermute | solution.py:252
  13.0 1.9 %collective-permute-start.1 = (f32[32,2048]{1,0:T(8,128)}, f32[32,2048]{1,0:T(8,128)S(1)}, u32[]{:S(2)}, u32[]{:S(2)}) collective-permute-start(f32[32,2048]{1,0:T(8,128)} %get-tuple-element.17), channel_id=1, source_target_pairs={{1,0},{2,1},{3,2},{4,3},{5,4},{6,5},{7,6},{8,7},{9,8},{10,9},{11,1... | collective-permute-start | bytes 786440 | tf_op jit(solution)/shard_map/ppermute | solution.py:253
  15.0 3.7 %collective-permute-done.above = f32[32,2048]{1,0:T(8,128)S(1)} collective-permute-done((f32[32,2048]{1,0:T(8,128)}, f32[32,2048]{1,0:T(8,128)S(1)}, u32[]{:S(2)}, u32[]{:S(2)}) %collective-permute-start) | collective-permute-done | bytes 262176 | tf_op jit(solution)/shard_map/ppermute | solution.py:252
  18.7 7.7 %collective-permute-done.1.below = f32[32,2048]{1,0:T(8,128)S(1)} collective-permute-done((f32[32,2048]{1,0:T(8,128)}, f32[32,2048]{1,0:T(8,128)S(1)}, u32[]{:S(2)}, u32[]{:S(2)}) %collective-permute-start.1) | collective-permute-done | bytes 262176 | tf_op jit(solution)/shard_map/ppermute | solution.py:253
  27.0 5.5 %step1.1 = (f32[8,32,2048]{2,1,0:T(8,128)}, f32[32,2048]{1,0:T(8,128)}, f32[32,2048]{1,0:T(8,128)}, f32[32,2048]{1,0:T(8,128)}) custom-call(f32[8,32,2048]{2,1,0:T(8,128)} %get-tuple-element.14.theta, f32[8,32,2048]{2,1,0:T(8,128)} %get-tuple-element.15.rho, f32[32,2048]{1,0:T(8,128)} %copy-done.2, f32[32,2048]{1,0:T(8,128)} %copy-done.4), custom_call_target="tpu_custom_call" | custom-call | tf_op jit(solution)/shard_map/step1/pallas_call | solution.py:254
  32.5 1.9 %collective-permute-start.2 = (f32[32,2048]{1,0:T(8,128)}, f32[32,2048]{1,0:T(8,128)S(1)}, u32[]{:S(2)}, u32[]{:S(2)}) collective-permute-start(f32[32,2048]{1,0:T(8,128)} %get-tuple-element.19), channel_id=1, source_target_pairs={{0,1},{1,2},{2,3},{3,4},{4,5},{5,6},{6,7},{7,8},{8,9},{9,10},{10,1... | collective-permute-start | bytes 786440 | tf_op jit(solution)/shard_map/ppermute | solution.py:261
  34.4 3.9 %collective-permute-start.3 = (f32[32,2048]{1,0:T(8,128)}, f32[32,2048]{1,0:T(8,128)S(1)}, u32[]{:S(2)}, u32[]{:S(2)}) collective-permute-start(f32[32,2048]{1,0:T(8,128)} %get-tuple-element.20), channel_id=1, source_target_pairs={{1,0},{2,1},{3,2},{4,3},{5,4},{6,5},{7,6},{8,7},{9,8},{10,9},{11,1... | collective-permute-start | bytes 786440 | tf_op jit(solution)/shard_map/ppermute | solution.py:262
  38.3 1.9 %collective-permute-start.4 = (f32[32,2048]{1,0:T(8,128)}, f32[32,2048]{1,0:T(8,128)S(1)}, u32[]{:S(2)}, u32[]{:S(2)}) collective-permute-start(f32[32,2048]{1,0:T(8,128)} %get-tuple-element.22), channel_id=1, source_target_pairs={{1,0},{2,1},{3,2},{4,3},{5,4},{6,5},{7,6},{8,7},{9,8},{10,9},{11,1... | collective-permute-start | bytes 786440 | tf_op jit(solution)/shard_map/ppermute | solution.py:263
  41.7 7.4 %collective-permute-done.3.below = f32[32,2048]{1,0:T(8,128)S(1)} collective-permute-done((f32[32,2048]{1,0:T(8,128)}, f32[32,2048]{1,0:T(8,128)S(1)}, u32[]{:S(2)}, u32[]{:S(2)}) %collective-permute-start.3) | collective-permute-done | bytes 262176 | tf_op jit(solution)/shard_map/ppermute | solution.py:262
  49.8 35.5 %step2.1 = (f32[32,2048]{1,0:T(8,128)}, f32[32,2048]{1,0:T(8,128)}) custom-call(f32[8,32,2048]{2,1,0:T(8,128)} %get-tuple-element.14.theta, f32[8,32,2048]{2,1,0:T(8,128)} %get-tuple-element.18.rho, f32[32,2048]{1,0:T(8,128)} %copy-done.5, f32[32,2048]{1,0:T(8,128)} %copy-done.6, s32[16,128]{1,0:T(8,128)} %bitcast.26), custom_call_target="tpu_custom_call" | custom-call | tf_op jit(solution)/shard_map/step2/pallas_call | solution.py:265
  86.1 6.1 %finish.1.own = f32[32,2048]{1,0:T(8,128)} custom-call(f32[32,2048]{1,0:T(8,128)} %get-tuple-element.21.rest, f32[32,2048]{1,0:T(8,128)} %copy-done.8, s32[16,128]{1,0:T(8,128)} %bitcast.27, f32[32,2048]{1,0:T(8,128)} %get-tuple-element.23.counts), custom_call_target="tpu_custom_call" | custom-call | tf_op jit(solution)/shard_map/finish/pallas_call | solution.py:272
  92.2 6.6 %collective-permute-done.6.chip = f32[32,2048]{1,0:T(8,128)S(1)} collective-permute-done((f32[32,2048]{1,0:T(8,128)}, f32[32,2048]{1,0:T(8,128)S(1)}, u32[]{:S(2)}, u32[]{:S(2)}) %collective-permute-start.6) | collective-permute-done | bytes 262176 | tf_op jit(solution)/shard_map/ppermute | solution.py:280
  101.0 3.3 %product.1 = (f32[128,2048]{1,0:T(8,128)}, f32[160,128]{1,0:T(8,128)}) custom-call(s32[1]{0:T(128)} %bitcast.g_ref, f32[32,2048]{1,0:T(8,128)} %finish.1.own, f32[32,2048]{1,0:T(8,128)} %copy-done.3, f32[32,2048]{1,0:T(8,128)} %copy-done.1, f32[32,2048]{1,0:T(8,128)} %copy-done.7, f32[128,2048]{1,0:T(8,128)} %perturbed.1, f32[1,2048]{1,0:T(1,128)} %bitcast.28), custom_call_target="tpu_custom_call" | custom-call | tf_op jit(solution)/shard_map/product/pallas_call | solution.py:284
  104.4 4.7 %collective-permute-done.8 = f32[160,128]{1,0:T(8,128)S(1)} collective-permute-done((f32[160,128]{1,0:T(8,128)}, f32[160,128]{1,0:T(8,128)S(1)}, u32[]{:S(2)}, u32[]{:S(2)}) %collective-permute-start.8) | collective-permute-done | bytes 81952 | tf_op jit(solution)/shard_map/ppermute | solution.py:309
  110.7 5.3 %collective-permute-done.9 = f32[160,128]{1,0:T(8,128)S(1)} collective-permute-done((f32[160,128]{1,0:T(8,128)S(1)}, f32[160,128]{1,0:T(8,128)S(1)}, u32[]{:S(2)}, u32[]{:S(2)}) %collective-permute-start.9) | collective-permute-done | bytes 81952 | tf_op jit(solution)/shard_map/ppermute | solution.py:309
  116.0 2.5 %collective-permute-start.10 = (f32[160,128]{1,0:T(8,128)S(1)}, f32[160,128]{1,0:T(8,128)S(1)}, u32[]{:S(2)}, u32[]{:S(2)}) collective-permute-start(f32[160,128]{1,0:T(8,128)S(1)} %add.34), channel_id=1, source_target_pairs={{0,4},{1,5},{2,6},{3,7},{4,0},{5,1},{6,2},{7,3},{8,12},{9,13},{10,... | collective-permute-start | bytes 245768 | tf_op jit(solution)/shard_map/ppermute | solution.py:309
  118.5 3.6 %collective-permute-done.10 = f32[160,128]{1,0:T(8,128)S(1)} collective-permute-done((f32[160,128]{1,0:T(8,128)S(1)}, f32[160,128]{1,0:T(8,128)S(1)}, u32[]{:S(2)}, u32[]{:S(2)}) %collective-permute-start.10) | collective-permute-done | bytes 81952 | tf_op jit(solution)/shard_map/ppermute | solution.py:309
  123.4 4.0 %collective-permute-done.11 = f32[160,128]{1,0:T(8,128)S(1)} collective-permute-done((f32[160,128]{1,0:T(8,128)S(1)}, f32[160,128]{1,0:T(8,128)S(1)}, u32[]{:S(2)}, u32[]{:S(2)}) %collective-permute-start.11) | collective-permute-done | bytes 81952 | tf_op jit(solution)/shard_map/ppermute | solution.py:309
  127.6 5.9 %collective-permute-done.12 = f32[160,128]{1,0:T(8,128)S(1)} collective-permute-done((f32[160,128]{1,0:T(8,128)S(1)}, f32[160,128]{1,0:T(8,128)S(1)}, u32[]{:S(2)}, u32[]{:S(2)}) %collective-permute-start.12) | collective-permute-done | bytes 81952 | tf_op jit(solution)/shard_map/ppermute | solution.py:309
  133.7 11.7 %cholesky.16 = f32[128,128]{1,0:T(8,128)S(1)} custom-call(f32[128,128]{1,0:T(8,128)S(1)} %fusion.5), custom_call_target="Cholesky" | custom-call | tf_op jit(solution)/shard_map/jit(cholesky)/cholesky | solution.py:312
  146.8 9.8 %custom-call.10 = f32[1,128,128]{1,2,0:T(8,128)S(1)} custom-call(f32[1,128,128]{2,1,0:T(8,128)S(1)} %fusion), custom_call_target="InvertDiagBlocksLowerTriangular" | custom-call | tf_op jit(solution)/shard_map/jit(_cho_solve)/triangular_solve | solution.py:313
  158.0 10.6 %update.1 = f32[256,2048]{1,0:T(8,128)} custom-call(s32[1]{0:T(128)} %bitcast.g_ref, f32[128,32]{1,0:T(8,128)} %broadcast_subtract_fusion.mixing, f32[256,2048]{1,0:T(8,128)} %bitcast.22, f32[256,2048]{1,0:T(8,128)} %collective-permute-done.13.core, f32[256,2048]{1,0:T(8,128)} %collective-permute-done.14.chip, f32[256,2048]{1,0:T(8,128)} %collective-permute-done.15.both), custom_call_target="tpu_custom_call" | custom-call | tf_op jit(solution)/shard_map/update/pallas_call | solution.py:319
  (51 shorter events, 11.9 us)
Async XLA Ops:
  0.6 109.5 %collective-permute-start.14 = (f32[256,2048]{1,0:T(8,128)}, f32[256,2048]{1,0:T(8,128)}, u32[]{:S(2)}, u32[]{:S(2)}) collective-permute-start(f32[256,2048]{1,0:T(8,128)} %bitcast.20), channel_id=1, source_target_pairs={{0,64},{32,96},{64,0},{96,32},{1,65},{33,97},{65,1},{97,33},{2,66}... | collective-permute-start | bytes 6291464 | tf_op jit(solution)/shard_map/ppermute | solution.py:316
  7.6 11.0 %collective-permute-start = (f32[32,2048]{1,0:T(8,128)}, f32[32,2048]{1,0:T(8,128)S(1)}, u32[]{:S(2)}, u32[]{:S(2)}) collective-permute-start(f32[32,2048]{1,0:T(8,128)} %get-tuple-element.16), channel_id=1, source_target_pairs={{0,1},{1,2},{2,3},{3,4},{4,5},{5,6},{6,7},{7,8},{8,9},{9,10},{10,1... | collective-permute-start | bytes 786440 | tf_op jit(solution)/shard_map/ppermute | solution.py:252
  13.0 13.3 %collective-permute-start.1 = (f32[32,2048]{1,0:T(8,128)}, f32[32,2048]{1,0:T(8,128)S(1)}, u32[]{:S(2)}, u32[]{:S(2)}) collective-permute-start(f32[32,2048]{1,0:T(8,128)} %get-tuple-element.17), channel_id=1, source_target_pairs={{1,0},{2,1},{3,2},{4,3},{5,4},{6,5},{7,6},{8,7},{9,8},{10,9},{11,1... | collective-permute-start | bytes 786440 | tf_op jit(solution)/shard_map/ppermute | solution.py:253
  18.7 7.7 %copy-start.2 = (f32[32,2048]{1,0:T(8,128)}, f32[32,2048]{1,0:T(8,128)S(1)}, u32[]{:S(2)}) copy-start(f32[32,2048]{1,0:T(8,128)S(1)} %collective-permute-done.above) | copy-start | bytes 786436
  32.5 9.2 %collective-permute-start.2 = (f32[32,2048]{1,0:T(8,128)}, f32[32,2048]{1,0:T(8,128)S(1)}, u32[]{:S(2)}, u32[]{:S(2)}) collective-permute-start(f32[32,2048]{1,0:T(8,128)} %get-tuple-element.19), channel_id=1, source_target_pairs={{0,1},{1,2},{2,3},{3,4},{4,5},{5,6},{6,7},{7,8},{8,9},{9,10},{10,1... | collective-permute-start | bytes 786440 | tf_op jit(solution)/shard_map/ppermute | solution.py:261
  34.4 14.7 %collective-permute-start.3 = (f32[32,2048]{1,0:T(8,128)}, f32[32,2048]{1,0:T(8,128)S(1)}, u32[]{:S(2)}, u32[]{:S(2)}) collective-permute-start(f32[32,2048]{1,0:T(8,128)} %get-tuple-element.20), channel_id=1, source_target_pairs={{1,0},{2,1},{3,2},{4,3},{5,4},{6,5},{7,6},{8,7},{9,8},{10,9},{11,1... | collective-permute-start | bytes 786440 | tf_op jit(solution)/shard_map/ppermute | solution.py:262
  38.3 47.0 %collective-permute-start.4 = (f32[32,2048]{1,0:T(8,128)}, f32[32,2048]{1,0:T(8,128)S(1)}, u32[]{:S(2)}, u32[]{:S(2)}) collective-permute-start(f32[32,2048]{1,0:T(8,128)} %get-tuple-element.22), channel_id=1, source_target_pairs={{1,0},{2,1},{3,2},{4,3},{5,4},{6,5},{7,6},{8,7},{9,8},{10,9},{11,1... | collective-permute-start | bytes 786440 | tf_op jit(solution)/shard_map/ppermute | solution.py:263
  41.7 7.4 %copy-start.5 = (f32[32,2048]{1,0:T(8,128)}, f32[32,2048]{1,0:T(8,128)S(1)}, u32[]{:S(2)}) copy-start(f32[32,2048]{1,0:T(8,128)S(1)} %collective-permute-done.2.above) | copy-start | bytes 786436
  49.1 0.7 copy-start.6
  85.3 24.7 %copy-start = (f32[32,8,2048]{2,1,0:T(8,128)S(1)}, f32[32,8,2048]{2,1,0:T(8,128)}, u32[]{:S(2)}) copy-start(f32[32,8,2048]{2,1,0:T(8,128)} %param.5) | copy-start | bytes 6291460
  85.4 0.7 copy-start.8
  92.2 6.6 %collective-permute-start.6 = (f32[32,2048]{1,0:T(8,128)}, f32[32,2048]{1,0:T(8,128)S(1)}, u32[]{:S(2)}, u32[]{:S(2)}) collective-permute-start(f32[32,2048]{1,0:T(8,128)} %finish.1.own), channel_id=1, source_target_pairs={{0,64},{32,96},{64,0},{96,32},{1,65},{33,97},{65,1},{97,33},{2,66}... | collective-permute-start | bytes 786440 | tf_op jit(solution)/shard_map/ppermute | solution.py:280
  92.2 6.6 %collective-permute-start.5 = (f32[32,2048]{1,0:T(8,128)}, f32[32,2048]{1,0:T(8,128)S(1)}, u32[]{:S(2)}, u32[]{:S(2)}) collective-permute-start(f32[32,2048]{1,0:T(8,128)} %finish.1.own), channel_id=1, source_target_pairs={{0,32},{32,0},{64,96},{96,64},{1,33},{33,1},{65,97},{97,65},{2,34}... | collective-permute-start | bytes 786440 | tf_op jit(solution)/shard_map/ppermute | solution.py:281
  98.8 1.5 copy-start.1
  98.8 1.5 collective-permute-start.7
  98.8 1.5 copy-start.3
  100.3 0.7 copy-start.7
  104.4 4.7 %collective-permute-start.8 = (f32[160,128]{1,0:T(8,128)}, f32[160,128]{1,0:T(8,128)S(1)}, u32[]{:S(2)}, u32[]{:S(2)}) collective-permute-start(f32[160,128]{1,0:T(8,128)} %get-tuple-element.24), channel_id=1, source_target_pairs={{0,1},{1,0},{2,3},{3,2},{4,5},{5,4},{6,7},{7,6},{8,9},{9,8},{10,11... | collective-permute-start | bytes 245768 | tf_op jit(solution)/shard_map/ppermute | solution.py:309
  110.0 6.0 %collective-permute-start.9 = (f32[160,128]{1,0:T(8,128)S(1)}, f32[160,128]{1,0:T(8,128)S(1)}, u32[]{:S(2)}, u32[]{:S(2)}) collective-permute-start(f32[160,128]{1,0:T(8,128)S(1)} %add.33), channel_id=1, source_target_pairs={{0,2},{1,3},{2,0},{3,1},{4,6},{5,7},{6,4},{7,5},{8,10},{9,11},{10,... | collective-permute-start | bytes 245768 | tf_op jit(solution)/shard_map/ppermute | solution.py:309
  110.1 48.0 %collective-permute-start.13 = (f32[256,2048]{1,0:T(8,128)S(1)}, f32[256,2048]{1,0:T(8,128)}, u32[]{:S(2)}, u32[]{:S(2)}) collective-permute-start(f32[256,2048]{1,0:T(8,128)S(1)} %bitcast.23), channel_id=1, source_target_pairs={{0,32},{32,0},{64,96},{96,64},{1,33},{33,1},{65,97},{97,65},{2,34}... | collective-permute-start | bytes 6291464 | tf_op jit(solution)/shard_map/ppermute | solution.py:317
  110.2 47.9 %collective-permute-start.15 = (f32[256,2048]{1,0:T(8,128)}, f32[256,2048]{1,0:T(8,128)}, u32[]{:S(2)}, u32[]{:S(2)}) collective-permute-start(f32[256,2048]{1,0:T(8,128)} %collective-permute-done.14.chip), channel_id=1, source_target_pairs={{0,32},{32,0},{64,96},{96,64},{1,33},{33,1},{65,97},{97,65},{2,34}... | collective-permute-start | bytes 6291464 | tf_op jit(solution)/shard_map/ppermute | solution.py:318
  116.0 6.0 %collective-permute-start.10 = (f32[160,128]{1,0:T(8,128)S(1)}, f32[160,128]{1,0:T(8,128)S(1)}, u32[]{:S(2)}, u32[]{:S(2)}) collective-permute-start(f32[160,128]{1,0:T(8,128)S(1)} %add.34), channel_id=1, source_target_pairs={{0,4},{1,5},{2,6},{3,7},{4,0},{5,1},{6,2},{7,3},{8,12},{9,13},{10,... | collective-permute-start | bytes 245768 | tf_op jit(solution)/shard_map/ppermute | solution.py:309
  122.0 5.3 %collective-permute-start.11 = (f32[160,128]{1,0:T(8,128)S(1)}, f32[160,128]{1,0:T(8,128)S(1)}, u32[]{:S(2)}, u32[]{:S(2)}) collective-permute-start(f32[160,128]{1,0:T(8,128)S(1)} %add.35), channel_id=1, source_target_pairs={{0,8},{1,9},{2,10},{3,11},{4,12},{5,13},{6,14},{7,15},{8,0},{9,1},... | collective-permute-start | bytes 245768 | tf_op jit(solution)/shard_map/ppermute | solution.py:309
  127.4 6.2 %collective-permute-start.12 = (f32[160,128]{1,0:T(8,128)S(1)}, f32[160,128]{1,0:T(8,128)S(1)}, u32[]{:S(2)}, u32[]{:S(2)}) collective-permute-start(f32[160,128]{1,0:T(8,128)S(1)} %add.36), channel_id=1, source_target_pairs={{0,16},{1,17},{2,18},{3,19},{4,20},{5,21},{6,22},{7,23},{8,24},{9,... | collective-permute-start | bytes 245768 | tf_op jit(solution)/shard_map/ppermute | solution.py:309
  (1 other events, 0.7 us)

commit v2 on v1

v2 whole, which is shorter than its diff:
```python
import functools

import jax
import jax.numpy as jnp
from jax import lax
from jax.experimental import pallas as pl
from jax.experimental.pallas import tpu as pltpu
from jax.sharding import PartitionSpec as P

LANES = 128
F32 = jnp.float32


def along(axis, shift):
    count = lax.axis_size(axis)
    return [(i, i + shift) for i in range(count) if 0 <= i + shift < count]


def swapped(axis, bit):
    return [(i, i ^ bit) for i in range(lax.axis_size(axis))]


def outflow(speed, rho):
    return 0.2 * (speed * rho * (1.0 - rho)) + 0.1 * rho


def from_left(x):
    lane = lax.broadcasted_iota(jnp.int32, x.shape, 1)
    return jnp.where(lane == 0, 0.0, pltpu.roll(x, 1, 1))


def from_right(x):
    last = x.shape[1] - 1
    lane = lax.broadcasted_iota(jnp.int32, x.shape, 1)
    return jnp.where(lane == last, 0.0, pltpu.roll(x, last, 1))


def without_above(rho, out, below):
    return 0.8 * rho - 2.0 * out + from_left(out) + 0.1 * (below + from_right(rho))


def box4(x):
    n = x.shape[1]
    pair = x + pltpu.roll(x, n - 1, 1)
    return pair + pltpu.roll(pair, n - 2, 1)


def load_columns(source, target, sems, first=0):
    copies = []
    for b in range(source.shape[1] // LANES):
        copy = pltpu.make_async_copy(
            source.at[:, pl.ds(b * LANES, LANES)], target.at[b, pl.ds(first, source.shape[0])], sems.at[b]
        )
        copy.start()
        copies.append(copy)
    return copies


def edge_kernel(rows, odd, theta, rho, low_pair, high_pair, theta_in, rho_in, sems):
    waits = load_columns(rho, rho_in, sems.at[0]), load_columns(theta, theta_in, sems.at[1])
    members = low_pair.shape[0]
    swap = odd[0] == 1
    for b in range(theta_in.shape[0]):
        at = slice(b * LANES, (b + 1) * LANES)
        waits[0][b].wait()
        waits[1][b].wait()
        last = pl.ds(rows - 1, members, stride=rows)
        down = outflow(theta_in[b, last, :], rho_in[b, last, :])
        top = rho_in[b, pl.ds(0, members, stride=rows), :]
        low_pair[:, at] = jnp.where(swap, top, down)
        high_pair[:, at] = jnp.where(swap, down, top)


def prep_kernel(members, rows, theta, rho, theta_t, rho_t, theta_in, rho_in, sems):
    waits = load_columns(rho, rho_in, sems.at[0]), load_columns(theta, theta_in, sems.at[1])
    for b in range(theta_in.shape[0]):
        at = slice(b * LANES, (b + 1) * LANES)
        waits[0][b].wait()
        waits[1][b].wait()
        for r in range(rows):
            theta_t[r, :, at] = theta_in[b, pl.ds(r, members, stride=rows), :]
            rho_t[r, :, at] = rho_in[b, pl.ds(r, members, stride=rows), :]


def step1_kernel(odd, theta, rho, from_low, from_high, rho1, low_pair, high_pair, part):
    rows, members, _ = rho.shape
    swap = odd[0] == 1

    def chunk(c, carry):
        at = pl.ds(c * 8, 8)
        low, high = from_low[at, :], from_high[at, :]
        up = jnp.where(swap, low, high)
        beneath = jnp.where(swap, high, low)
        kept = None
        for r in range(rows):
            now = rho[r, at, :]
            under = rho[r + 1, at, :] if r + 1 < rows else beneath
            speed = theta[r, at, :]
            out = outflow(speed, now)
            new = without_above(now, out, under) + up
            rho1[r, at, :] = new
            up = out
            if r == 0:
                kept = (new, outflow(speed, new))
            if r == 1:
                part[at, :] = without_above(kept[0], kept[1], new)
            if r == rows - 1:
                down = outflow(speed, new)
                low_pair[at, :] = jnp.where(swap, kept[0], down)
                high_pair[at, :] = jnp.where(swap, down, kept[0])
        return carry

    lax.fori_loop(0, members // 8, chunk, 0)


def pick(table, first, last, low, high, pos_ref, start, out_ref):
    members = out_ref.shape[0]
    parts = members // 8
    width = 4
    for g0 in range(0, pos_ref.shape[0], width):
        groups = range(g0, g0 + width)
        where = [jnp.broadcast_to(pos_ref[g : g + 1, :], (8, LANES)) for g in groups]
        lane = [w & (LANES - 1) for w in where]
        block = [w >> 7 for w in where]
        begin = [jnp.maximum(low[g], first) for g in groups]
        trips = functools.reduce(
            jnp.maximum, [jnp.minimum(high[g], last) + 1 - lo for g, lo in zip(groups, begin)]
        )
        init = tuple(
            start[i * 8 : i * 8 + 8, g * LANES : (g + 1) * LANES] if start is not None else jnp.zeros((8, LANES), F32)
            for g in groups
            for i in range(parts)
        )

        def look(t, acc):
            new = []
            for k in range(width):
                p = begin[k] + t
                at = jnp.minimum(p, last) - first
                hit = block[k] == p
                for i in range(parts):
                    row = table[at, i * 8 : i * 8 + 8, :]
                    got = jnp.take_along_axis(row, lane[k], axis=1, mode="promise_in_bounds")
                    new.append(jnp.where(hit, got, acc[k * parts + i]))
            return tuple(new)

        acc = lax.fori_loop(0, trips, look, init)
        for k, g in enumerate(groups):
            for i in range(parts):
                out_ref[i * 8 : i * 8 + 8, g * LANES : (g + 1) * LANES] = acc[k * parts + i]


def reorder_kernel(index, source, out):
    members = out.shape[0]
    groups = index.shape[0]

    def one(g, carry):
        where = jnp.broadcast_to(index[pl.ds(g, 1), :], (8, LANES))
        lane = where & (LANES - 1)
        block = where >> 7
        at = pl.ds(pl.multiple_of(g * LANES, LANES), LANES)
        for i in range(0, members, 8):
            acc = jnp.zeros((8, LANES), F32)
            for h in range(groups):
                row = source[i : i + 8, h * LANES : (h + 1) * LANES]
                got = jnp.take_along_axis(row, lane, axis=1, mode="promise_in_bounds")
                acc = jnp.where(block == h, got, acc)
            out[i : i + 8, at] = acc
        return carry

    lax.fori_loop(0, groups, one, 0)


def step2_kernel(odd, theta, rho, from_low, from_high, pos, low, high, counts, rest, table):
    rows, members, columns = rho.shape
    swap = odd[0] == 1
    blocks = columns // LANES

    def chunk(c, carry):
        at = pl.ds(c * 8, 8)
        first, second = from_low[at, :], from_high[at, :]
        up = jnp.where(swap, first, second)
        beneath = jnp.where(swap, second, first)
        last = None
        for r in range(rows):
            now = rho[r, at, :]
            under = rho[r + 1, at, :] if r + 1 < rows else beneath
            out = outflow(theta[r, at, :], now)
            new = without_above(now, out, under) + up
            up = out
            if r > 0:
                sums = box4(last + new)
                for b in range(blocks):
                    table[(r - 1) * blocks + b, at, :] = sums[:, b * LANES : (b + 1) * LANES]
            if r == rows - 1:
                rest[at, :] = new + out
            last = new
        return carry

    lax.fori_loop(0, members // 8, chunk, 0)
    pick(table, 0, (rows - 1) * blocks - 1, low, high, pos, None, counts)


def finish_kernel(first, rest, part, pos, low, high, counts, mine, table):
    members, columns = rest.shape
    blocks = columns // LANES
    for c in range(0, members, 8):
        sums = box4(rest[c : c + 8, :] + part[c : c + 8, :])
        for b in range(blocks):
            table[b, c : c + 8, :] = sums[:, b * LANES : (b + 1) * LANES]
    pick(table, first, first + blocks - 1, low, high, pos, counts, mine)


def product_kernel(total, g_ref, own, core, chip, both, perturbed, noise, packed, every):
    members, sensors = own.shape
    g = g_ref[0]
    for step, piece in enumerate((own, core, chip, both)):
        every[pl.ds(pl.multiple_of((g ^ step) * members, members), members), :] = piece[...]
    width = 512
    acc = None
    for s in range(0, sensors, width):
        at = slice(s, s + width)
        counts = every[:, at]
        anomaly = counts - jnp.sum(counts, axis=0, keepdims=True) / total
        weighted = anomaly / noise[:, at]
        left = jnp.concatenate([anomaly, perturbed[:, at] - own[:, at]], axis=0)
        term = lax.dot_general(
            left, weighted, (((1,), (1,)), ((), ())), precision=lax.Precision.HIGHEST, preferred_element_type=F32
        )
        acc = term if acc is None else acc + term
    packed[...] = acc


def bcast_lane(x, k):
    return jnp.broadcast_to(x[:, k : k + 1], x.shape)


def solve_kernel(shift, packed, mixing_t):
    n = packed.shape[1]
    lane = lax.broadcasted_iota(jnp.int32, (8, n), 1)
    sub = lax.broadcasted_iota(jnp.int32, (8, n), 0)
    a = []
    for i in range(packed.shape[0] // 8):
        x = packed[i * 8 : i * 8 + 8, :]
        a.append(jnp.where(lane == sub + i * 8, x + shift, x) if i * 8 < n else x)
    keep = jnp.zeros((8, n), F32)
    mix = jnp.zeros((8, n), F32)
    for k in range(0, n, 2):
        r = k % 8
        top = a[k // 8]
        r0 = jnp.broadcast_to(top[r : r + 1, :], (8, n))
        r1 = jnp.broadcast_to(top[r + 1 : r + 2, :], (8, n))
        p00, p01, p10, p11 = bcast_lane(r0, k), bcast_lane(r0, k + 1), bcast_lane(r1, k), bcast_lane(r1, k + 1)
        scale = 1.0 / (p00 * p11 - p01 * p10)
        here = (lane == k) | (lane == k + 1)
        f0 = jnp.where(here, 0.0, scale * (p11 * r0 - p01 * r1))
        f1 = jnp.where(here, 0.0, scale * (p00 * r1 - p10 * r0))
        keep = jnp.where(lane == k, scale * p11, jnp.where(lane == k + 1, scale * p00, keep))
        mix = jnp.where(lane == k, -(scale * p10), jnp.where(lane == k + 1, -(scale * p01), mix))
        for i in range(k // 8, len(a)):
            a[i] = a[i] - (bcast_lane(a[i], k) * f0 + bcast_lane(a[i], k + 1) * f1)
    even = (lane & 1) == 0
    for i in range(n // 8, len(a)):
        x = a[i]
        other = jnp.where(even, pltpu.roll(x, n - 1, 1), pltpu.roll(x, 1, 1))
        w = x * keep + other * mix
        w = w - jnp.sum(w, axis=1, keepdims=True) / n
        at = i * 8 - n
        mixing_t[at : at + 8, :] = w


def split(x):
    high = x.astype(jnp.bfloat16)
    return high, (x - high.astype(F32)).astype(jnp.bfloat16)


def update_kernel(rows, g_ref, mixing, own, core, chip, both, chip2, both2, out, fields, new, sems, out_sems):
    members = own.shape[0] // rows
    g = g_ref[0]
    cut = chip.shape[0]
    places = ((own, 0, 0), (core, 1, 0), (chip, 2, 0), (chip2, 2, cut), (both, 3, 0), (both2, 3, cut))
    waits = [load_columns(piece, fields.at[k], sems.at[i], first) for i, (piece, k, first) in enumerate(places)]
    wt = mixing[...]
    n = wt.shape[1]
    lane = lax.broadcasted_iota(jnp.int32, wt.shape, 1)
    crossed = jnp.where((lane & members) == 0, pltpu.roll(wt, n - members, 1), pltpu.roll(wt, members, 1))
    wt = jnp.where((g & 1) == 1, crossed, wt)
    wt = jnp.where((g & 2) == 2, pltpu.roll(wt, n // 2, 1), wt)
    wh, wl = split(wt)
    sent = []
    for b in range(new.shape[0]):
        for wait in waits:
            wait[b].wait()
        for r in range(rows):
            at = pl.ds(r, members, stride=rows)
            x = [fields[k, b, at, :] for k in range(4)]
            xh, xl = split(jnp.concatenate(x, axis=0))
            add = (
                jnp.dot(wh, xh, preferred_element_type=F32)
                + jnp.dot(wh, xl, preferred_element_type=F32)
                + jnp.dot(wl, xh, preferred_element_type=F32)
            )
            new[b, at, :] = x[0] + add
        copy = pltpu.make_async_copy(new.at[b], out.at[:, pl.ds(b * LANES, LANES)], out_sems.at[b])
        copy.start()
        sent.append(copy)
    for copy in sent:
        copy.wait()


def tie(*values):
    return lax.optimization_barrier(values)


def kernel_params(mib):
    return pltpu.CompilerParams(vmem_limit_bytes=mib * 1024 * 1024)


def body(theta, density, footprint, perturbed, noise_var):
    members, rows, columns = theta.shape
    total = members * lax.axis_size("grp")
    sensors = footprint.shape[0]
    slab = rows * columns
    blocks = columns // LANES
    groups = sensors // LANES
    flat_theta = theta.reshape(members * rows, columns)
    flat_rho = density.reshape(members * rows, columns)
    g = lax.axis_index("grp").astype(jnp.int32).reshape(1)
    row = jax.ShapeDtypeStruct((members, columns), F32)
    turned = jax.ShapeDtypeStruct((rows, members, columns), F32)
    counts_shape = jax.ShapeDtypeStruct((members, sensors), F32)
    anywhere = pl.BlockSpec(memory_space=pltpu.HBM)
    vmem = pl.BlockSpec(memory_space=pltpu.VMEM)
    smem = pl.BlockSpec(memory_space=pltpu.SMEM)
    columns_of = pltpu.VMEM((blocks, members * rows, LANES), F32)

    odd = (lax.axis_index("cell") & 1).astype(jnp.int32).reshape(1)
    count = lax.axis_size("cell")
    far = [(i, i + 1 if i & 1 else i - 1) for i in range(1, count - 1)]

    def both_ways(low_pair, high_pair):
        from_high = lax.ppermute(high_pair, "cell", far)
        return lax.ppermute(low_pair, "cell", swapped("cell", 1)), from_high

    down, top = pl.pallas_call(
        functools.partial(edge_kernel, rows),
        in_specs=[smem, anywhere, anywhere],
        out_shape=[row, row],
        scratch_shapes=[columns_of, columns_of, pltpu.SemaphoreType.DMA((2, blocks))],
        name="edge",
        compiler_params=kernel_params(60),
    )(odd, flat_theta, flat_rho)
    above, below = both_ways(down, top)
    cut = members // 2 * rows
    chip_theta = lax.ppermute(flat_theta[:cut], "grp", swapped("grp", 2))

    down, flat_theta, flat_rho, first = tie(down, flat_theta, flat_rho, footprint[:, 0])
    theta_t, rho_t = pl.pallas_call(
        functools.partial(prep_kernel, members, rows),
        in_specs=[anywhere, anywhere],
        out_shape=[turned, turned],
        scratch_shapes=[columns_of, columns_of, pltpu.SemaphoreType.DMA((2, blocks))],
        name="prep",
        compiler_params=kernel_params(12),
    )(flat_theta, flat_rho)
    key = (first - lax.axis_index("cell") * slab) * sensors + lax.iota(jnp.int32, sensors)
    rank = jnp.sum((key[:, None] < key[None, :]).astype(jnp.int32), axis=0)
    chosen = rank[:, None] == lax.iota(jnp.int32, sensors)[None, :]
    ordered = jnp.sum(jnp.where(chosen, key[:, None], 0), axis=0)
    above, below, ordered, rank = tie(above, below, ordered, rank)

    rho1, down, top, part = pl.pallas_call(
        step1_kernel,
        in_specs=[smem] + [vmem] * 4,
        out_shape=[turned, row, row, row],
        name="step1",
        compiler_params=kernel_params(12),
    )(odd, theta_t, rho_t, above, below)
    above, below = both_ways(down, top)
    part = lax.ppermute(part, "cell", along("cell", -1))

    down, rank, ordered, noise_var, perturbed = tie(down, rank, ordered, noise_var, perturbed)
    chosen = rank[:, None] == lax.iota(jnp.int32, sensors)[None, :]
    noise = jnp.sum(jnp.where(chosen, noise_var[:, None], 0.0), axis=0).reshape(1, sensors)
    pos = (ordered // sensors).reshape(groups, LANES)
    order = (ordered & (sensors - 1)).reshape(groups, LANES)
    rank = rank.reshape(groups, LANES)
    low = pos[:, 0] >> 7
    high = pos[:, LANES - 1] >> 7
    perturbed_own = pl.pallas_call(
        lambda g, index, source, out: reorder_kernel(index, source, out),
        grid_spec=pltpu.PrefetchScalarGridSpec(
            num_scalar_prefetch=1,
            grid=(1,),
            in_specs=[
                pl.BlockSpec((groups, LANES), lambda i, g: (0, 0)),
                pl.BlockSpec((members, sensors), lambda i, g: (g[0], 0)),
            ],
            out_specs=pl.BlockSpec((members, sensors), lambda i, g: (0, 0)),
        ),
        out_shape=counts_shape,
        name="reorder",
        compiler_params=kernel_params(4),
    )(g, order, perturbed)
    above, below, noise, perturbed_own, pos, low, high, rank = tie(
        above, below, noise, perturbed_own, pos, low, high, rank
    )

    counts, rest = pl.pallas_call(
        step2_kernel,
        in_specs=[smem] + [vmem] * 5 + [smem] * 2,
        out_shape=[counts_shape, row],
        scratch_shapes=[pltpu.VMEM(((rows - 1) * blocks, members, LANES), F32)],
        name="step2",
        compiler_params=kernel_params(12),
    )(odd, theta_t, rho1, above, below, pos, low, high)
    rest, part = tie(rest, part)
    own = pl.pallas_call(
        functools.partial(finish_kernel, (rows - 1) * blocks),
        in_specs=[vmem] * 3 + [smem] * 2 + [vmem],
        out_shape=counts_shape,
        scratch_shapes=[pltpu.VMEM((blocks, members, LANES), F32)],
        name="finish",
        compiler_params=kernel_params(4),
    )(rest, part, pos, low, high, counts)

    chip = lax.ppermute(own, "grp", swapped("grp", 2))
    core = lax.ppermute(own, "grp", swapped("grp", 1))
    both = lax.ppermute(chip, "grp", swapped("grp", 1))
    mine = pl.pallas_call(
        reorder_kernel, out_shape=counts_shape, name="restore", compiler_params=kernel_params(4)
    )(rank, own)
    rest = flat_theta[cut:]
    chip, core, mine, rest, chip_theta = tie(chip, core, mine, rest, chip_theta)
    chip_rest = lax.ppermute(rest, "grp", swapped("grp", 2))
    both_theta = lax.ppermute(chip_theta, "grp", swapped("grp", 1))
    packed = pl.pallas_call(
        functools.partial(product_kernel, total),
        in_specs=[smem] + [vmem] * 6,
        out_shape=jax.ShapeDtypeStruct((total + members, total), F32),
        scratch_shapes=[pltpu.VMEM((total, sensors), F32)],
        name="product",
        compiler_params=kernel_params(12),
    )(g, own, core, chip, both, perturbed_own, noise)

    flat_theta, packed = tie(flat_theta, packed)

    def restore(counts):
        return pl.pallas_call(
            reorder_kernel, out_shape=counts_shape, name="restore", compiler_params=kernel_params(4)
        )(rank, counts)

    def assemble(g_ref, own, core, chip, both, out):
        g = g_ref[0]
        for step, piece in enumerate((own, core, chip, both)):
            out[pl.ds(pl.multiple_of((g ^ step) * members, members), members), :] = piece[...]

    core_theta = lax.ppermute(flat_theta, "grp", swapped("grp", 1))
    for stage, bit in enumerate((1, 2, 8, 16, 4)):
        other = lax.ppermute(packed, "cell", swapped("cell", bit))
        if stage == 0:
            core, packed = tie(core, packed)
            core = restore(core)
            other, core = tie(other, core)
        if stage == 1:
            chip, packed = tie(chip, packed)
            chip = restore(chip)
            other, chip = tie(other, chip)
        if stage == 2:
            both, packed = tie(both, packed)
            both = restore(both)
            other, both = tie(other, both)
        if stage == 4:
            both_rest = lax.ppermute(chip_rest, "grp", swapped("grp", 1))
            predicted = pl.pallas_call(
                assemble,
                in_specs=[smem] + [vmem] * 4,
                out_shape=jax.ShapeDtypeStruct((total, sensors), F32),
                name="assemble",
                compiler_params=kernel_params(4),
            )(g, mine, core, chip, both)
            other, predicted = tie(other, predicted)
        packed = packed + other
        if stage == 3:
            packed, chip_rest = tie(packed, chip_rest)
    mixing_t = pl.pallas_call(
        functools.partial(solve_kernel, total - 1.0),
        out_shape=jax.ShapeDtypeStruct((members, total), F32),
        name="solve",
        compiler_params=kernel_params(4),
    )(packed)
    new = pl.pallas_call(
        functools.partial(update_kernel, rows),
        in_specs=[smem, vmem] + [anywhere] * 6,
        out_specs=anywhere,
        out_shape=jax.ShapeDtypeStruct((members * rows, columns), F32),
        scratch_shapes=[
            pltpu.VMEM((4, blocks, members * rows, LANES), F32),
            columns_of,
            pltpu.SemaphoreType.DMA((6, blocks)),
            pltpu.SemaphoreType.DMA((blocks,)),
        ],
        name="update",
        compiler_params=kernel_params(16),
    )(g, mixing_t, flat_theta, core_theta, chip_theta, both_theta, chip_rest, both_rest)
    return (new.reshape(members, rows, columns), predicted)


def solution(mesh):
    return jax.shard_map(
        body,
        mesh=mesh,
        in_specs=(
            P("grp", "cell", None),
            P("grp", "cell", None),
            P("cell", None),
            P(None, "cell"),
            P("cell"),
        ),
        out_specs=(P("grp", "cell", None), P(None, "cell")),
        check_vma=False,
    )
```

time: 169 us -> 112 us (0.66)
  waiting for transfers between devices: 50.3 us -> 30.8 us
  other arithmetic: 25.9 us -> 6.61 us
  Pallas kernels: 66 us -> 49.9 us
    another operation x5 -> x0, other arithmetic: 22.9 us -> none  [the longest x3 12.4 us: body(): factor = jnp.linalg.cholesky(system)]
    ppermute x10 -> x12, waiting for transfers between devices: 42.2 us -> 21.4 us  [the longest x5 18.3 us: body(): other = lax.ppermute(packed, 'cell', swapped('cell', bit))]
    pallas_call x5 -> x13, Pallas kernels: 61.1 us -> 48.2 us  [the longest x1 9.25 us: body(): pl.pallas_call(functools.partial(solve_kernel, total - 1.0), out_shape=ja...]
    reduce_sum x0 -> x3, other arithmetic: none -> 6.36 us  [the longest x1 2.44 us: body(): jnp.sum(jnp.where(chosen, noise_var[:, None], 0.0), axis=0)]
    pallas_call x1, Pallas kernels: 4.99 us -> 1.7 us  [body(): pl.pallas_call(functools.partial(prep_kernel, members, rows), in_specs=[a...]
    ppermute x10 -> x12, starting transfers between devices: 19.3 us -> 16.3 us  [the longest x2 11.5 us: both_ways(): from_high = lax.ppermute(high_pair, 'cell', far)]
    ppermute x1, waiting for transfers between devices: 6.58 us -> 9.42 us  [body(): chip = lax.ppermute(own, 'grp', swapped('grp', 2))]
    sub x2 -> x0, other arithmetic: 2.07 us -> none  [the longest x1 1.44 us: body(): footprint[:, 0] - lax.axis_index('cell') * slab]
  transfers between devices with their start and end apart: 16 -> 18, of which waited for: 10 -> 8; matrix products, arithmetic and copies ran while one was open for 16% -> 7% of each run, Pallas kernels for 33% -> 34%
where the time goes in v2:
time: 112 us
  Pallas kernels  49.9 us (45%)
  waiting for transfers between devices  30.8 us (28%)
  starting transfers between devices  20.6 us (18%)
  other arithmetic  6.61 us (6%)
  local copies, waits for them, and re-layouts  2.74 us (2%)
  between operations  1.13 us (1%)
    ppermute x5, waiting for transfers between devices, body(): other = lax.ppermute(packed, 'cell', swapped('cell', bit))  18.3 us
    ppermute x2, starting transfers between devices, both_ways(): from_high = lax.ppermute(high_pair, 'cell', far)  11.5 us
    ppermute x1, waiting for transfers between devices, body(): chip = lax.ppermute(own, 'grp', swapped('grp', 2))  9.42 us
    pallas_call x1, Pallas kernels, body(): pl.pallas_call(functools.partial(solve_kernel, total - 1.0), out_shape=ja...  9.25 us
    pallas_call x1, Pallas kernels, body(): pl.pallas_call(step2_kernel, in_specs=[smem] + [vmem] * 5 + [smem] * 2, o...  8.8 us
    pallas_call x1, Pallas kernels, body(): pl.pallas_call(functools.partial(update_kernel, rows), in_specs=[smem, vm...  8.49 us
    pallas_call x3, Pallas kernels, restore(): pl.pallas_call(reorder_kernel, out_shape=counts_shape, name='restore', co...  6.69 us
    pallas_call x1, Pallas kernels, body(): pl.pallas_call(functools.partial(edge_kernel, rows), in_specs=[smem, anyw...  3.51 us
  transfers between devices with their start and end apart: 18, of which 8 were waited for; matrix products, arithmetic and copies ran while one was open for 7% of the time, Pallas kernels for 34%

profile of v2, /device:TPU:22, one launch (start us, length us, event | category | flops | bytes accessed | tf_op | source)
XLA Modules:
  0.0 111.8 jit_solution(12001895081323103781)
XLA Ops:
  0.6 3.5 %edge.1 = (f32[32,2048]{1,0:T(8,128)}, f32[32,2048]{1,0:T(8,128)}) custom-call(s32[1]{0:T(128)} %bitcast.1.odd, f32[256,2048]{1,0:T(8,128)} %bitcast.14, f32[256,2048]{1,0:T(8,128)} %bitcast.19), custom_call_target="tpu_custom_call" | custom-call | tf_op jit(solution)/shard_map/edge/pallas_call | solution.py:345
  5.1 6.4 %collective-permute-start.1 = (f32[32,2048]{1,0:T(8,128)}, f32[32,2048]{1,0:T(8,128)}, u32[]{:S(2)}, u32[]{:S(2)}) collective-permute-start(f32[32,2048]{1,0:T(8,128)} %get-tuple-element.61), channel_id=1, source_target_pairs={{1,2},{2,1},{3,4},{4,3},{5,6},{6,5},{7,8},{8,7},{9,10},{10,9},{11,... | collective-permute-start | bytes 786440 | tf_op jit(solution)/shard_map/ppermute | solution.py:342
  18.5 2.2 %select_reduce_fusion.1 = s32[2048]{0:T(1024)S(1)} fusion(s32[2048]{0:T(1024)S(1)} %convert_reduce_fusion, s32[2048]{0:T(1024)S(1)} %iota_add_fusion), kind=kLoop, calls=%fused_computation.2 | loop fusion | flops 12580864 | bytes 24576 | tf_op jit(solution)/shard_map/reduce_sum | solution.py:369
  20.8 2.8 %step1.1 = (f32[8,32,2048]{2,1,0:T(8,128)S(1)}, f32[32,2048]{1,0:T(8,128)S(1)}, f32[32,2048]{1,0:T(8,128)S(1)}, f32[32,2048]{1,0:T(8,128)S(1)}) custom-call(s32[1]{0:T(128)} %bitcast.1.odd, f32[8,32,2048]{2,1,0:T(8,128)S(1)} %get-tuple-element.59.theta, f32[8,32,2048]{2,1,0:T(8,128)S(1)} %get-tuple-element.60.rho, ...), custom_call_target="tpu_custom_call" | custom-call | tf_op jit(solution)/shard_map/step1/pallas_call | solution.py:372
  23.7 5.2 %collective-permute-start.3 = (f32[32,2048]{1,0:T(8,128)S(1)}, f32[32,2048]{1,0:T(8,128)S(1)}, u32[]{:S(2)}, u32[]{:S(2)}) collective-permute-start(f32[32,2048]{1,0:T(8,128)S(1)} %get-tuple-element.67), channel_id=1, source_target_pairs={{1,2},{2,1},{3,4},{4,3},{5,6},{6,5},{7,8},{8,7},{9,10},{10,9},{11,... | collective-permute-start | bytes 786440 | tf_op jit(solution)/shard_map/ppermute | solution.py:342
  28.9 2.0 %collective-permute-start.4 = (f32[32,2048]{1,0:T(8,128)S(1)}, f32[32,2048]{1,0:T(8,128)S(1)}, u32[]{:S(2)}, u32[]{:S(2)}) collective-permute-start(f32[32,2048]{1,0:T(8,128)S(1)} %get-tuple-element.80), channel_id=1, source_target_pairs={{1,0},{2,1},{3,2},{4,3},{5,4},{6,5},{7,6},{8,7},{9,8},{10,9},{11,1... | collective-permute-start | bytes 786440 | tf_op jit(solution)/shard_map/ppermute | solution.py:380
  30.9 2.4 %select_reduce_fusion = f32[2048]{0:T(1024)S(1)} fusion(f32[2048]{0:T(1024)S(1)} %copy-done.3, s32[2048]{0:T(1024)S(1)} %convert_reduce_fusion), kind=kLoop, calls=%fused_computation | loop fusion | flops 12580864 | bytes 24576 | tf_op jit(solution)/shard_map/reduce_sum | solution.py:384
  33.4 2.2 %reorder.1.perturbed = f32[32,2048]{1,0:T(8,128)S(1)} custom-call(s32[1]{0:T(128)} %bitcast.g.g_ref, s32[16,128]{1,0:T(8,128)S(1)} %get-tuple-element.113.index, f32[128,2048]{1,0:T(8,128)S(1)} %copy-done.2), custom_call_target="tpu_custom_call" | custom-call | tf_op jit(solution)/shard_map/reorder/pallas_call | solution.py:390
  35.8 1.7 %collective-permute-done.3.from_high = f32[32,2048]{1,0:T(8,128)S(1)} collective-permute-done((f32[32,2048]{1,0:T(8,128)S(1)}, f32[32,2048]{1,0:T(8,128)S(1)}, u32[]{:S(2)}, u32[]{:S(2)}) %collective-permute-start.3) | collective-permute-done | bytes 262176 | tf_op jit(solution)/shard_map/ppermute | solution.py:342
  37.5 8.8 %step2.1 = (f32[32,2048]{1,0:T(8,128)S(1)}, f32[32,2048]{1,0:T(8,128)S(1)}) custom-call(s32[1]{0:T(128)} %bitcast.1.odd, f32[8,32,2048]{2,1,0:T(8,128)S(1)} %get-tuple-element.59.theta, f32[8,32,2048]{2,1,0:T(8,128)S(1)} %get-tuple-element.65.rho, f32[32,2048]{1,0:T(8,128)S(1)} %collective-permute-done.2.from_low, ...), custom_call_target="tpu_custom_call" | custom-call | tf_op jit(solution)/shard_map/step2/pallas_call | solution.py:409
  46.4 1.7 %finish.1.source.own = f32[32,2048]{1,0:T(8,128)S(1)} custom-call(f32[32,2048]{1,0:T(8,128)S(1)} %get-tuple-element.81.rest, f32[32,2048]{1,0:T(8,128)S(1)} %collective-permute-done.4.part, s32[16,128]{1,0:T(8,128)S(1)} %get-tuple-element.76.pos, s32[16]{0:T(128)S(1)} %get-tuple-element.77.low, s32[16]{0:T(128)S(1)} %get-tuple-element.78.high, ...), custom_call_target="tpu_custom_call" | custom-call | tf_op jit(solution)/shard_map/finish/pallas_call | solution.py:418
  48.1 2.0 %collective-permute-start.5 = (f32[32,2048]{1,0:T(8,128)S(1)}, f32[32,2048]{1,0:T(8,128)S(1)}, u32[]{:S(2)}, u32[]{:S(2)}) collective-permute-start(f32[32,2048]{1,0:T(8,128)S(1)} %finish.1.source.own), channel_id=1, source_target_pairs={{0,64},{32,96},{64,0},{96,32},{1,65},{33,97},{65,1},{97,33},{2,66}... | collective-permute-start | bytes 786440 | tf_op jit(solution)/shard_map/ppermute | solution.py:427
  50.1 9.4 %collective-permute-done.5.chip.source = f32[32,2048]{1,0:T(8,128)S(1)} collective-permute-done((f32[32,2048]{1,0:T(8,128)S(1)}, f32[32,2048]{1,0:T(8,128)S(1)}, u32[]{:S(2)}, u32[]{:S(2)}) %collective-permute-start.5) | collective-permute-done | bytes 262176 | tf_op jit(solution)/shard_map/ppermute | solution.py:427
  59.6 2.2 %restore.4.own = f32[32,2048]{1,0:T(8,128)S(1)} custom-call(s32[16,128]{1,0:T(8,128)S(1)} %bitcast.21, f32[32,2048]{1,0:T(8,128)S(1)} %finish.1.source.own), custom_call_target="tpu_custom_call" | custom-call | tf_op jit(solution)/shard_map/restore/pallas_call | solution.py:430
  64.7 2.2 %restore.5.core = f32[32,2048]{1,0:T(8,128)S(1)} custom-call(s32[16,128]{1,0:T(8,128)S(1)} %bitcast.22, f32[32,2048]{1,0:T(8,128)S(1)} %collective-permute-done.7.core.source), custom_call_target="tpu_custom_call" | custom-call | tf_op jit(solution)/shard_map/restore/pallas_call | solution.py:449
  67.0 2.4 %collective-permute-done.9 = f32[160,128]{1,0:T(8,128)S(1)} collective-permute-done((f32[160,128]{1,0:T(8,128)S(1)}, f32[160,128]{1,0:T(8,128)S(1)}, u32[]{:S(2)}, u32[]{:S(2)}) %collective-permute-start.9) | collective-permute-done | bytes 81952 | tf_op jit(solution)/shard_map/ppermute | solution.py:460
  69.5 2.2 %restore.6.chip = f32[32,2048]{1,0:T(8,128)S(1)} custom-call(s32[16,128]{1,0:T(8,128)S(1)} %bitcast.23, f32[32,2048]{1,0:T(8,128)S(1)} %collective-permute-done.5.chip.source), custom_call_target="tpu_custom_call" | custom-call | tf_op jit(solution)/shard_map/restore/pallas_call | solution.py:449
  71.7 3.7 %collective-permute-done.10 = f32[160,128]{1,0:T(8,128)S(1)} collective-permute-done((f32[160,128]{1,0:T(8,128)S(1)}, f32[160,128]{1,0:T(8,128)S(1)}, u32[]{:S(2)}, u32[]{:S(2)}) %collective-permute-start.10) | collective-permute-done | bytes 81952 | tf_op jit(solution)/shard_map/ppermute | solution.py:460
  75.7 2.2 %restore.7.both = f32[32,2048]{1,0:T(8,128)S(1)} custom-call(s32[16,128]{1,0:T(8,128)S(1)} %bitcast.24, f32[32,2048]{1,0:T(8,128)S(1)} %collective-permute-done.6.both.source), custom_call_target="tpu_custom_call" | custom-call | tf_op jit(solution)/shard_map/restore/pallas_call | solution.py:449
  77.9 2.2 %collective-permute-done.11 = f32[160,128]{1,0:T(8,128)S(1)} collective-permute-done((f32[160,128]{1,0:T(8,128)S(1)}, f32[160,128]{1,0:T(8,128)S(1)}, u32[]{:S(2)}, u32[]{:S(2)}) %collective-permute-start.11) | collective-permute-done | bytes 81952 | tf_op jit(solution)/shard_map/ppermute | solution.py:460
  80.5 5.6 %collective-permute-done.12 = f32[160,128]{1,0:T(8,128)S(1)} collective-permute-done((f32[160,128]{1,0:T(8,128)S(1)}, f32[160,128]{1,0:T(8,128)S(1)}, u32[]{:S(2)}, u32[]{:S(2)}) %collective-permute-start.12) | collective-permute-done | bytes 81952 | tf_op jit(solution)/shard_map/ppermute | solution.py:460
  89.5 4.4 %collective-permute-done.14 = f32[160,128]{1,0:T(8,128)S(1)} collective-permute-done((f32[160,128]{1,0:T(8,128)S(1)}, f32[160,128]{1,0:T(8,128)S(1)}, u32[]{:S(2)}, u32[]{:S(2)}) %collective-permute-start.14) | collective-permute-done | bytes 81952 | tf_op jit(solution)/shard_map/ppermute | solution.py:460
  93.9 9.2 %solve.1.mixing = f32[32,128]{1,0:T(8,128)S(1)} custom-call(f32[160,128]{1,0:T(8,128)S(1)} %add.24.packed), custom_call_target="tpu_custom_call" | custom-call | tf_op jit(solution)/shard_map/solve/pallas_call | solution.py:486
  103.2 8.5 %update.1 = f32[256,2048]{1,0:T(8,128)} custom-call(s32[1]{0:T(128)} %bitcast.g.g_ref, f32[32,128]{1,0:T(8,128)S(1)} %solve.1.mixing, f32[256,2048]{1,0:T(8,128)S(1)} %bitcast.18, f32[256,2048]{1,0:T(8,128)S(1)} %collective-permute-done.15.core, f32[128,2048]{1,0:T(8,128)S(1)} %collective-permute-done.8.chip, f32[128,2048]{1,0:T(8,128)S(1)} %collective-permute-done.16.both, ...), custom_call_target="tpu_custom_call" | custom-call | tf_op jit(solution)/shard_map/update/pallas_call | solution.py:492
  (49 shorter events, 15.3 us)
Async XLA Ops:
  0.6 10.8 %copy-start = (f32[32,8,2048]{2,1,0:T(8,128)S(1)}, f32[32,8,2048]{2,1,0:T(8,128)}, u32[]{:S(2)}) copy-start(f32[32,8,2048]{2,1,0:T(8,128)} %param.5) | copy-start | bytes 6291460
  4.2 9.4 %slice-start = ((s32[2048,8]{0,1:T(8,128)}), s32[2048,1]{0,1:T(1,128)S(1)}, s32[]{:S(2)}) async-start(s32[2048,8]{0,1:T(8,128)} %param.7), calls=%async_computation | async-start | bytes 16384 | tf_op jit(solution)/shard_map/slice | solution.py:357
  4.2 16.6 %collective-permute-start = (f32[32,2048]{1,0:T(8,128)}, f32[32,2048]{1,0:T(8,128)S(1)}, u32[]{:S(2)}, u32[]{:S(2)}) collective-permute-start(f32[32,2048]{1,0:T(8,128)} %get-tuple-element.56), channel_id=1, source_target_pairs={{0,1},{1,0},{2,3},{3,2},{4,5},{5,4},{6,7},{7,6},{8,9},{9,8},{10,11... | collective-permute-start | bytes 786440 | tf_op jit(solution)/shard_map/ppermute | solution.py:343
  5.1 15.7 %collective-permute-start.1 = (f32[32,2048]{1,0:T(8,128)}, f32[32,2048]{1,0:T(8,128)}, u32[]{:S(2)}, u32[]{:S(2)}) collective-permute-start(f32[32,2048]{1,0:T(8,128)} %get-tuple-element.61), channel_id=1, source_target_pairs={{1,2},{2,1},{3,4},{4,3},{5,6},{6,5},{7,8},{8,7},{9,10},{10,9},{11,... | collective-permute-start | bytes 786440 | tf_op jit(solution)/shard_map/ppermute | solution.py:342
  12.5 49.4 %collective-permute-start.8 = (f32[128,2048]{1,0:T(8,128)}, f32[128,2048]{1,0:T(8,128)S(1)}, u32[]{:S(2)}, u32[]{:S(2)}) collective-permute-start(f32[128,2048]{1,0:T(8,128)} %slice_bitcast_fusion), channel_id=1, source_target_pairs={{0,64},{32,96},{64,0},{96,32},{1,65},{33,97},{65,1},{97,33},{2,66}... | collective-permute-start | bytes 3145736 | tf_op jit(solution)/shard_map/ppermute | solution.py:355
  15.2 1.6 %copy-start.1 = (f32[32,8,2048]{2,1,0:T(8,128)S(1)}, f32[32,8,2048]{2,1,0:T(8,128)}, u32[]{:S(2)}) copy-start(f32[32,8,2048]{2,1,0:T(8,128)} %param.6) | copy-start | bytes 6291460
  20.8 10.1 %copy-start.3 = (f32[2048]{0:T(1024)S(1)}, f32[2048]{0:T(1024)}, u32[]{:S(2)}) copy-start(f32[2048]{0:T(1024)} %param.9) | copy-start | bytes 24580
  20.8 12.6 %copy-start.2 = (f32[128,2048]{1,0:T(8,128)S(1)}, f32[128,2048]{1,0:T(8,128)}, u32[]{:S(2)}) copy-start(f32[128,2048]{1,0:T(8,128)} %source) | copy-start | bytes 3145732
  23.6 12.2 %collective-permute-start.2 = (f32[32,2048]{1,0:T(8,128)S(1)}, f32[32,2048]{1,0:T(8,128)S(1)}, u32[]{:S(2)}, u32[]{:S(2)}) collective-permute-start(f32[32,2048]{1,0:T(8,128)S(1)} %get-tuple-element.66), channel_id=1, source_target_pairs={{0,1},{1,0},{2,3},{3,2},{4,5},{5,4},{6,7},{7,6},{8,9},{9,8},{10,11... | collective-permute-start | bytes 786440 | tf_op jit(solution)/shard_map/ppermute | solution.py:343
  23.7 13.9 %collective-permute-start.3 = (f32[32,2048]{1,0:T(8,128)S(1)}, f32[32,2048]{1,0:T(8,128)S(1)}, u32[]{:S(2)}, u32[]{:S(2)}) collective-permute-start(f32[32,2048]{1,0:T(8,128)S(1)} %get-tuple-element.67), channel_id=1, source_target_pairs={{1,2},{2,1},{3,4},{4,3},{5,6},{6,5},{7,8},{8,7},{9,10},{10,9},{11,... | collective-permute-start | bytes 786440 | tf_op jit(solution)/shard_map/ppermute | solution.py:342
  28.9 17.5 %collective-permute-start.4 = (f32[32,2048]{1,0:T(8,128)S(1)}, f32[32,2048]{1,0:T(8,128)S(1)}, u32[]{:S(2)}, u32[]{:S(2)}) collective-permute-start(f32[32,2048]{1,0:T(8,128)S(1)} %get-tuple-element.80), channel_id=1, source_target_pairs={{1,0},{2,1},{3,2},{4,3},{5,4},{6,5},{7,6},{8,7},{9,8},{10,9},{11,1... | collective-permute-start | bytes 786440 | tf_op jit(solution)/shard_map/ppermute | solution.py:380
  48.1 11.4 %collective-permute-start.5 = (f32[32,2048]{1,0:T(8,128)S(1)}, f32[32,2048]{1,0:T(8,128)S(1)}, u32[]{:S(2)}, u32[]{:S(2)}) collective-permute-start(f32[32,2048]{1,0:T(8,128)S(1)} %finish.1.source.own), channel_id=1, source_target_pairs={{0,64},{32,96},{64,0},{96,32},{1,65},{33,97},{65,1},{97,33},{2,66}... | collective-permute-start | bytes 786440 | tf_op jit(solution)/shard_map/ppermute | solution.py:427
  50.1 11.8 %collective-permute-start.7 = (f32[32,2048]{1,0:T(8,128)S(1)}, f32[32,2048]{1,0:T(8,128)S(1)}, u32[]{:S(2)}, u32[]{:S(2)}) collective-permute-start(f32[32,2048]{1,0:T(8,128)S(1)} %finish.1.source.own), channel_id=1, source_target_pairs={{0,32},{32,0},{64,96},{96,64},{1,33},{33,1},{65,97},{97,65},{2,34}... | collective-permute-start | bytes 786440 | tf_op jit(solution)/shard_map/ppermute | solution.py:428
  59.5 3.5 %collective-permute-start.6 = (f32[32,2048]{1,0:T(8,128)S(1)}, f32[32,2048]{1,0:T(8,128)S(1)}, u32[]{:S(2)}, u32[]{:S(2)}) collective-permute-start(f32[32,2048]{1,0:T(8,128)S(1)} %collective-permute-done.5.chip.source), channel_id=1, source_target_pairs={{0,32},{32,0},{64,96},{96,64},{1,33},{33,1},{65,97},{97,65},{2,34}... | collective-permute-start | bytes 786440 | tf_op jit(solution)/shard_map/ppermute | solution.py:429
  61.9 25.7 %collective-permute-start.13 = (f32[128,2048]{1,0:T(8,128)S(1)}, f32[128,2048]{1,0:T(8,128)S(1)}, u32[]{:S(2)}, u32[]{:S(2)}) collective-permute-start(f32[128,2048]{1,0:T(8,128)S(1)} %slice.21), channel_id=1, source_target_pairs={{0,64},{32,96},{64,0},{96,32},{1,65},{33,97},{65,1},{97,33},{2,66}... | collective-permute-start | bytes 3145736 | tf_op jit(solution)/shard_map/ppermute | solution.py:435
  64.4 38.8 %collective-permute-start.15 = (f32[256,2048]{1,0:T(8,128)S(1)}, f32[256,2048]{1,0:T(8,128)S(1)}, u32[]{:S(2)}, u32[]{:S(2)}) collective-permute-start(f32[256,2048]{1,0:T(8,128)S(1)} %bitcast.17), channel_id=1, source_target_pairs={{0,32},{32,0},{64,96},{96,64},{1,33},{33,1},{65,97},{97,65},{2,34}... | collective-permute-start | bytes 6291464 | tf_op jit(solution)/shard_map/ppermute | solution.py:458
  64.7 4.6 %collective-permute-start.9 = (f32[160,128]{1,0:T(8,128)S(1)}, f32[160,128]{1,0:T(8,128)S(1)}, u32[]{:S(2)}, u32[]{:S(2)}) collective-permute-start(f32[160,128]{1,0:T(8,128)S(1)} %product.1), channel_id=1, source_target_pairs={{0,1},{1,0},{2,3},{3,2},{4,5},{5,4},{6,7},{7,6},{8,9},{9,8},{10,11... | collective-permute-start | bytes 245768 | tf_op jit(solution)/shard_map/ppermute | solution.py:460
  69.4 6.0 %collective-permute-start.10 = (f32[160,128]{1,0:T(8,128)S(1)}, f32[160,128]{1,0:T(8,128)S(1)}, u32[]{:S(2)}, u32[]{:S(2)}) collective-permute-start(f32[160,128]{1,0:T(8,128)S(1)} %add.20), channel_id=1, source_target_pairs={{0,2},{1,3},{2,0},{3,1},{4,6},{5,7},{6,4},{7,5},{8,10},{9,11},{10,... | collective-permute-start | bytes 245768 | tf_op jit(solution)/shard_map/ppermute | solution.py:460
  75.4 4.7 %collective-permute-start.11 = (f32[160,128]{1,0:T(8,128)S(1)}, f32[160,128]{1,0:T(8,128)S(1)}, u32[]{:S(2)}, u32[]{:S(2)}) collective-permute-start(f32[160,128]{1,0:T(8,128)S(1)} %add.21), channel_id=1, source_target_pairs={{0,8},{1,9},{2,10},{3,11},{4,12},{5,13},{6,14},{7,15},{8,0},{9,1},... | collective-permute-start | bytes 245768 | tf_op jit(solution)/shard_map/ppermute | solution.py:460
  80.1 6.0 %collective-permute-start.12 = (f32[160,128]{1,0:T(8,128)S(1)}, f32[160,128]{1,0:T(8,128)S(1)}, u32[]{:S(2)}, u32[]{:S(2)}) collective-permute-start(f32[160,128]{1,0:T(8,128)S(1)} %add.22), channel_id=1, source_target_pairs={{0,16},{1,17},{2,18},{3,19},{4,20},{5,21},{6,22},{7,23},{8,24},{9,... | collective-permute-start | bytes 245768 | tf_op jit(solution)/shard_map/ppermute | solution.py:460
  80.5 22.6 %collective-permute-start.16 = (f32[128,2048]{1,0:T(8,128)S(1)}, f32[128,2048]{1,0:T(8,128)S(1)}, u32[]{:S(2)}, u32[]{:S(2)}) collective-permute-start(f32[128,2048]{1,0:T(8,128)S(1)} %collective-permute-done.8.chip), channel_id=1, source_target_pairs={{0,32},{32,0},{64,96},{96,64},{1,33},{33,1},{65,97},{97,65},{2,34}... | collective-permute-start | bytes 3145736 | tf_op jit(solution)/shard_map/ppermute | solution.py:436
  87.5 15.6 %collective-permute-start.17 = (f32[128,2048]{1,0:T(8,128)S(1)}, f32[128,2048]{1,0:T(8,128)S(1)}, u32[]{:S(2)}, u32[]{:S(2)}) collective-permute-start(f32[128,2048]{1,0:T(8,128)S(1)} %collective-permute-done.13.chip2), channel_id=1, source_target_pairs={{0,32},{32,0},{64,96},{96,64},{1,33},{33,1},{65,97},{97,65},{2,34}... | collective-permute-start | bytes 3145736 | tf_op jit(solution)/shard_map/ppermute | solution.py:474
  87.5 6.4 %collective-permute-start.14 = (f32[160,128]{1,0:T(8,128)S(1)}, f32[160,128]{1,0:T(8,128)S(1)}, u32[]{:S(2)}, u32[]{:S(2)}) collective-permute-start(f32[160,128]{1,0:T(8,128)S(1)} %add.23), channel_id=1, source_target_pairs={{0,4},{1,5},{2,6},{3,7},{4,0},{5,1},{6,2},{7,3},{8,12},{9,13},{10,... | collective-permute-start | bytes 245768 | tf_op jit(solution)/shard_map/ppermute | solution.py:460

commit v3 on v2

v3 whole, which is shorter than its diff:
```python
import functools

import jax
import jax.numpy as jnp
from jax import lax
from jax.experimental import pallas as pl
from jax.experimental.pallas import tpu as pltpu
from jax.sharding import PartitionSpec as P

LANES = 128
F32 = jnp.float32


def along(axis, shift):
    count = lax.axis_size(axis)
    return [(i, i + shift) for i in range(count) if 0 <= i + shift < count]


def swapped(axis, bit):
    return [(i, i ^ bit) for i in range(lax.axis_size(axis))]


def outflow(speed, rho):
    return 0.2 * (speed * rho * (1.0 - rho)) + 0.1 * rho


def from_left(x):
    lane = lax.broadcasted_iota(jnp.int32, x.shape, 1)
    return jnp.where(lane == 0, 0.0, pltpu.roll(x, 1, 1))


def from_right(x):
    last = x.shape[1] - 1
    lane = lax.broadcasted_iota(jnp.int32, x.shape, 1)
    return jnp.where(lane == last, 0.0, pltpu.roll(x, last, 1))


def without_above(rho, out, below):
    return 0.8 * rho - 2.0 * out + from_left(out) + 0.1 * (below + from_right(rho))


def box4(x):
    n = x.shape[1]
    pair = x + pltpu.roll(x, n - 1, 1)
    return pair + pltpu.roll(pair, n - 2, 1)


def load_columns(source, target, sems):
    copies = []
    for b in range(source.shape[1] // LANES):
        copy = pltpu.make_async_copy(source.at[:, pl.ds(b * LANES, LANES)], target.at[b], sems.at[b])
        copy.start()
        copies.append(copy)
    return copies


def prep_kernel(rows, odd, theta, rho, low_pair, high_pair, theta_a, theta_b, theta_in, rho_in, sems):
    waits = load_columns(rho, rho_in, sems.at[0]), load_columns(theta, theta_in, sems.at[1])
    members = low_pair.shape[0]
    half = theta_a.shape[0]
    swap = odd[0] == 1
    for b in range(theta_in.shape[0]):
        at = slice(b * LANES, (b + 1) * LANES)
        waits[0][b].wait()
        waits[1][b].wait()
        speed = [theta_in[b, pl.ds(r, members, stride=rows), :] for r in range(rows)]
        first, last = (rho_in[b, pl.ds(r, members, stride=rows), :] for r in (0, rows - 1))
        for r in range(rows):
            if r < half:
                theta_a[r, :, at] = speed[r]
            else:
                theta_b[r - half, :, at] = speed[r]
        down = outflow(speed[-1], last)
        low_pair[:, at] = jnp.where(swap, first, down)
        high_pair[:, at] = jnp.where(swap, down, first)


def rows_of(theta_a, theta_b, at):
    return [ref[r, at, :] for ref in (theta_a, theta_b) for r in range(ref.shape[0])]


def advance(speed, rho):
    out = [outflow(s, x) for s, x in zip(speed, rho)]
    new = []
    for r, x in enumerate(rho):
        under = rho[r + 1] + from_right(x) if r + 1 < len(rho) else from_right(x)
        y = 0.8 * x - 2.0 * out[r] + from_left(out[r]) + 0.1 * under
        new.append(y + out[r - 1] if r else y)
    return new, out


def inner1_kernel(theta_a, theta_b, rho, rho1, rho_in, sems):
    rows, members, _ = rho1.shape
    for b, copy in enumerate(load_columns(rho, rho_in, sems)):
        copy.wait()
        for r in range(rows):
            rho1[r, :, b * LANES : (b + 1) * LANES] = rho_in[b, pl.ds(r, members, stride=rows), :]

    def chunk(c, carry):
        at = pl.ds(c * 8, 8)
        new, _ = advance(rows_of(theta_a, theta_b, at), [rho1[r, at, :] for r in range(rows)])
        for r in range(rows):
            rho1[r, at, :] = new[r]
        return carry

    lax.fori_loop(0, members // 8, chunk, 0)


def edge1_kernel(odd, theta_a, theta_b, rho1, from_low, from_high, low_pair, high_pair, part, first, last):
    rows, members, _ = rho1.shape
    swap = odd[0] == 1

    def chunk(c, carry):
        at = pl.ds(c * 8, 8)
        low, high = from_low[at, :], from_high[at, :]
        top = rho1[0, at, :] + jnp.where(swap, low, high)
        bottom = rho1[rows - 1, at, :] + 0.1 * jnp.where(swap, high, low)
        down = outflow(theta_b[theta_b.shape[0] - 1, at, :], bottom)
        low_pair[at, :] = jnp.where(swap, top, down)
        high_pair[at, :] = jnp.where(swap, down, top)
        part[at, :] = without_above(top, outflow(theta_a[0, at, :], top), rho1[1, at, :])
        first[at, :] = top
        last[at, :] = bottom
        return carry

    lax.fori_loop(0, members // 8, chunk, 0)


def pick(table, first, last, low, high, pos_ref, start, out_ref):
    members = out_ref.shape[0]
    parts = members // 8
    width = 4
    for g0 in range(0, pos_ref.shape[0], width):
        groups = range(g0, g0 + width)
        where = [jnp.broadcast_to(pos_ref[g : g + 1, :], (8, LANES)) for g in groups]
        lane = [w & (LANES - 1) for w in where]
        block = [w >> 7 for w in where]
        begin = [jnp.maximum(low[g], first) for g in groups]
        trips = functools.reduce(
            jnp.maximum, [jnp.minimum(high[g], last) + 1 - lo for g, lo in zip(groups, begin)]
        )
        init = tuple(
            start[i * 8 : i * 8 + 8, g * LANES : (g + 1) * LANES] if start is not None else jnp.zeros((8, LANES), F32)
            for g in groups
            for i in range(parts)
        )

        def look(t, acc):
            new = []
            for k in range(width):
                p = begin[k] + t
                at = jnp.minimum(p, last) - first
                hit = block[k] == jnp.where(p <= last, p, -1)
                for i in range(parts):
                    row = table[at, i * 8 : i * 8 + 8, :]
                    got = jnp.take_along_axis(row, lane[k], axis=1, mode="promise_in_bounds")
                    new.append(jnp.where(hit, got, acc[k * parts + i]))
            return tuple(new)

        acc = lax.fori_loop(0, trips, look, init)
        for k, g in enumerate(groups):
            for i in range(parts):
                out_ref[i * 8 : i * 8 + 8, g * LANES : (g + 1) * LANES] = acc[k * parts + i]


def reorder_kernel(index, source, out, extra=None, extra_out=None):
    members = out.shape[0]
    groups = index.shape[0]

    def one(g, carry):
        where = jnp.broadcast_to(index[pl.ds(g, 1), :], (8, LANES))
        lane = where & (LANES - 1)
        block = where >> 7
        at = pl.ds(pl.multiple_of(g * LANES, LANES), LANES)
        for i in range(0, members, 8):
            acc = jnp.zeros((8, LANES), F32)
            for h in range(groups):
                row = source[i : i + 8, h * LANES : (h + 1) * LANES]
                got = jnp.take_along_axis(row, lane, axis=1, mode="promise_in_bounds")
                acc = jnp.where(block == h, got, acc)
            out[i : i + 8, at] = acc
        if extra is not None:
            acc = jnp.zeros((8, LANES), F32)
            for h in range(groups):
                row = jnp.broadcast_to(extra[:, h * LANES : (h + 1) * LANES], (8, LANES))
                got = jnp.take_along_axis(row, lane, axis=1, mode="promise_in_bounds")
                acc = jnp.where(block == h, got, acc)
            extra_out[:, at] = acc[:1]
        return carry

    lax.fori_loop(0, groups, one, 0)


def store_sums(table, row, at, x):
    sums = box4(x)
    blocks = x.shape[1] // LANES
    for b in range(blocks):
        table[row * blocks + b, at, :] = sums[:, b * LANES : (b + 1) * LANES]


def inner2_kernel(theta_a, theta_b, rho, first, last, pos, low, high, counts, head, tail, rest, table):
    rows, members, columns = rho.shape
    blocks = columns // LANES

    def chunk(c, carry):
        at = pl.ds(c * 8, 8)
        now = [first[at, :]] + [rho[r, at, :] for r in range(1, rows - 1)] + [last[at, :]]
        new, out = advance(rows_of(theta_a, theta_b, at), now)
        head[at, :] = new[0] + new[1]
        tail[at, :] = new[rows - 2] + new[rows - 1]
        rest[at, :] = new[rows - 1] + out[rows - 1]
        for r in range(1, rows - 2):
            store_sums(table, r - 1, at, new[r] + new[r + 1])
        return carry

    lax.fori_loop(0, members // 8, chunk, 0)
    pick(table, blocks, (rows - 2) * blocks - 1, low, high, pos, None, counts)


def edge2_kernel(rows, odd, head, tail, from_low, from_high, pos, low, high, counts, more, table):
    members, columns = head.shape
    blocks = columns // LANES
    swap = odd[0] == 1
    for c in range(0, members, 8):
        at = pl.ds(c, 8)
        one, two = from_low[at, :], from_high[at, :]
        store_sums(table, 0, at, head[at, :] + jnp.where(swap, one, two))
        store_sums(table, 1, at, tail[at, :] + 0.1 * jnp.where(swap, two, one))
    pick(table, 0, blocks - 1, low, high, pos, counts, more)
    pick(table.at[pl.ds(blocks, blocks)], (rows - 2) * blocks, (rows - 1) * blocks - 1, low, high, pos, more, more)


def finish_kernel(first, odd, rest, from_low, from_high, part, pos, low, high, counts, mine, table):
    members, columns = rest.shape
    blocks = columns // LANES
    swap = odd[0] == 1
    for c in range(0, members, 8):
        at = pl.ds(c, 8)
        beneath = jnp.where(swap, from_high[at, :], from_low[at, :])
        store_sums(table, 0, at, rest[at, :] + 0.1 * beneath + part[at, :])
    pick(table, first, first + blocks - 1, low, high, pos, counts, mine)


def product_kernel(total, g_ref, own, core, chip, both, perturbed, noise, packed, every):
    members, sensors = own.shape
    g = g_ref[0]
    for step, piece in enumerate((own, core, chip, both)):
        every[pl.ds(pl.multiple_of((g ^ step) * members, members), members), :] = piece[...]
    width = 512
    acc = None
    for s in range(0, sensors, width):
        at = slice(s, s + width)
        counts = every[:, at]
        anomaly = counts - jnp.sum(counts, axis=0, keepdims=True) / total
        weighted = anomaly / noise[:, at]
        left = jnp.concatenate([anomaly, perturbed[:, at] - own[:, at]], axis=0)
        term = lax.dot_general(
            left, weighted, (((1,), (1,)), ((), ())), precision=lax.Precision.HIGHEST, preferred_element_type=F32
        )
        acc = term if acc is None else acc + term
    packed[...] = acc


def lane_of(x, k):
    return jnp.take_along_axis(x, jnp.full(x.shape, k, jnp.int32), axis=1, mode="promise_in_bounds")


def sublane_of(x, r):
    return jnp.broadcast_to(x[r : r + 1, :], x.shape)


def solve_kernel(shift, packed, mixing_t):
    n = packed.shape[1]
    lane = lax.broadcasted_iota(jnp.int32, (8, n), 1)
    sub = lax.broadcasted_iota(jnp.int32, (8, n), 0)
    a = []
    for i in range(packed.shape[0] // 8):
        x = packed[i * 8 : i * 8 + 8, :]
        a.append(jnp.where(lane == sub + i * 8, x + shift, x) if i * 8 < n else x)
    keep = jnp.zeros((8, n), F32)
    mix = jnp.zeros((8, n), F32)
    for k in range(0, n, 2):
        r = k % 8
        top = a[k // 8]
        c0, c1 = lane_of(top, k), lane_of(top, k + 1)
        r0, r1 = sublane_of(top, r), sublane_of(top, r + 1)
        p00, p01, p10, p11 = sublane_of(c0, r), sublane_of(c1, r), sublane_of(c0, r + 1), sublane_of(c1, r + 1)
        scale = 1.0 / (p00 * p11 - p01 * p10)
        here = (lane == k) | (lane == k + 1)
        f0 = jnp.where(here, 0.0, scale * (p11 * r0 - p01 * r1))
        f1 = jnp.where(here, 0.0, scale * (p00 * r1 - p10 * r0))
        keep = jnp.where(lane == k, scale * p11, jnp.where(lane == k + 1, scale * p00, keep))
        mix = jnp.where(lane == k, -(scale * p10), jnp.where(lane == k + 1, -(scale * p01), mix))
        for i in range(k // 8, len(a)):
            if i > k // 8:
                c0, c1 = lane_of(a[i], k), lane_of(a[i], k + 1)
            a[i] = a[i] - (c0 * f0 + c1 * f1)
    even = (lane & 1) == 0
    for i in range(n // 8, len(a)):
        x = a[i]
        other = jnp.where(even, pltpu.roll(x, n - 1, 1), pltpu.roll(x, 1, 1))
        w = x * keep + other * mix
        w = w - jnp.sum(w, axis=1, keepdims=True) / n
        at = i * 8 - n
        mixing_t[at : at + 8, :] = w


def split(x):
    high = x.astype(jnp.bfloat16)
    return high, (x - high.astype(F32)).astype(jnp.bfloat16)


def update_kernel(g_ref, mixing, *refs):
    pieces, (out, new, sems) = (refs[:4], refs[4:8]), refs[8:]
    half, members, columns = pieces[0][0].shape
    rows = half + pieces[1][0].shape[0]
    g = g_ref[0]
    wt = mixing[...]
    n = wt.shape[1]
    lane = lax.broadcasted_iota(jnp.int32, wt.shape, 1)
    crossed = jnp.where((lane & members) == 0, pltpu.roll(wt, n - members, 1), pltpu.roll(wt, members, 1))
    wt = jnp.where((g & 1) == 1, crossed, wt)
    wt = jnp.where((g & 2) == 2, pltpu.roll(wt, n // 2, 1), wt)
    wh, wl = split(wt)
    both = jnp.concatenate([wh, wl], axis=0)
    width = 2 * LANES
    sent = []
    for c in range(0, columns, width):
        for r in range(rows):
            x = [piece[r % half if r < half else r - half, :, c : c + width] for piece in pieces[r >= half]]
            xh, xl = split(jnp.concatenate(x, axis=0))
            high = jnp.dot(both, xh, preferred_element_type=F32)
            y = x[0] + (high[:members] + high[members:] + jnp.dot(wh, xl, preferred_element_type=F32))
            for k in range(width // LANES):
                new[c // LANES + k, pl.ds(r, members, stride=rows), :] = y[:, k * LANES : (k + 1) * LANES]
        for b in range(c // LANES, (c + width) // LANES):
            copy = pltpu.make_async_copy(new.at[b], out.at[:, pl.ds(b * LANES, LANES)], sems.at[b])
            copy.start()
            sent.append(copy)
    for copy in sent:
        copy.wait()


def tie(*values):
    return lax.optimization_barrier(values)


def kernel_params(mib):
    return pltpu.CompilerParams(vmem_limit_bytes=mib * 1024 * 1024)


def body(theta, density, footprint, perturbed, noise_var):
    members, rows, columns = theta.shape
    total = members * lax.axis_size("grp")
    sensors = footprint.shape[0]
    slab = rows * columns
    blocks = columns // LANES
    groups = sensors // LANES
    flat_theta = theta.reshape(members * rows, columns)
    flat_rho = density.reshape(members * rows, columns)
    g = lax.axis_index("grp").astype(jnp.int32).reshape(1)
    row = jax.ShapeDtypeStruct((members, columns), F32)
    turned = jax.ShapeDtypeStruct((rows, members, columns), F32)
    counts_shape = jax.ShapeDtypeStruct((members, sensors), F32)
    anywhere = pl.BlockSpec(memory_space=pltpu.HBM)
    vmem = pl.BlockSpec(memory_space=pltpu.VMEM)
    smem = pl.BlockSpec(memory_space=pltpu.SMEM)
    columns_of = pltpu.VMEM((blocks, members * rows, LANES), F32)

    odd = (lax.axis_index("cell") & 1).astype(jnp.int32).reshape(1)
    count = lax.axis_size("cell")
    far = [(i, i + 1 if i & 1 else i - 1) for i in range(1, count - 1)]

    def both_ways(low_pair, high_pair):
        from_low = lax.ppermute(low_pair, "cell", swapped("cell", 1))
        from_high = lax.ppermute(high_pair, "cell", far)
        return from_low, from_high

    early, late = (jax.ShapeDtypeStruct((n, members, columns), F32) for n in (rows * 3 // 8, rows - rows * 3 // 8))
    down, top, theta_a, theta_b = pl.pallas_call(
        functools.partial(prep_kernel, rows),
        in_specs=[smem, anywhere, anywhere],
        out_shape=[row, row, early, late],
        scratch_shapes=[columns_of, columns_of, pltpu.SemaphoreType.DMA((2, blocks))],
        name="prep",
        compiler_params=kernel_params(16),
    )(odd, flat_theta, flat_rho)
    above, below = both_ways(down, top)
    chip_a = lax.ppermute(theta_a, "grp", swapped("grp", 2))

    first = footprint[:, 0]
    rho1 = pl.pallas_call(
        inner1_kernel,
        in_specs=[vmem, vmem, anywhere],
        out_shape=turned,
        scratch_shapes=[columns_of, pltpu.SemaphoreType.DMA((blocks,))],
        name="inner1",
        compiler_params=kernel_params(12),
    )(theta_a, theta_b, flat_rho)
    rho1, first = tie(rho1, first)
    key = (first - lax.axis_index("cell") * slab) * sensors + lax.iota(jnp.int32, sensors)
    rank = jnp.sum((key[:, None] < key[None, :]).astype(jnp.int32), axis=0)
    chosen = rank[:, None] == lax.iota(jnp.int32, sensors)[None, :]
    ordered = jnp.sum(jnp.where(chosen, key[:, None], 0), axis=0)
    pos = (ordered // sensors).reshape(groups, LANES)
    order = (ordered & (sensors - 1)).reshape(groups, LANES)
    rank = rank.reshape(groups, LANES)
    low = pos[:, 0] >> 7
    high = pos[:, LANES - 1] >> 7
    above, below, pos, order, low, high, rank, rho1 = tie(above, below, pos, order, low, high, rank, rho1)

    low_pair, high_pair, part, first, last = pl.pallas_call(
        edge1_kernel,
        in_specs=[smem] + [vmem] * 5,
        out_shape=[row] * 5,
        name="edge1",
        compiler_params=kernel_params(12),
    )(odd, theta_a, theta_b, rho1, above, below)
    above, below = both_ways(low_pair, high_pair)
    part = lax.ppermute(part, "cell", along("cell", -1))

    counts, head, tail, rest = pl.pallas_call(
        inner2_kernel,
        in_specs=[vmem] * 6 + [smem] * 2,
        out_shape=[counts_shape, row, row, row],
        scratch_shapes=[pltpu.VMEM(((rows - 3) * blocks, members, LANES), F32)],
        name="inner2",
        compiler_params=kernel_params(14),
    )(theta_a, theta_b, rho1, first, last, pos, low, high)
    above, below, counts, head, tail, rest = tie(above, below, counts, head, tail, rest)
    counts = pl.pallas_call(
        functools.partial(edge2_kernel, rows),
        in_specs=[smem] + [vmem] * 5 + [smem] * 2 + [vmem],
        out_shape=counts_shape,
        scratch_shapes=[pltpu.VMEM((2 * blocks, members, LANES), F32)],
        name="edge2",
        compiler_params=kernel_params(6),
    )(odd, head, tail, above, below, pos, low, high, counts)
    counts, part = tie(counts, part)
    own = pl.pallas_call(
        functools.partial(finish_kernel, (rows - 1) * blocks),
        in_specs=[smem] + [vmem] * 5 + [smem] * 2 + [vmem],
        out_shape=counts_shape,
        scratch_shapes=[pltpu.VMEM((blocks, members, LANES), F32)],
        name="finish",
        compiler_params=kernel_params(6),
    )(odd, rest, above, below, part, pos, low, high, counts)

    def restore(counts):
        return pl.pallas_call(
            reorder_kernel, out_shape=counts_shape, name="restore", compiler_params=kernel_params(4)
        )(rank, counts)

    chip = lax.ppermute(own, "grp", swapped("grp", 2))
    core = lax.ppermute(own, "grp", swapped("grp", 1))
    own, perturbed = tie(own, perturbed)
    perturbed_own, noise = pl.pallas_call(
        lambda g, index, source, extra, out, extra_out: reorder_kernel(index, source, out, extra, extra_out),
        grid_spec=pltpu.PrefetchScalarGridSpec(
            num_scalar_prefetch=1,
            grid=(1,),
            in_specs=[
                pl.BlockSpec((groups, LANES), lambda i, g: (0, 0)),
                pl.BlockSpec((members, sensors), lambda i, g: (g[0], 0)),
                pl.BlockSpec((1, sensors), lambda i, g: (0, 0)),
            ],
            out_specs=[
                pl.BlockSpec((members, sensors), lambda i, g: (0, 0)),
                pl.BlockSpec((1, sensors), lambda i, g: (0, 0)),
            ],
        ),
        out_shape=[counts_shape, jax.ShapeDtypeStruct((1, sensors), F32)],
        name="reorder",
        compiler_params=kernel_params(4),
    )(g, order, perturbed, noise_var.reshape(1, sensors))
    chip, perturbed_own = tie(chip, perturbed_own)
    both = lax.ppermute(chip, "grp", swapped("grp", 1))
    core, both, chip_a, theta_b = tie(core, both, chip_a, theta_b)
    chip_b = lax.ppermute(theta_b, "grp", swapped("grp", 2))
    both_a = lax.ppermute(chip_a, "grp", swapped("grp", 1))
    packed = pl.pallas_call(
        functools.partial(product_kernel, total),
        in_specs=[smem] + [vmem] * 6,
        out_shape=jax.ShapeDtypeStruct((total + members, total), F32),
        scratch_shapes=[pltpu.VMEM((total, sensors), F32)],
        name="product",
        compiler_params=kernel_params(12),
    )(g, own, core, chip, both, perturbed_own, noise)

    theta_a, packed = tie(theta_a, packed)

    def assemble(g_ref, own, core, chip, both, out):
        g = g_ref[0]
        for step, piece in enumerate((own, core, chip, both)):
            out[pl.ds(pl.multiple_of((g ^ step) * members, members), members), :] = piece[...]

    core_a = lax.ppermute(theta_a, "grp", swapped("grp", 1))
    core_b = lax.ppermute(theta_b, "grp", swapped("grp", 1))
    for stage, bit in enumerate((1, 2, 8, 16, 4)):
        other = lax.ppermute(packed, "cell", swapped("cell", bit))
        if stage == 0:
            core, packed = tie(core, packed)
            core = restore(core)
            other, core = tie(other, core)
        if stage == 1:
            chip, packed = tie(chip, packed)
            chip = restore(chip)
            other, chip = tie(other, chip)
        if stage == 2:
            both, packed = tie(both, packed)
            both = restore(both)
            other, both = tie(other, both)
        if stage == 3:
            own, packed = tie(own, packed)
            mine = restore(own)
            other, mine = tie(other, mine)
        if stage == 4:
            predicted = pl.pallas_call(
                assemble,
                in_specs=[smem] + [vmem] * 4,
                out_shape=jax.ShapeDtypeStruct((total, sensors), F32),
                name="assemble",
                compiler_params=kernel_params(4),
            )(g, mine, core, chip, both)
            other, predicted = tie(other, predicted)
        packed = packed + other
    packed, chip_b = tie(packed, chip_b)
    both_b = lax.ppermute(chip_b, "grp", swapped("grp", 1))
    mixing_t = pl.pallas_call(
        functools.partial(solve_kernel, total - 1.0),
        out_shape=jax.ShapeDtypeStruct((members, total), F32),
        name="solve",
        compiler_params=kernel_params(4),
    )(packed)
    new = pl.pallas_call(
        update_kernel,
        in_specs=[smem] + [vmem] * 9,
        out_specs=anywhere,
        out_shape=jax.ShapeDtypeStruct((members * rows, columns), F32),
        scratch_shapes=[columns_of, pltpu.SemaphoreType.DMA((blocks,))],
        name="update",
        compiler_params=kernel_params(16),
    )(g, mixing_t, theta_a, core_a, chip_a, both_a, theta_b, core_b, chip_b, both_b)
    return (new.reshape(members, rows, columns), predicted)


def solution(mesh):
    return jax.shard_map(
        body,
        mesh=mesh,
        in_specs=(
            P("grp", "cell", None),
            P("grp", "cell", None),
            P("cell", None),
            P(None, "cell"),
            P("cell"),
        ),
        out_specs=(P("grp", "cell", None), P(None, "cell")),
        check_vma=False,
    )
```

time: 112 us -> 107 us (0.955)
  Pallas kernels: 49.9 us -> 37.6 us
  waiting for transfers between devices: 30.8 us -> 37.7 us
  local copies, waits for them, and re-layouts: 2.74 us -> 6 us
  other arithmetic: 6.61 us -> 4.16 us
  starting transfers between devices: 20.6 us -> 19.4 us
    pallas_call x7, Pallas kernels: 29.7 us -> 18.4 us  [the longest x1 6.17 us: body(): pl.pallas_call(inner2_kernel, in_specs=[vmem] * 6 + [smem] * 2, out_shape...]
    ppermute x1, waiting for transfers between devices: 9.42 us -> 16.8 us  [body(): chip = lax.ppermute(own, 'grp', swapped('grp', 2))]
    unnamed x8 -> x10, local copies, waits for them, and re-layouts: 1.6 us -> 5.99 us
    pallas_call x1, Pallas kernels: 9.25 us -> 6.08 us  [body(): pl.pallas_call(functools.partial(solve_kernel, total - 1.0), out_shape=ja...]
    reduce_sum x1 -> x0, other arithmetic: 2.44 us -> none  [body(): jnp.sum(jnp.where(chosen, noise_var[:, None], 0.0), axis=0)]
    pallas_call x3 -> x4, Pallas kernels: 6.69 us -> 8.92 us  [restore(): pl.pallas_call(reorder_kernel, out_shape=counts_shape, name='restore', co...]
    ppermute x2, waiting for transfers between devices: 1.72 us -> 0.01 us  [both_ways(): from_high = lax.ppermute(high_pair, 'cell', far)]
    ppermute x1, waiting for transfers between devices: 0.01 us -> 1.52 us  [body(): both = lax.ppermute(chip, 'grp', swapped('grp', 1))]
  transfers between devices with their start and end apart: 18 -> 19, of which waited for: 8 -> 8; matrix products, arithmetic and copies ran while one was open for 7% -> 4% of each run, Pallas kernels for 34% -> 31%
where the time goes in v3:
time: 107 us; the launch traced here: 106 us
  waiting for transfers between devices  37.7 us (35%)
  Pallas kernels  37.6 us (35%)
  starting transfers between devices  19.4 us (18%)
  local copies, waits for them, and re-layouts  6 us (6%)
  other arithmetic  4.16 us (4%)
  between operations  1.13 us (1%)
    ppermute x5, waiting for transfers between devices, body(): other = lax.ppermute(packed, 'cell', swapped('cell', bit))  18.1 us
    ppermute x1, waiting for transfers between devices, body(): chip = lax.ppermute(own, 'grp', swapped('grp', 2))  16.8 us
    ppermute x2, starting transfers between devices, both_ways(): from_high = lax.ppermute(high_pair, 'cell', far)  11.6 us
    pallas_call x4, Pallas kernels, restore(): pl.pallas_call(reorder_kernel, out_shape=counts_shape, name='restore', co...  8.92 us
    pallas_call x1, Pallas kernels, body(): pl.pallas_call(inner2_kernel, in_specs=[vmem] * 6 + [smem] * 2, out_shape...  6.17 us
    pallas_call x1, Pallas kernels, body(): pl.pallas_call(functools.partial(solve_kernel, total - 1.0), out_shape=ja...  6.08 us
    unnamed x10, local copies, waits for them, and re-layouts  5.99 us
    pallas_call x1, Pallas kernels, body(): pl.pallas_call(functools.partial(edge2_kernel, rows), in_specs=[smem] + [...  2.91 us
  transfers between devices with their start and end apart: 19, of which 8 were waited for; matrix products, arithmetic and copies ran while one was open for 4% of the time, Pallas kernels for 31%

profile of v3, /device:TPU:22, one launch (start us, length us, event | category | flops | bytes accessed | tf_op | source)
XLA Modules:
  0.0 106.0 jit_solution(8190902836547955636)
XLA Ops:
  0.6 1.6 %copy-done = f32[32,8,2048]{2,1,0:T(8,128)S(1)} copy-done((f32[32,8,2048]{2,1,0:T(8,128)S(1)}, f32[32,8,2048]{2,1,0:T(8,128)}, u32[]{:S(2)}) %copy-start) | copy-done | bytes 2097176
  2.2 1.6 %copy-done.2 = f32[32,8,2048]{2,1,0:T(8,128)S(1)} copy-done((f32[32,8,2048]{2,1,0:T(8,128)S(1)}, f32[32,8,2048]{2,1,0:T(8,128)}, u32[]{:S(2)}) %copy-start.2) | copy-done | bytes 2097176
  6.2 6.4 %collective-permute-start.1 = (f32[32,2048]{1,0:T(8,128)S(1)}, f32[32,2048]{1,0:T(8,128)S(1)}, u32[]{:S(2)}, u32[]{:S(2)}) collective-permute-start(f32[32,2048]{1,0:T(8,128)S(1)} %get-tuple-element.68), channel_id=1, source_target_pairs={{1,2},{2,1},{3,4},{4,3},{5,6},{6,5},{7,8},{8,7},{9,10},{10,9},{11,... | collective-permute-start | bytes 786440 | tf_op jit(solution)/shard_map/ppermute | solution.py:376
  14.2 2.2 %inner1.1.rho1.rho = f32[8,32,2048]{2,1,0:T(8,128)S(1)} custom-call(f32[3,32,2048]{2,1,0:T(8,128)S(1)} %get-tuple-element.124.theta_a.refs_0_, f32[5,32,2048]{2,1,0:T(8,128)S(1)} %get-tuple-element.122.theta_b.refs_4_, f32[256,2048]{1,0:T(8,128)S(1)} %bitcast.26), custom_call_target="tpu_custom_call" | custom-call | tf_op jit(solution)/shard_map/inner1/pallas_call | solution.py:392
  16.4 1.7 %convert_reduce_fusion = s32[2048]{0:T(1024)S(1)} fusion(s32[2048]{0:T(1024)S(1)} %iota_add_fusion), kind=kLoop, calls=%fused_computation.2 | loop fusion | flops 12580864 | bytes 16384 | tf_op jit(solution)/shard_map/reduce_sum | solution.py:402
  18.1 2.2 %select_reduce_fusion = s32[2048]{0:T(1024)S(1)} fusion(s32[2048]{0:T(1024)S(1)} %convert_reduce_fusion, s32[2048]{0:T(1024)S(1)} %iota_add_fusion), kind=kLoop, calls=%fused_computation | loop fusion | flops 12580864 | bytes 24576 | tf_op jit(solution)/shard_map/reduce_sum | solution.py:404
  21.2 5.2 %collective-permute-start.3 = (f32[32,2048]{1,0:T(8,128)S(1)}, f32[32,2048]{1,0:T(8,128)S(1)}, u32[]{:S(2)}, u32[]{:S(2)}) collective-permute-start(f32[32,2048]{1,0:T(8,128)S(1)} %get-tuple-element.75), channel_id=1, source_target_pairs={{1,2},{2,1},{3,4},{4,3},{5,6},{6,5},{7,8},{8,7},{9,10},{10,9},{11,... | collective-permute-start | bytes 786440 | tf_op jit(solution)/shard_map/ppermute | solution.py:376
  26.4 1.9 %collective-permute-start.4 = (f32[32,2048]{1,0:T(8,128)S(1)}, f32[32,2048]{1,0:T(8,128)S(1)}, u32[]{:S(2)}, u32[]{:S(2)}) collective-permute-start(f32[32,2048]{1,0:T(8,128)S(1)} %get-tuple-element.91), channel_id=1, source_target_pairs={{1,0},{2,1},{3,2},{4,3},{5,4},{6,5},{7,6},{8,7},{9,8},{10,9},{11,1... | collective-permute-start | bytes 786440 | tf_op jit(solution)/shard_map/ppermute | solution.py:420
  29.5 6.2 %inner2.1 = (f32[32,2048]{1,0:T(8,128)S(1)}, f32[32,2048]{1,0:T(8,128)S(1)}, f32[32,2048]{1,0:T(8,128)S(1)}, f32[32,2048]{1,0:T(8,128)S(1)}) custom-call(f32[3,32,2048]{2,1,0:T(8,128)S(1)} %get-tuple-element.124.theta_a.refs_0_, f32[5,32,2048]{2,1,0:T(8,128)S(1)} %get-tuple-element.122.theta_b.refs_4_, f32[8,32,2048]{2,1,0:T(8,128)S(1)} %inner1.1.rho1.rho, ...), custom_call_target="tpu_custom_call" | custom-call | tf_op jit(solution)/shard_map/inner2/pallas_call | solution.py:422
  35.7 2.9 %edge2.1.counts = f32[32,2048]{1,0:T(8,128)S(1)} custom-call(s32[1]{0:T(128)} %bitcast.1.odd, f32[32,2048]{1,0:T(8,128)S(1)} %get-tuple-element.88.head, f32[32,2048]{1,0:T(8,128)S(1)} %get-tuple-element.89.tail, f32[32,2048]{1,0:T(8,128)S(1)} %collective-permute-done.2.from_low, f32[32,2048]{1,0:T(8,128)S(1)} %collective-permute-done.3.from_high, ...), custom_call_target="tpu_custom_call" | custom-call | tf_op jit(solution)/shard_map/edge2/pallas_call | solution.py:431
  39.9 1.7 %finish.1.own.source = f32[32,2048]{1,0:T(8,128)S(1)} custom-call(s32[1]{0:T(128)} %bitcast.1.odd, f32[32,2048]{1,0:T(8,128)S(1)} %get-tuple-element.85.rest, f32[32,2048]{1,0:T(8,128)S(1)} %collective-permute-done.2.from_low, f32[32,2048]{1,0:T(8,128)S(1)} %collective-permute-done.3.from_high, f32[32,2048]{1,0:T(8,128)S(1)} %collective-permute-done.4.part, ...), custom_call_target="tpu_custom_call" | custom-call | tf_op jit(solution)/shard_map/finish/pallas_call | solution.py:440
  43.9 2.5 %reorder.1 = (f32[32,2048]{1,0:T(8,128)S(1)}, f32[1,2048]{1,0:T(1,128)S(1)}) custom-call(s32[1]{0:T(128)} %bitcast.g.g_ref, s32[16,128]{1,0:T(8,128)S(1)} %get-tuple-element.95.index, f32[128,2048]{1,0:T(8,128)S(1)} %copy-done.3, f32[1,2048]{1,0:T(1,128)S(1)} %bitcast.32), custom_call_target="tpu_custom_call" | custom-call | tf_op jit(solution)/shard_map/reorder/pallas_call | solution.py:457
  46.4 16.8 %collective-permute-done.6.chip.source = f32[32,2048]{1,0:T(8,128)S(1)} collective-permute-done((f32[32,2048]{1,0:T(8,128)S(1)}, f32[32,2048]{1,0:T(8,128)S(1)}, u32[]{:S(2)}, u32[]{:S(2)}) %collective-permute-start.6) | collective-permute-done | bytes 262176 | tf_op jit(solution)/shard_map/ppermute | solution.py:454
  67.3 2.2 %restore.4.core = f32[32,2048]{1,0:T(8,128)S(1)} custom-call(s32[16,128]{1,0:T(8,128)S(1)} %bitcast.28, f32[32,2048]{1,0:T(8,128)S(1)} %collective-permute-done.5.core.source), custom_call_target="tpu_custom_call" | custom-call | tf_op jit(solution)/shard_map/restore/pallas_call | solution.py:450
  69.5 2.2 %collective-permute-done.9 = f32[160,128]{1,0:T(8,128)S(1)} collective-permute-done((f32[160,128]{1,0:T(8,128)S(1)}, f32[160,128]{1,0:T(8,128)S(1)}, u32[]{:S(2)}, u32[]{:S(2)}) %collective-permute-start.9) | collective-permute-done | bytes 81952 | tf_op jit(solution)/shard_map/ppermute | solution.py:500
  71.8 2.2 %restore.5.chip = f32[32,2048]{1,0:T(8,128)S(1)} custom-call(s32[16,128]{1,0:T(8,128)S(1)} %bitcast.29, f32[32,2048]{1,0:T(8,128)S(1)} %collective-permute-done.6.chip.source), custom_call_target="tpu_custom_call" | custom-call | tf_op jit(solution)/shard_map/restore/pallas_call | solution.py:450
  74.0 3.7 %collective-permute-done.10 = f32[160,128]{1,0:T(8,128)S(1)} collective-permute-done((f32[160,128]{1,0:T(8,128)S(1)}, f32[160,128]{1,0:T(8,128)S(1)}, u32[]{:S(2)}, u32[]{:S(2)}) %collective-permute-start.10) | collective-permute-done | bytes 81952 | tf_op jit(solution)/shard_map/ppermute | solution.py:500
  77.8 2.2 %restore.6.both = f32[32,2048]{1,0:T(8,128)S(1)} custom-call(s32[16,128]{1,0:T(8,128)S(1)} %bitcast.30, f32[32,2048]{1,0:T(8,128)S(1)} %collective-permute-done.7.both.source), custom_call_target="tpu_custom_call" | custom-call | tf_op jit(solution)/shard_map/restore/pallas_call | solution.py:450
  80.1 2.2 %collective-permute-done.11 = f32[160,128]{1,0:T(8,128)S(1)} collective-permute-done((f32[160,128]{1,0:T(8,128)S(1)}, f32[160,128]{1,0:T(8,128)S(1)}, u32[]{:S(2)}, u32[]{:S(2)}) %collective-permute-start.11) | collective-permute-done | bytes 81952 | tf_op jit(solution)/shard_map/ppermute | solution.py:500
  82.8 2.2 %restore.7.own = f32[32,2048]{1,0:T(8,128)S(1)} custom-call(s32[16,128]{1,0:T(8,128)S(1)} %bitcast.31, f32[32,2048]{1,0:T(8,128)S(1)} %finish.1.own.source), custom_call_target="tpu_custom_call" | custom-call | tf_op jit(solution)/shard_map/restore/pallas_call | solution.py:450
  85.1 3.4 %collective-permute-done.12 = f32[160,128]{1,0:T(8,128)S(1)} collective-permute-done((f32[160,128]{1,0:T(8,128)S(1)}, f32[160,128]{1,0:T(8,128)S(1)}, u32[]{:S(2)}, u32[]{:S(2)}) %collective-permute-start.12) | collective-permute-done | bytes 81952 | tf_op jit(solution)/shard_map/ppermute | solution.py:500
  89.7 6.6 %collective-permute-done.13 = f32[160,128]{1,0:T(8,128)S(1)} collective-permute-done((f32[160,128]{1,0:T(8,128)S(1)}, f32[160,128]{1,0:T(8,128)S(1)}, u32[]{:S(2)}, u32[]{:S(2)}) %collective-permute-start.13) | collective-permute-done | bytes 81952 | tf_op jit(solution)/shard_map/ppermute | solution.py:500
  97.1 6.1 %solve.1.mixing = f32[32,128]{1,0:T(8,128)S(1)} custom-call(f32[160,128]{1,0:T(8,128)S(1)} %add.25.packed), custom_call_target="tpu_custom_call" | custom-call | tf_op jit(solution)/shard_map/solve/pallas_call | solution.py:529
  103.2 2.6 %update.1 = f32[256,2048]{1,0:T(8,128)} custom-call(s32[1]{0:T(128)} %bitcast.g.g_ref, f32[32,128]{1,0:T(8,128)S(1)} %solve.1.mixing, f32[3,32,2048]{2,1,0:T(8,128)S(1)} %get-tuple-element.124.theta_a.refs_0_, f32[3,32,2048]{2,1,0:T(8,128)S(1)} %collective-permute-done.15.refs_1_, f32[3,32,2048]{2,1,0:T(8,128)S(1)} %collective-permute-done.8.refs_2_, ...), custom_call_target="tpu_custom_call" | custom-call | tf_op jit(solution)/shard_map/update/pallas_call | solution.py:535
  (51 shorter events, 16.2 us)
Async XLA Ops:
  0.6 1.6 %copy-start = (f32[32,8,2048]{2,1,0:T(8,128)S(1)}, f32[32,8,2048]{2,1,0:T(8,128)}, u32[]{:S(2)}) copy-start(f32[32,8,2048]{2,1,0:T(8,128)} %param.6) | copy-start | bytes 6291460
  2.2 1.6 %copy-start.2 = (f32[32,8,2048]{2,1,0:T(8,128)S(1)}, f32[32,8,2048]{2,1,0:T(8,128)}, u32[]{:S(2)}) copy-start(f32[32,8,2048]{2,1,0:T(8,128)} %param.5) | copy-start | bytes 6291460
  5.3 15.3 %collective-permute-start = (f32[32,2048]{1,0:T(8,128)S(1)}, f32[32,2048]{1,0:T(8,128)S(1)}, u32[]{:S(2)}, u32[]{:S(2)}) collective-permute-start(f32[32,2048]{1,0:T(8,128)S(1)} %get-tuple-element.67), channel_id=1, source_target_pairs={{0,1},{1,0},{2,3},{3,2},{4,5},{5,4},{6,7},{7,6},{8,9},{9,8},{10,11... | collective-permute-start | bytes 786440 | tf_op jit(solution)/shard_map/ppermute | solution.py:375
  6.2 14.4 %collective-permute-start.1 = (f32[32,2048]{1,0:T(8,128)S(1)}, f32[32,2048]{1,0:T(8,128)S(1)}, u32[]{:S(2)}, u32[]{:S(2)}) collective-permute-start(f32[32,2048]{1,0:T(8,128)S(1)} %get-tuple-element.68), channel_id=1, source_target_pairs={{1,2},{2,1},{3,4},{4,3},{5,6},{6,5},{7,8},{8,7},{9,10},{10,9},{11,... | collective-permute-start | bytes 786440 | tf_op jit(solution)/shard_map/ppermute | solution.py:376
  12.6 1.6 %copy-start.1 = (f32[32,8,2048]{2,1,0:T(8,128)S(1)}, f32[32,8,2048]{2,1,0:T(8,128)}, u32[]{:S(2)}) copy-start(f32[32,8,2048]{2,1,0:T(8,128)} %param.6) | copy-start | bytes 6291460
  14.2 2.2 %slice-start = ((s32[2048,8]{0,1:T(8,128)}), s32[2048,1]{0,1:T(1,128)S(1)}, s32[]{:S(2)}) async-start(s32[2048,8]{0,1:T(8,128)} %param.7), calls=%async_computation | async-start | bytes 16384 | tf_op jit(solution)/shard_map/slice | solution.py:391
  21.1 14.6 %collective-permute-start.2 = (f32[32,2048]{1,0:T(8,128)S(1)}, f32[32,2048]{1,0:T(8,128)S(1)}, u32[]{:S(2)}, u32[]{:S(2)}) collective-permute-start(f32[32,2048]{1,0:T(8,128)S(1)} %get-tuple-element.74), channel_id=1, source_target_pairs={{0,1},{1,0},{2,3},{3,2},{4,5},{5,4},{6,7},{7,6},{8,9},{9,8},{10,11... | collective-permute-start | bytes 786440 | tf_op jit(solution)/shard_map/ppermute | solution.py:375
  21.2 14.5 %collective-permute-start.3 = (f32[32,2048]{1,0:T(8,128)S(1)}, f32[32,2048]{1,0:T(8,128)S(1)}, u32[]{:S(2)}, u32[]{:S(2)}) collective-permute-start(f32[32,2048]{1,0:T(8,128)S(1)} %get-tuple-element.75), channel_id=1, source_target_pairs={{1,2},{2,1},{3,4},{4,3},{5,6},{6,5},{7,8},{8,7},{9,10},{10,9},{11,... | collective-permute-start | bytes 786440 | tf_op jit(solution)/shard_map/ppermute | solution.py:376
  26.4 13.5 %collective-permute-start.4 = (f32[32,2048]{1,0:T(8,128)S(1)}, f32[32,2048]{1,0:T(8,128)S(1)}, u32[]{:S(2)}, u32[]{:S(2)}) collective-permute-start(f32[32,2048]{1,0:T(8,128)S(1)} %get-tuple-element.91), channel_id=1, source_target_pairs={{1,0},{2,1},{3,2},{4,3},{5,4},{6,5},{7,6},{8,7},{9,8},{10,9},{11,1... | collective-permute-start | bytes 786440 | tf_op jit(solution)/shard_map/ppermute | solution.py:420
  28.4 34.8 %collective-permute-start.8 = (f32[3,32,2048]{2,1,0:T(8,128)S(1)}, f32[3,32,2048]{2,1,0:T(8,128)S(1)}, u32[]{:S(2)}, u32[]{:S(2)}) collective-permute-start(f32[3,32,2048]{2,1,0:T(8,128)S(1)} %get-tuple-element.124.theta_a.refs_0_), channel_id=1, source_target_pairs={{0,64},{32,96},{64,0},{96,32},{1,65},{33,97},{65,1},{97,33},{2,66}... | collective-permute-start | bytes 2359304 | tf_op jit(solution)/shard_map/ppermute | solution.py:389
  35.6 7.1 %copy-start.4 = (f32[2048]{0:T(1024)S(1)}, f32[2048]{0:T(1024)}, u32[]{:S(2)}) copy-start(f32[2048]{0:T(1024)} %param.9) | copy-start | bytes 24580
  41.6 21.6 %collective-permute-start.6 = (f32[32,2048]{1,0:T(8,128)S(1)}, f32[32,2048]{1,0:T(8,128)S(1)}, u32[]{:S(2)}, u32[]{:S(2)}) collective-permute-start(f32[32,2048]{1,0:T(8,128)S(1)} %finish.1.own.source), channel_id=1, source_target_pairs={{0,64},{32,96},{64,0},{96,32},{1,65},{33,97},{65,1},{97,33},{2,66}... | collective-permute-start | bytes 786440 | tf_op jit(solution)/shard_map/ppermute | solution.py:454
  42.7 20.5 %collective-permute-start.5 = (f32[32,2048]{1,0:T(8,128)S(1)}, f32[32,2048]{1,0:T(8,128)S(1)}, u32[]{:S(2)}, u32[]{:S(2)}) collective-permute-start(f32[32,2048]{1,0:T(8,128)S(1)} %finish.1.own.source), channel_id=1, source_target_pairs={{0,32},{32,0},{64,96},{96,64},{1,33},{33,1},{65,97},{97,65},{2,34}... | collective-permute-start | bytes 786440 | tf_op jit(solution)/shard_map/ppermute | solution.py:455
  63.2 1.5 %collective-permute-start.7 = (f32[32,2048]{1,0:T(8,128)S(1)}, f32[32,2048]{1,0:T(8,128)S(1)}, u32[]{:S(2)}, u32[]{:S(2)}) collective-permute-start(f32[32,2048]{1,0:T(8,128)S(1)} %collective-permute-done.6.chip.source), channel_id=1, source_target_pairs={{0,32},{32,0},{64,96},{96,64},{1,33},{33,1},{65,97},{97,65},{2,34}... | collective-permute-start | bytes 786440 | tf_op jit(solution)/shard_map/ppermute | solution.py:477
  64.7 31.6 %collective-permute-start.14 = (f32[5,32,2048]{2,1,0:T(8,128)S(1)}, f32[5,32,2048]{2,1,0:T(8,128)S(1)}, u32[]{:S(2)}, u32[]{:S(2)}) collective-permute-start(f32[5,32,2048]{2,1,0:T(8,128)S(1)} %get-tuple-element.122.theta_b.refs_4_), channel_id=1, source_target_pairs={{0,64},{32,96},{64,0},{96,32},{1,65},{33,97},{65,1},{97,33},{2,66}... | collective-permute-start | bytes 3932168 | tf_op jit(solution)/shard_map/ppermute | solution.py:479
  67.2 4.5 %collective-permute-start.9 = (f32[160,128]{1,0:T(8,128)S(1)}, f32[160,128]{1,0:T(8,128)S(1)}, u32[]{:S(2)}, u32[]{:S(2)}) collective-permute-start(f32[160,128]{1,0:T(8,128)S(1)} %product.1), channel_id=1, source_target_pairs={{0,1},{1,0},{2,3},{3,2},{4,5},{5,4},{6,7},{7,6},{8,9},{9,8},{10,11... | collective-permute-start | bytes 245768 | tf_op jit(solution)/shard_map/ppermute | solution.py:500
  71.7 6.0 %collective-permute-start.10 = (f32[160,128]{1,0:T(8,128)S(1)}, f32[160,128]{1,0:T(8,128)S(1)}, u32[]{:S(2)}, u32[]{:S(2)}) collective-permute-start(f32[160,128]{1,0:T(8,128)S(1)} %add.21), channel_id=1, source_target_pairs={{0,2},{1,3},{2,0},{3,1},{4,6},{5,7},{6,4},{7,5},{8,10},{9,11},{10,... | collective-permute-start | bytes 245768 | tf_op jit(solution)/shard_map/ppermute | solution.py:500
  77.8 4.5 %collective-permute-start.11 = (f32[160,128]{1,0:T(8,128)S(1)}, f32[160,128]{1,0:T(8,128)S(1)}, u32[]{:S(2)}, u32[]{:S(2)}) collective-permute-start(f32[160,128]{1,0:T(8,128)S(1)} %add.22), channel_id=1, source_target_pairs={{0,8},{1,9},{2,10},{3,11},{4,12},{5,13},{6,14},{7,15},{8,0},{9,1},... | collective-permute-start | bytes 245768 | tf_op jit(solution)/shard_map/ppermute | solution.py:500
  82.3 6.2 %collective-permute-start.12 = (f32[160,128]{1,0:T(8,128)S(1)}, f32[160,128]{1,0:T(8,128)S(1)}, u32[]{:S(2)}, u32[]{:S(2)}) collective-permute-start(f32[160,128]{1,0:T(8,128)S(1)} %add.23), channel_id=1, source_target_pairs={{0,16},{1,17},{2,18},{3,19},{4,20},{5,21},{6,22},{7,23},{8,24},{9,... | collective-permute-start | bytes 245768 | tf_op jit(solution)/shard_map/ppermute | solution.py:500
  88.5 7.8 %collective-permute-start.13 = (f32[160,128]{1,0:T(8,128)S(1)}, f32[160,128]{1,0:T(8,128)S(1)}, u32[]{:S(2)}, u32[]{:S(2)}) collective-permute-start(f32[160,128]{1,0:T(8,128)S(1)} %add.24), channel_id=1, source_target_pairs={{0,4},{1,5},{2,6},{3,7},{4,0},{5,1},{6,2},{7,3},{8,12},{9,13},{10,... | collective-permute-start | bytes 245768 | tf_op jit(solution)/shard_map/ppermute | solution.py:500
  88.7 14.5 %collective-permute-start.17 = (f32[5,32,2048]{2,1,0:T(8,128)S(1)}, f32[5,32,2048]{2,1,0:T(8,128)S(1)}, u32[]{:S(2)}, u32[]{:S(2)}) collective-permute-start(f32[5,32,2048]{2,1,0:T(8,128)S(1)} %get-tuple-element.122.theta_b.refs_4_), channel_id=1, source_target_pairs={{0,32},{32,0},{64,96},{96,64},{1,33},{33,1},{65,97},{97,65},{2,34}... | collective-permute-start | bytes 3932168 | tf_op jit(solution)/shard_map/ppermute | solution.py:498
  96.4 6.8 %collective-permute-start.18 = (f32[5,32,2048]{2,1,0:T(8,128)S(1)}, f32[5,32,2048]{2,1,0:T(8,128)S(1)}, u32[]{:S(2)}, u32[]{:S(2)}) collective-permute-start(f32[5,32,2048]{2,1,0:T(8,128)S(1)} %collective-permute-done.14.refs_6_), channel_id=1, source_target_pairs={{0,32},{32,0},{64,96},{96,64},{1,33},{33,1},{65,97},{97,65},{2,34}... | collective-permute-start | bytes 3932168 | tf_op jit(solution)/shard_map/ppermute | solution.py:528
  96.5 6.7 %collective-permute-start.15 = (f32[3,32,2048]{2,1,0:T(8,128)S(1)}, f32[3,32,2048]{2,1,0:T(8,128)S(1)}, u32[]{:S(2)}, u32[]{:S(2)}) collective-permute-start(f32[3,32,2048]{2,1,0:T(8,128)S(1)} %get-tuple-element.124.theta_a.refs_0_), channel_id=1, source_target_pairs={{0,32},{32,0},{64,96},{96,64},{1,33},{33,1},{65,97},{97,65},{2,34}... | collective-permute-start | bytes 2359304 | tf_op jit(solution)/shard_map/ppermute | solution.py:497
  97.0 6.2 %collective-permute-start.16 = (f32[3,32,2048]{2,1,0:T(8,128)S(1)}, f32[3,32,2048]{2,1,0:T(8,128)S(1)}, u32[]{:S(2)}, u32[]{:S(2)}) collective-permute-start(f32[3,32,2048]{2,1,0:T(8,128)S(1)} %collective-permute-done.8.refs_2_), channel_id=1, source_target_pairs={{0,32},{32,0},{64,96},{96,64},{1,33},{33,1},{65,97},{97,65},{2,34}... | collective-permute-start | bytes 2359304 | tf_op jit(solution)/shard_map/ppermute | solution.py:480
  (1 other events, 1.2 us)

commit v4 on v3

--- a/solution.py
+++ b/solution.py
@@ -241,6 +241,30 @@
     pick(table, first, first + blocks - 1, low, high, pos, counts, mine)
 
 
+def pack(x, m, packed):
+    n = 4 * m
+    lane = lax.broadcasted_iota(jnp.int32, (m, n), 1)
+    packed[0:m, :] = x[0:m]
+    packed[m : 2 * m, :] = jnp.where(lane < m, pltpu.roll(x[3 * m : n], m, 1), x[m : 2 * m])
+    half = m // 2
+    low, high = x[2 * m : 2 * m + half], x[2 * m + half : 3 * m]
+    packed[2 * m : 2 * m + half, :] = jnp.where(lane[:half] < 2 * m, pltpu.roll(high, 2 * m, 1), low)
+    packed[2 * m + half :, :] = x[n:]
+
+
+def unpack(packed, m):
+    n = 4 * m
+    half = m // 2
+    second, third = packed[m : 2 * m, :], packed[2 * m : 2 * m + half, :]
+    upper = jnp.concatenate(
+        [packed[0:m, :], second, third, pltpu.roll(third, 2 * m, 1), pltpu.roll(second, 3 * m, 1)], axis=0
+    )
+    lane = lax.broadcasted_iota(jnp.int32, (n, n), 1)
+    sub = lax.broadcasted_iota(jnp.int32, (n, n), 0)
+    full = jnp.where(lane >= (sub & -m), upper, upper.T)
+    return jnp.concatenate([full, packed[2 * m + half :, :]], axis=0)
+
+
 def product_kernel(total, g_ref, own, core, chip, both, perturbed, noise, packed, every):
     members, sensors = own.shape
     g = g_ref[0]
@@ -258,7 +282,7 @@
             left, weighted, (((1,), (1,)), ((), ())), precision=lax.Precision.HIGHEST, preferred_element_type=F32
         )
         acc = term if acc is None else acc + term
-    packed[...] = acc
+    pack(acc, members, packed)
 
 
 def lane_of(x, k):
@@ -274,8 +298,9 @@
     lane = lax.broadcasted_iota(jnp.int32, (8, n), 1)
     sub = lax.broadcasted_iota(jnp.int32, (8, n), 0)
     a = []
-    for i in range(packed.shape[0] // 8):
-        x = packed[i * 8 : i * 8 + 8, :]
+    wide = unpack(packed, n // 4)
+    for i in range(wide.shape[0] // 8):
+        x = wide[i * 8 : i * 8 + 8, :]
         a.append(jnp.where(lane == sub + i * 8, x + shift, x) if i * 8 < n else x)
     keep = jnp.zeros((8, n), F32)
     mix = jnp.zeros((8, n), F32)
@@ -356,8 +381,8 @@
     slab = rows * columns
     blocks = columns // LANES
     groups = sensors // LANES
-    flat_theta = theta.reshape(members * rows, columns)
-    flat_rho = density.reshape(members * rows, columns)
+    flat_theta = pltpu.with_memory_space_constraint(theta.reshape(members * rows, columns), pltpu.HBM)
+    flat_rho = pltpu.with_memory_space_constraint(density.reshape(members * rows, columns), pltpu.HBM)
     g = lax.axis_index("grp").astype(jnp.int32).reshape(1)
     row = jax.ShapeDtypeStruct((members, columns), F32)
     turned = jax.ShapeDtypeStruct((rows, members, columns), F32)
@@ -453,7 +478,9 @@
 
     chip = lax.ppermute(own, "grp", swapped("grp", 2))
     core = lax.ppermute(own, "grp", swapped("grp", 1))
-    own, perturbed = tie(own, perturbed)
+    own, perturbed, theta_a, theta_b = tie(own, perturbed, theta_a, theta_b)
+    core_a = lax.ppermute(theta_a, "grp", swapped("grp", 1))
+    core_b = lax.ppermute(theta_b, "grp", swapped("grp", 1))
     perturbed_own, noise = pl.pallas_call(
         lambda g, index, source, extra, out, extra_out: reorder_kernel(index, source, out, extra, extra_out),
         grid_spec=pltpu.PrefetchScalarGridSpec(
@@ -475,27 +502,23 @@
     )(g, order, perturbed, noise_var.reshape(1, sensors))
     chip, perturbed_own = tie(chip, perturbed_own)
     both = lax.ppermute(chip, "grp", swapped("grp", 1))
-    core, both, chip_a, theta_b = tie(core, both, chip_a, theta_b)
+    core, chip_a, theta_b, chip = tie(core, chip_a, theta_b, chip)
     chip_b = lax.ppermute(theta_b, "grp", swapped("grp", 2))
     both_a = lax.ppermute(chip_a, "grp", swapped("grp", 1))
     packed = pl.pallas_call(
         functools.partial(product_kernel, total),
         in_specs=[smem] + [vmem] * 6,
-        out_shape=jax.ShapeDtypeStruct((total + members, total), F32),
+        out_shape=jax.ShapeDtypeStruct((members * 7 // 2, total), F32),
         scratch_shapes=[pltpu.VMEM((total, sensors), F32)],
         name="product",
         compiler_params=kernel_params(12),
     )(g, own, core, chip, both, perturbed_own, noise)
 
-    theta_a, packed = tie(theta_a, packed)
-
     def assemble(g_ref, own, core, chip, both, out):
         g = g_ref[0]
         for step, piece in enumerate((own, core, chip, both)):
             out[pl.ds(pl.multiple_of((g ^ step) * members, members), members), :] = piece[...]
 
-    core_a = lax.ppermute(theta_a, "grp", swapped("grp", 1))
-    core_b = lax.ppermute(theta_b, "grp", swapped("grp", 1))
     for stage, bit in enumerate((1, 2, 8, 16, 4)):
         other = lax.ppermute(packed, "cell", swapped("cell", bit))
         if stage == 0:

time: 107 us -> 94.9 us (0.89)
  waiting for transfers between devices: 37.7 us -> 26.4 us
  local copies, waits for them, and re-layouts: 6 us -> 1.24 us
  Pallas kernels: 37.6 us -> 40.9 us
    ppermute x1, waiting for transfers between devices: 16.8 us -> 7.25 us  [body(): chip = lax.ppermute(own, 'grp', swapped('grp', 2))]
    unnamed x10 -> x4, local copies, waits for them, and re-layouts: 5.99 us -> 1.23 us
    ppermute x5, waiting for transfers between devices: 18.1 us -> 15.4 us  [body(): other = lax.ppermute(packed, 'cell', swapped('cell', bit))]
    pallas_call x1, Pallas kernels: 1.46 us -> 2.61 us  [body(): pl.pallas_call(functools.partial(prep_kernel, rows), in_specs=[smem, anyw...]
    pallas_call x1, Pallas kernels: 2.64 us -> 3.75 us  [body(): pl.pallas_call(update_kernel, in_specs=[smem] + [vmem] * 9, out_specs=any...]
  transfers between devices with their start and end apart: 19 -> 19, of which waited for: 8 -> 9; matrix products, arithmetic and copies ran while one was open for 4% -> 4% of each run, Pallas kernels for 31% -> 37%
where the time goes in v4:
time: 94.9 us; the launch traced here: 93.4 us
  Pallas kernels  40.9 us (43%)
  waiting for transfers between devices  26.4 us (28%)
  starting transfers between devices  19.7 us (21%)
  other arithmetic  4.15 us (4%)
  local copies, waits for them, and re-layouts  1.24 us (1%)
  between operations  1.07 us (1%)
    ppermute x5, waiting for transfers between devices, body(): other = lax.ppermute(packed, 'cell', swapped('cell', bit))  15.4 us
    ppermute x2, starting transfers between devices, both_ways(): from_high = lax.ppermute(high_pair, 'cell', far)  11.5 us
    pallas_call x4, Pallas kernels, restore(): pl.pallas_call(reorder_kernel, out_shape=counts_shape, name='restore', co...  8.92 us
    ppermute x1, waiting for transfers between devices, body(): chip = lax.ppermute(own, 'grp', swapped('grp', 2))  7.25 us
    pallas_call x1, Pallas kernels, body(): pl.pallas_call(inner2_kernel, in_specs=[vmem] * 6 + [smem] * 2, out_shape...  6.17 us
    pallas_call x1, Pallas kernels, body(): pl.pallas_call(functools.partial(solve_kernel, total - 1.0), out_shape=ja...  6.16 us
    pallas_call x1, Pallas kernels, body(): pl.pallas_call(update_kernel, in_specs=[smem] + [vmem] * 9, out_specs=any...  3.75 us
    pallas_call x1, Pallas kernels, body(): pl.pallas_call(inner1_kernel, in_specs=[vmem, vmem, anywhere], out_shape=...  3.17 us
  transfers between devices with their start and end apart: 19, of which 9 were waited for; matrix products, arithmetic and copies ran while one was open for 4% of the time, Pallas kernels for 37%

profile of v4, /device:TPU:22, one launch (start us, length us, event | category | flops | bytes accessed | tf_op | source)
XLA Modules:
  0.0 93.4 jit_solution(3231230570404046347)
XLA Ops:
  0.6 2.6 %prep.1 = (f32[32,2048]{1,0:T(8,128)S(1)}, f32[32,2048]{1,0:T(8,128)S(1)}, f32[3,32,2048]{2,1,0:T(8,128)S(1)}, f32[5,32,2048]{2,1,0:T(8,128)S(1)}) custom-call(s32[1]{0:T(128)} %bitcast.1.odd, f32[256,2048]{1,0:T(8,128)} %bitcast.32, f32[256,2048]{1,0:T(8,128)} %bitcast.30), custom_call_target="tpu_custom_call" | custom-call | tf_op jit(solution)/shard_map/prep/pallas_call | solution.py:405
  4.2 6.4 %collective-permute-start.1 = (f32[32,2048]{1,0:T(8,128)S(1)}, f32[32,2048]{1,0:T(8,128)S(1)}, u32[]{:S(2)}, u32[]{:S(2)}) collective-permute-start(f32[32,2048]{1,0:T(8,128)S(1)} %get-tuple-element.68), channel_id=1, source_target_pairs={{1,2},{2,1},{3,4},{4,3},{5,6},{6,5},{7,8},{8,7},{9,10},{10,9},{11,... | collective-permute-start | bytes 786440 | tf_op jit(solution)/shard_map/ppermute | solution.py:401
  11.6 3.2 %inner1.1.rho1.rho = f32[8,32,2048]{2,1,0:T(8,128)S(1)} custom-call(f32[3,32,2048]{2,1,0:T(8,128)S(1)} %get-tuple-element.124.theta_a.refs_0_, f32[5,32,2048]{2,1,0:T(8,128)S(1)} %get-tuple-element.122.theta_b.refs_4_, f32[256,2048]{1,0:T(8,128)} %bitcast.31), custom_call_target="tpu_custom_call" | custom-call | tf_op jit(solution)/shard_map/inner1/pallas_call | solution.py:417
  14.8 1.7 %convert_reduce_fusion = s32[2048]{0:T(1024)S(1)} fusion(s32[2048]{0:T(1024)S(1)} %iota_add_fusion), kind=kLoop, calls=%fused_computation.2 | loop fusion | flops 12580864 | bytes 16384 | tf_op jit(solution)/shard_map/reduce_sum | solution.py:427
  16.5 2.2 %select_reduce_fusion = s32[2048]{0:T(1024)S(1)} fusion(s32[2048]{0:T(1024)S(1)} %convert_reduce_fusion, s32[2048]{0:T(1024)S(1)} %iota_add_fusion), kind=kLoop, calls=%fused_computation | loop fusion | flops 12580864 | bytes 24576 | tf_op jit(solution)/shard_map/reduce_sum | solution.py:429
  19.6 5.2 %collective-permute-start.3 = (f32[32,2048]{1,0:T(8,128)S(1)}, f32[32,2048]{1,0:T(8,128)S(1)}, u32[]{:S(2)}, u32[]{:S(2)}) collective-permute-start(f32[32,2048]{1,0:T(8,128)S(1)} %get-tuple-element.75), channel_id=1, source_target_pairs={{1,2},{2,1},{3,4},{4,3},{5,6},{6,5},{7,8},{8,7},{9,10},{10,9},{11,... | collective-permute-start | bytes 786440 | tf_op jit(solution)/shard_map/ppermute | solution.py:401
  24.7 2.0 %collective-permute-start.4 = (f32[32,2048]{1,0:T(8,128)S(1)}, f32[32,2048]{1,0:T(8,128)S(1)}, u32[]{:S(2)}, u32[]{:S(2)}) collective-permute-start(f32[32,2048]{1,0:T(8,128)S(1)} %get-tuple-element.91), channel_id=1, source_target_pairs={{1,0},{2,1},{3,2},{4,3},{5,4},{6,5},{7,6},{8,7},{9,8},{10,9},{11,1... | collective-permute-start | bytes 786440 | tf_op jit(solution)/shard_map/ppermute | solution.py:445
  26.8 6.2 %inner2.1 = (f32[32,2048]{1,0:T(8,128)S(1)}, f32[32,2048]{1,0:T(8,128)S(1)}, f32[32,2048]{1,0:T(8,128)S(1)}, f32[32,2048]{1,0:T(8,128)S(1)}) custom-call(f32[3,32,2048]{2,1,0:T(8,128)S(1)} %get-tuple-element.124.theta_a.refs_0_, f32[5,32,2048]{2,1,0:T(8,128)S(1)} %get-tuple-element.122.theta_b.refs_4_, f32[8,32,2048]{2,1,0:T(8,128)S(1)} %inner1.1.rho1.rho, ...), custom_call_target="tpu_custom_call" | custom-call | tf_op jit(solution)/shard_map/inner2/pallas_call | solution.py:447
  33.4 2.9 %edge2.1.counts = f32[32,2048]{1,0:T(8,128)S(1)} custom-call(s32[1]{0:T(128)} %bitcast.1.odd, f32[32,2048]{1,0:T(8,128)S(1)} %get-tuple-element.88.head, f32[32,2048]{1,0:T(8,128)S(1)} %get-tuple-element.89.tail, f32[32,2048]{1,0:T(8,128)S(1)} %collective-permute-done.2.from_low, f32[32,2048]{1,0:T(8,128)S(1)} %collective-permute-done.3.from_high, ...), custom_call_target="tpu_custom_call" | custom-call | tf_op jit(solution)/shard_map/edge2/pallas_call | solution.py:456
  36.3 1.7 %collective-permute-done.4.part = f32[32,2048]{1,0:T(8,128)S(1)} collective-permute-done((f32[32,2048]{1,0:T(8,128)S(1)}, f32[32,2048]{1,0:T(8,128)S(1)}, u32[]{:S(2)}, u32[]{:S(2)}) %collective-permute-start.4) | collective-permute-done | bytes 262176 | tf_op jit(solution)/shard_map/ppermute | solution.py:445
  38.0 1.7 %finish.1.own.source = f32[32,2048]{1,0:T(8,128)S(1)} custom-call(s32[1]{0:T(128)} %bitcast.1.odd, f32[32,2048]{1,0:T(8,128)S(1)} %get-tuple-element.85.rest, f32[32,2048]{1,0:T(8,128)S(1)} %collective-permute-done.2.from_low, f32[32,2048]{1,0:T(8,128)S(1)} %collective-permute-done.3.from_high, f32[32,2048]{1,0:T(8,128)S(1)} %collective-permute-done.4.part, ...), custom_call_target="tpu_custom_call" | custom-call | tf_op jit(solution)/shard_map/finish/pallas_call | solution.py:465
  42.0 2.5 %reorder.1 = (f32[32,2048]{1,0:T(8,128)S(1)}, f32[1,2048]{1,0:T(1,128)S(1)}) custom-call(s32[1]{0:T(128)} %bitcast.g.g_ref, s32[16,128]{1,0:T(8,128)S(1)} %get-tuple-element.95.index, f32[128,2048]{1,0:T(8,128)S(1)} %copy-done, f32[1,2048]{1,0:T(1,128)S(1)} %bitcast.29), custom_call_target="tpu_custom_call" | custom-call | tf_op jit(solution)/shard_map/reorder/pallas_call | solution.py:484
  44.5 7.3 %collective-permute-done.5.chip.source = f32[32,2048]{1,0:T(8,128)S(1)} collective-permute-done((f32[32,2048]{1,0:T(8,128)S(1)}, f32[32,2048]{1,0:T(8,128)S(1)}, u32[]{:S(2)}, u32[]{:S(2)}) %collective-permute-start.5) | collective-permute-done | bytes 262176 | tf_op jit(solution)/shard_map/ppermute | solution.py:479
  55.9 2.2 %restore.4.core = f32[32,2048]{1,0:T(8,128)S(1)} custom-call(s32[16,128]{1,0:T(8,128)S(1)} %bitcast.25, f32[32,2048]{1,0:T(8,128)S(1)} %collective-permute-done.7.core.source), custom_call_target="tpu_custom_call" | custom-call | tf_op jit(solution)/shard_map/restore/pallas_call | solution.py:475
  58.2 1.9 %collective-permute-done.9 = f32[112,128]{1,0:T(8,128)S(1)} collective-permute-done((f32[112,128]{1,0:T(8,128)S(1)}, f32[112,128]{1,0:T(8,128)S(1)}, u32[]{:S(2)}, u32[]{:S(2)}) %collective-permute-start.9) | collective-permute-done | bytes 57376 | tf_op jit(solution)/shard_map/ppermute | solution.py:523
  60.2 2.2 %restore.5.chip = f32[32,2048]{1,0:T(8,128)S(1)} custom-call(s32[16,128]{1,0:T(8,128)S(1)} %bitcast.26, f32[32,2048]{1,0:T(8,128)S(1)} %collective-permute-done.5.chip.source), custom_call_target="tpu_custom_call" | custom-call | tf_op jit(solution)/shard_map/restore/pallas_call | solution.py:475
  62.4 3.4 %collective-permute-done.10 = f32[112,128]{1,0:T(8,128)S(1)} collective-permute-done((f32[112,128]{1,0:T(8,128)S(1)}, f32[112,128]{1,0:T(8,128)S(1)}, u32[]{:S(2)}, u32[]{:S(2)}) %collective-permute-start.10) | collective-permute-done | bytes 57376 | tf_op jit(solution)/shard_map/ppermute | solution.py:523
  66.0 2.2 %restore.6.both = f32[32,2048]{1,0:T(8,128)S(1)} custom-call(s32[16,128]{1,0:T(8,128)S(1)} %bitcast.27, f32[32,2048]{1,0:T(8,128)S(1)} %collective-permute-done.6.both.source), custom_call_target="tpu_custom_call" | custom-call | tf_op jit(solution)/shard_map/restore/pallas_call | solution.py:475
  68.2 1.9 %collective-permute-done.11 = f32[112,128]{1,0:T(8,128)S(1)} collective-permute-done((f32[112,128]{1,0:T(8,128)S(1)}, f32[112,128]{1,0:T(8,128)S(1)}, u32[]{:S(2)}, u32[]{:S(2)}) %collective-permute-start.11) | collective-permute-done | bytes 57376 | tf_op jit(solution)/shard_map/ppermute | solution.py:523
  70.5 2.2 %restore.7.own = f32[32,2048]{1,0:T(8,128)S(1)} custom-call(s32[16,128]{1,0:T(8,128)S(1)} %bitcast.28, f32[32,2048]{1,0:T(8,128)S(1)} %finish.1.own.source), custom_call_target="tpu_custom_call" | custom-call | tf_op jit(solution)/shard_map/restore/pallas_call | solution.py:475
  72.8 3.1 %collective-permute-done.12 = f32[112,128]{1,0:T(8,128)S(1)} collective-permute-done((f32[112,128]{1,0:T(8,128)S(1)}, f32[112,128]{1,0:T(8,128)S(1)}, u32[]{:S(2)}, u32[]{:S(2)}) %collective-permute-start.12) | collective-permute-done | bytes 57376 | tf_op jit(solution)/shard_map/ppermute | solution.py:523
  77.4 5.1 %collective-permute-done.13 = f32[112,128]{1,0:T(8,128)S(1)} collective-permute-done((f32[112,128]{1,0:T(8,128)S(1)}, f32[112,128]{1,0:T(8,128)S(1)}, u32[]{:S(2)}, u32[]{:S(2)}) %collective-permute-start.13) | collective-permute-done | bytes 57376 | tf_op jit(solution)/shard_map/ppermute | solution.py:523
  83.3 6.2 %solve.1.mixing = f32[32,128]{1,0:T(8,128)S(1)} custom-call(f32[112,128]{1,0:T(8,128)S(1)} %add.25.packed), custom_call_target="tpu_custom_call" | custom-call | tf_op jit(solution)/shard_map/solve/pallas_call | solution.py:552
  89.5 3.8 %update.1 = f32[256,2048]{1,0:T(8,128)} custom-call(s32[1]{0:T(128)} %bitcast.g.g_ref, f32[32,128]{1,0:T(8,128)S(1)} %solve.1.mixing, f32[3,32,2048]{2,1,0:T(8,128)S(1)} %get-tuple-element.124.theta_a.refs_0_, f32[3,32,2048]{2,1,0:T(8,128)S(1)} %collective-permute-done.15.refs_1_, f32[3,32,2048]{2,1,0:T(8,128)} %collective-permute-done.8.refs_2_, ...), custom_call_target="tpu_custom_call" | custom-call | tf_op jit(solution)/shard_map/update/pallas_call | solution.py:558
  (45 shorter events, 12.6 us)
Async XLA Ops:
  3.3 15.7 %collective-permute-start = (f32[32,2048]{1,0:T(8,128)S(1)}, f32[32,2048]{1,0:T(8,128)S(1)}, u32[]{:S(2)}, u32[]{:S(2)}) collective-permute-start(f32[32,2048]{1,0:T(8,128)S(1)} %get-tuple-element.67), channel_id=1, source_target_pairs={{0,1},{1,0},{2,3},{3,2},{4,5},{5,4},{6,7},{7,6},{8,9},{9,8},{10,11... | collective-permute-start | bytes 786440 | tf_op jit(solution)/shard_map/ppermute | solution.py:400
  4.2 14.8 %collective-permute-start.1 = (f32[32,2048]{1,0:T(8,128)S(1)}, f32[32,2048]{1,0:T(8,128)S(1)}, u32[]{:S(2)}, u32[]{:S(2)}) collective-permute-start(f32[32,2048]{1,0:T(8,128)S(1)} %get-tuple-element.68), channel_id=1, source_target_pairs={{1,2},{2,1},{3,4},{4,3},{5,6},{6,5},{7,8},{8,7},{9,10},{10,9},{11,... | collective-permute-start | bytes 786440 | tf_op jit(solution)/shard_map/ppermute | solution.py:401
  10.5 41.3 %collective-permute-start.8 = (f32[3,32,2048]{2,1,0:T(8,128)S(1)}, f32[3,32,2048]{2,1,0:T(8,128)}, u32[]{:S(2)}, u32[]{:S(2)}) collective-permute-start(f32[3,32,2048]{2,1,0:T(8,128)S(1)} %get-tuple-element.124.theta_a.refs_0_), channel_id=1, source_target_pairs={{0,64},{32,96},{64,0},{96,32},{1,65},{33,97},{65,1},{97,33},{2,66}... | collective-permute-start | bytes 2359304 | tf_op jit(solution)/shard_map/ppermute | solution.py:414
  11.6 3.2 %slice-start = ((s32[2048,8]{0,1:T(8,128)}), s32[2048,1]{0,1:T(1,128)S(1)}, s32[]{:S(2)}) async-start(s32[2048,8]{0,1:T(8,128)} %param.7), calls=%async_computation | async-start | bytes 16384 | tf_op jit(solution)/shard_map/slice | solution.py:416
  19.5 13.5 %collective-permute-start.2 = (f32[32,2048]{1,0:T(8,128)S(1)}, f32[32,2048]{1,0:T(8,128)S(1)}, u32[]{:S(2)}, u32[]{:S(2)}) collective-permute-start(f32[32,2048]{1,0:T(8,128)S(1)} %get-tuple-element.74), channel_id=1, source_target_pairs={{0,1},{1,0},{2,3},{3,2},{4,5},{5,4},{6,7},{7,6},{8,9},{9,8},{10,11... | collective-permute-start | bytes 786440 | tf_op jit(solution)/shard_map/ppermute | solution.py:400
  19.6 13.9 %collective-permute-start.3 = (f32[32,2048]{1,0:T(8,128)S(1)}, f32[32,2048]{1,0:T(8,128)S(1)}, u32[]{:S(2)}, u32[]{:S(2)}) collective-permute-start(f32[32,2048]{1,0:T(8,128)S(1)} %get-tuple-element.75), channel_id=1, source_target_pairs={{1,2},{2,1},{3,4},{4,3},{5,6},{6,5},{7,8},{8,7},{9,10},{10,9},{11,... | collective-permute-start | bytes 786440 | tf_op jit(solution)/shard_map/ppermute | solution.py:401
  24.7 13.2 %collective-permute-start.4 = (f32[32,2048]{1,0:T(8,128)S(1)}, f32[32,2048]{1,0:T(8,128)S(1)}, u32[]{:S(2)}, u32[]{:S(2)}) collective-permute-start(f32[32,2048]{1,0:T(8,128)S(1)} %get-tuple-element.91), channel_id=1, source_target_pairs={{1,0},{2,1},{3,2},{4,3},{5,4},{6,5},{7,6},{8,7},{9,8},{10,9},{11,1... | collective-permute-start | bytes 786440 | tf_op jit(solution)/shard_map/ppermute | solution.py:445
  32.9 7.9 %copy-start.1 = (f32[2048]{0:T(1024)S(1)}, f32[2048]{0:T(1024)}, u32[]{:S(2)}) copy-start(f32[2048]{0:T(1024)} %param.9) | copy-start | bytes 24580
  39.7 12.1 %collective-permute-start.5 = (f32[32,2048]{1,0:T(8,128)S(1)}, f32[32,2048]{1,0:T(8,128)S(1)}, u32[]{:S(2)}, u32[]{:S(2)}) collective-permute-start(f32[32,2048]{1,0:T(8,128)S(1)} %finish.1.own.source), channel_id=1, source_target_pairs={{0,64},{32,96},{64,0},{96,32},{1,65},{33,97},{65,1},{97,33},{2,66}... | collective-permute-start | bytes 786440 | tf_op jit(solution)/shard_map/ppermute | solution.py:479
  40.8 11.0 %collective-permute-start.7 = (f32[32,2048]{1,0:T(8,128)S(1)}, f32[32,2048]{1,0:T(8,128)S(1)}, u32[]{:S(2)}, u32[]{:S(2)}) collective-permute-start(f32[32,2048]{1,0:T(8,128)S(1)} %finish.1.own.source), channel_id=1, source_target_pairs={{0,32},{32,0},{64,96},{96,64},{1,33},{33,1},{65,97},{97,65},{2,34}... | collective-permute-start | bytes 786440 | tf_op jit(solution)/shard_map/ppermute | solution.py:480
  40.8 1.2 %copy-start = (f32[128,2048]{1,0:T(8,128)S(1)}, f32[128,2048]{1,0:T(8,128)}, u32[]{:S(2)}) copy-start(f32[128,2048]{1,0:T(8,128)} %source) | copy-start | bytes 3145732
  51.8 30.6 %collective-permute-start.14 = (f32[5,32,2048]{2,1,0:T(8,128)S(1)}, f32[5,32,2048]{2,1,0:T(8,128)S(1)}, u32[]{:S(2)}, u32[]{:S(2)}) collective-permute-start(f32[5,32,2048]{2,1,0:T(8,128)S(1)} %get-tuple-element.122.theta_b.refs_4_), channel_id=1, source_target_pairs={{0,64},{32,96},{64,0},{96,32},{1,65},{33,97},{65,1},{97,33},{2,66}... | collective-permute-start | bytes 3932168 | tf_op jit(solution)/shard_map/ppermute | solution.py:506
  52.8 1.5 %collective-permute-start.6 = (f32[32,2048]{1,0:T(8,128)S(1)}, f32[32,2048]{1,0:T(8,128)S(1)}, u32[]{:S(2)}, u32[]{:S(2)}) collective-permute-start(f32[32,2048]{1,0:T(8,128)S(1)} %collective-permute-done.5.chip.source), channel_id=1, source_target_pairs={{0,32},{32,0},{64,96},{96,64},{1,33},{33,1},{65,97},{97,65},{2,34}... | collective-permute-start | bytes 786440 | tf_op jit(solution)/shard_map/ppermute | solution.py:504
  55.9 4.2 %collective-permute-start.9 = (f32[112,128]{1,0:T(8,128)S(1)}, f32[112,128]{1,0:T(8,128)S(1)}, u32[]{:S(2)}, u32[]{:S(2)}) collective-permute-start(f32[112,128]{1,0:T(8,128)S(1)} %product.1), channel_id=1, source_target_pairs={{0,1},{1,0},{2,3},{3,2},{4,5},{5,4},{6,7},{7,6},{8,9},{9,8},{10,11... | collective-permute-start | bytes 172040 | tf_op jit(solution)/shard_map/ppermute | solution.py:523
  60.1 5.8 %collective-permute-start.10 = (f32[112,128]{1,0:T(8,128)S(1)}, f32[112,128]{1,0:T(8,128)S(1)}, u32[]{:S(2)}, u32[]{:S(2)}) collective-permute-start(f32[112,128]{1,0:T(8,128)S(1)} %add.21), channel_id=1, source_target_pairs={{0,2},{1,3},{2,0},{3,1},{4,6},{5,7},{6,4},{7,5},{8,10},{9,11},{10,... | collective-permute-start | bytes 172040 | tf_op jit(solution)/shard_map/ppermute | solution.py:523
  65.9 4.3 %collective-permute-start.11 = (f32[112,128]{1,0:T(8,128)S(1)}, f32[112,128]{1,0:T(8,128)S(1)}, u32[]{:S(2)}, u32[]{:S(2)}) collective-permute-start(f32[112,128]{1,0:T(8,128)S(1)} %add.22), channel_id=1, source_target_pairs={{0,8},{1,9},{2,10},{3,11},{4,12},{5,13},{6,14},{7,15},{8,0},{9,1},... | collective-permute-start | bytes 172040 | tf_op jit(solution)/shard_map/ppermute | solution.py:523
  70.1 5.8 %collective-permute-start.12 = (f32[112,128]{1,0:T(8,128)S(1)}, f32[112,128]{1,0:T(8,128)S(1)}, u32[]{:S(2)}, u32[]{:S(2)}) collective-permute-start(f32[112,128]{1,0:T(8,128)S(1)} %add.23), channel_id=1, source_target_pairs={{0,16},{1,17},{2,18},{3,19},{4,20},{5,21},{6,22},{7,23},{8,24},{9,... | collective-permute-start | bytes 172040 | tf_op jit(solution)/shard_map/ppermute | solution.py:523
  75.9 6.5 %collective-permute-start.13 = (f32[112,128]{1,0:T(8,128)S(1)}, f32[112,128]{1,0:T(8,128)S(1)}, u32[]{:S(2)}, u32[]{:S(2)}) collective-permute-start(f32[112,128]{1,0:T(8,128)S(1)} %add.24), channel_id=1, source_target_pairs={{0,4},{1,5},{2,6},{3,7},{4,0},{5,1},{6,2},{7,3},{8,12},{9,13},{10,... | collective-permute-start | bytes 172040 | tf_op jit(solution)/shard_map/ppermute | solution.py:523
  76.3 13.2 %collective-permute-start.17 = (f32[5,32,2048]{2,1,0:T(8,128)S(1)}, f32[5,32,2048]{2,1,0:T(8,128)S(1)}, u32[]{:S(2)}, u32[]{:S(2)}) collective-permute-start(f32[5,32,2048]{2,1,0:T(8,128)S(1)} %get-tuple-element.122.theta_b.refs_4_), channel_id=1, source_target_pairs={{0,32},{32,0},{64,96},{96,64},{1,33},{33,1},{65,97},{97,65},{2,34}... | collective-permute-start | bytes 3932168 | tf_op jit(solution)/shard_map/ppermute | solution.py:483
  82.5 7.1 %collective-permute-start.18 = (f32[5,32,2048]{2,1,0:T(8,128)S(1)}, f32[5,32,2048]{2,1,0:T(8,128)S(1)}, u32[]{:S(2)}, u32[]{:S(2)}) collective-permute-start(f32[5,32,2048]{2,1,0:T(8,128)S(1)} %collective-permute-done.14.refs_6_), channel_id=1, source_target_pairs={{0,32},{32,0},{64,96},{96,64},{1,33},{33,1},{65,97},{97,65},{2,34}... | collective-permute-start | bytes 3932168 | tf_op jit(solution)/shard_map/ppermute | solution.py:551
  82.7 6.8 %collective-permute-start.15 = (f32[3,32,2048]{2,1,0:T(8,128)S(1)}, f32[3,32,2048]{2,1,0:T(8,128)S(1)}, u32[]{:S(2)}, u32[]{:S(2)}) collective-permute-start(f32[3,32,2048]{2,1,0:T(8,128)S(1)} %get-tuple-element.124.theta_a.refs_0_), channel_id=1, source_target_pairs={{0,32},{32,0},{64,96},{96,64},{1,33},{33,1},{65,97},{97,65},{2,34}... | collective-permute-start | bytes 2359304 | tf_op jit(solution)/shard_map/ppermute | solution.py:482
  83.2 6.3 %collective-permute-start.16 = (f32[3,32,2048]{2,1,0:T(8,128)}, f32[3,32,2048]{2,1,0:T(8,128)S(1)}, u32[]{:S(2)}, u32[]{:S(2)}) collective-permute-start(f32[3,32,2048]{2,1,0:T(8,128)} %collective-permute-done.8.refs_2_), channel_id=1, source_target_pairs={{0,32},{32,0},{64,96},{96,64},{1,33},{33,1},{65,97},{97,65},{2,34}... | collective-permute-start | bytes 2359304 | tf_op jit(solution)/shard_map/ppermute | solution.py:507

commit v5 on v4

--- a/solution.py
+++ b/solution.py
@@ -364,6 +364,10 @@
             sent.append(copy)
     for copy in sent:
         copy.wait()
+
+
+def hold_kernel(source, out):
+    out[...] = source[...]
 
 
 def tie(*values):
@@ -538,6 +542,15 @@
             mine = restore(own)
             other, mine = tie(other, mine)
         if stage == 4:
+            chip_a, both_a, packed = tie(chip_a, both_a, packed)
+            chip_a = pl.pallas_call(
+                hold_kernel,
+                in_specs=[vmem],
+                out_shape=jax.ShapeDtypeStruct(chip_a.shape, F32),
+                name="hold",
+                compiler_params=kernel_params(4),
+            )(chip_a)
+            other, chip_a = tie(other, chip_a)
             predicted = pl.pallas_call(
                 assemble,
                 in_specs=[smem] + [vmem] * 4,

time: 94.9 us -> 93.2 us (0.982)
  waiting for transfers between devices: 26.4 us -> 25.2 us
    ppermute x5, waiting for transfers between devices: 15.4 us -> 13.5 us  [body(): other = lax.ppermute(packed, 'cell', swapped('cell', bit))]
    pallas_call x0 -> x1, Pallas kernels: none -> 1.18 us  [body(): pl.pallas_call(hold_kernel, in_specs=[vmem], out_shape=jax.ShapeDtypeStru...]
    pallas_call x1, Pallas kernels: 3.75 us -> 2.65 us  [body(): pl.pallas_call(update_kernel, in_specs=[smem] + [vmem] * 9, out_specs=any...]
  transfers between devices with their start and end apart: 19 -> 19, of which waited for: 9 -> 9; matrix products, arithmetic and copies ran while one was open for 4% -> 4% of each run, Pallas kernels for 37% -> 39%
where the time goes in v5:
time: 93.2 us; the launch traced here: 92.6 us
  Pallas kernels  41 us (44%)
  waiting for transfers between devices  25.2 us (27%)
  starting transfers between devices  19.9 us (21%)
  other arithmetic  4.15 us (4%)
  local copies, waits for them, and re-layouts  1.24 us (1%)
  between operations  1.07 us (1%)
    ppermute x5, waiting for transfers between devices, body(): other = lax.ppermute(packed, 'cell', swapped('cell', bit))  13.5 us
    ppermute x2, starting transfers between devices, both_ways(): from_high = lax.ppermute(high_pair, 'cell', far)  11.5 us
    pallas_call x4, Pallas kernels, restore(): pl.pallas_call(reorder_kernel, out_shape=counts_shape, name='restore', co...  8.92 us
    ppermute x1, waiting for transfers between devices, body(): chip = lax.ppermute(own, 'grp', swapped('grp', 2))  7.25 us
    pallas_call x1, Pallas kernels, body(): pl.pallas_call(inner2_kernel, in_specs=[vmem] * 6 + [smem] * 2, out_shape...  6.17 us
    pallas_call x1, Pallas kernels, body(): pl.pallas_call(functools.partial(solve_kernel, total - 1.0), out_shape=ja...  6.16 us
    pallas_call x1, Pallas kernels, body(): pl.pallas_call(inner1_kernel, in_specs=[vmem, vmem, anywhere], out_shape=...  3.17 us
    pallas_call x1, Pallas kernels, body(): pl.pallas_call(functools.partial(edge2_kernel, rows), in_specs=[smem] + [...  2.91 us
  transfers between devices with their start and end apart: 19, of which 9 were waited for; matrix products, arithmetic and copies ran while one was open for 4% of the time, Pallas kernels for 39%

profile of v5, /device:TPU:22, one launch (start us, length us, event | category | flops | bytes accessed | tf_op | source)
XLA Modules:
  0.0 92.6 jit_solution(8280026532397468177)
XLA Ops:
  0.6 2.6 %prep.1 = (f32[32,2048]{1,0:T(8,128)S(1)}, f32[32,2048]{1,0:T(8,128)S(1)}, f32[3,32,2048]{2,1,0:T(8,128)S(1)}, f32[5,32,2048]{2,1,0:T(8,128)S(1)}) custom-call(s32[1]{0:T(128)} %bitcast.1.odd, f32[256,2048]{1,0:T(8,128)} %bitcast.32, f32[256,2048]{1,0:T(8,128)} %bitcast.30), custom_call_target="tpu_custom_call" | custom-call | tf_op jit(solution)/shard_map/prep/pallas_call | solution.py:409
  4.2 6.4 %collective-permute-start.1 = (f32[32,2048]{1,0:T(8,128)S(1)}, f32[32,2048]{1,0:T(8,128)S(1)}, u32[]{:S(2)}, u32[]{:S(2)}) collective-permute-start(f32[32,2048]{1,0:T(8,128)S(1)} %get-tuple-element.73), channel_id=1, source_target_pairs={{1,2},{2,1},{3,4},{4,3},{5,6},{6,5},{7,8},{8,7},{9,10},{10,9},{11,... | collective-permute-start | bytes 786440 | tf_op jit(solution)/shard_map/ppermute | solution.py:405
  11.6 3.2 %inner1.1.rho1.rho = f32[8,32,2048]{2,1,0:T(8,128)S(1)} custom-call(f32[3,32,2048]{2,1,0:T(8,128)S(1)} %get-tuple-element.133.theta_a.refs_0_, f32[5,32,2048]{2,1,0:T(8,128)S(1)} %get-tuple-element.131.theta_b.refs_4_, f32[256,2048]{1,0:T(8,128)} %bitcast.31), custom_call_target="tpu_custom_call" | custom-call | tf_op jit(solution)/shard_map/inner1/pallas_call | solution.py:421
  14.8 1.7 %convert_reduce_fusion = s32[2048]{0:T(1024)S(1)} fusion(s32[2048]{0:T(1024)S(1)} %iota_add_fusion), kind=kLoop, calls=%fused_computation.2 | loop fusion | flops 12580864 | bytes 16384 | tf_op jit(solution)/shard_map/reduce_sum | solution.py:431
  16.5 2.2 %select_reduce_fusion = s32[2048]{0:T(1024)S(1)} fusion(s32[2048]{0:T(1024)S(1)} %convert_reduce_fusion, s32[2048]{0:T(1024)S(1)} %iota_add_fusion), kind=kLoop, calls=%fused_computation | loop fusion | flops 12580864 | bytes 24576 | tf_op jit(solution)/shard_map/reduce_sum | solution.py:433
  19.6 5.2 %collective-permute-start.3 = (f32[32,2048]{1,0:T(8,128)S(1)}, f32[32,2048]{1,0:T(8,128)S(1)}, u32[]{:S(2)}, u32[]{:S(2)}) collective-permute-start(f32[32,2048]{1,0:T(8,128)S(1)} %get-tuple-element.80), channel_id=1, source_target_pairs={{1,2},{2,1},{3,4},{4,3},{5,6},{6,5},{7,8},{8,7},{9,10},{10,9},{11,... | collective-permute-start | bytes 786440 | tf_op jit(solution)/shard_map/ppermute | solution.py:405
  24.7 2.0 %collective-permute-start.4 = (f32[32,2048]{1,0:T(8,128)S(1)}, f32[32,2048]{1,0:T(8,128)S(1)}, u32[]{:S(2)}, u32[]{:S(2)}) collective-permute-start(f32[32,2048]{1,0:T(8,128)S(1)} %get-tuple-element.96), channel_id=1, source_target_pairs={{1,0},{2,1},{3,2},{4,3},{5,4},{6,5},{7,6},{8,7},{9,8},{10,9},{11,1... | collective-permute-start | bytes 786440 | tf_op jit(solution)/shard_map/ppermute | solution.py:449
  26.8 6.2 %inner2.1 = (f32[32,2048]{1,0:T(8,128)S(1)}, f32[32,2048]{1,0:T(8,128)S(1)}, f32[32,2048]{1,0:T(8,128)S(1)}, f32[32,2048]{1,0:T(8,128)S(1)}) custom-call(f32[3,32,2048]{2,1,0:T(8,128)S(1)} %get-tuple-element.133.theta_a.refs_0_, f32[5,32,2048]{2,1,0:T(8,128)S(1)} %get-tuple-element.131.theta_b.refs_4_, f32[8,32,2048]{2,1,0:T(8,128)S(1)} %inner1.1.rho1.rho, ...), custom_call_target="tpu_custom_call" | custom-call | tf_op jit(solution)/shard_map/inner2/pallas_call | solution.py:451
  33.4 2.9 %edge2.1.counts = f32[32,2048]{1,0:T(8,128)S(1)} custom-call(s32[1]{0:T(128)} %bitcast.1.odd, f32[32,2048]{1,0:T(8,128)S(1)} %get-tuple-element.93.head, f32[32,2048]{1,0:T(8,128)S(1)} %get-tuple-element.94.tail, f32[32,2048]{1,0:T(8,128)S(1)} %collective-permute-done.2.from_low, f32[32,2048]{1,0:T(8,128)S(1)} %collective-permute-done.3.from_high, ...), custom_call_target="tpu_custom_call" | custom-call | tf_op jit(solution)/shard_map/edge2/pallas_call | solution.py:460
  38.0 1.7 %finish.1.own.source = f32[32,2048]{1,0:T(8,128)S(1)} custom-call(s32[1]{0:T(128)} %bitcast.1.odd, f32[32,2048]{1,0:T(8,128)S(1)} %get-tuple-element.90.rest, f32[32,2048]{1,0:T(8,128)S(1)} %collective-permute-done.2.from_low, f32[32,2048]{1,0:T(8,128)S(1)} %collective-permute-done.3.from_high, f32[32,2048]{1,0:T(8,128)S(1)} %collective-permute-done.4.part, ...), custom_call_target="tpu_custom_call" | custom-call | tf_op jit(solution)/shard_map/finish/pallas_call | solution.py:469
  42.0 2.5 %reorder.1 = (f32[32,2048]{1,0:T(8,128)S(1)}, f32[1,2048]{1,0:T(1,128)S(1)}) custom-call(s32[1]{0:T(128)} %bitcast.g.g_ref, s32[16,128]{1,0:T(8,128)S(1)} %get-tuple-element.100.index, f32[128,2048]{1,0:T(8,128)S(1)} %copy-done, f32[1,2048]{1,0:T(1,128)S(1)} %bitcast.29), custom_call_target="tpu_custom_call" | custom-call | tf_op jit(solution)/shard_map/reorder/pallas_call | solution.py:488
  44.5 7.3 %collective-permute-done.7.chip.source = f32[32,2048]{1,0:T(8,128)S(1)} collective-permute-done((f32[32,2048]{1,0:T(8,128)S(1)}, f32[32,2048]{1,0:T(8,128)S(1)}, u32[]{:S(2)}, u32[]{:S(2)}) %collective-permute-start.7) | collective-permute-done | bytes 262176 | tf_op jit(solution)/shard_map/ppermute | solution.py:483
  53.3 2.4 %collective-permute-done.9.both.source = f32[32,2048]{1,0:T(8,128)S(1)} collective-permute-done((f32[32,2048]{1,0:T(8,128)S(1)}, f32[32,2048]{1,0:T(8,128)S(1)}, u32[]{:S(2)}, u32[]{:S(2)}) %collective-permute-start.9) | collective-permute-done | bytes 262176 | tf_op jit(solution)/shard_map/ppermute | solution.py:508
  57.2 2.2 %restore.4.core = f32[32,2048]{1,0:T(8,128)S(1)} custom-call(s32[16,128]{1,0:T(8,128)S(1)} %bitcast.25, f32[32,2048]{1,0:T(8,128)S(1)} %collective-permute-done.5.core.source), custom_call_target="tpu_custom_call" | custom-call | tf_op jit(solution)/shard_map/restore/pallas_call | solution.py:479
  59.5 1.9 %collective-permute-done.10 = f32[112,128]{1,0:T(8,128)S(1)} collective-permute-done((f32[112,128]{1,0:T(8,128)S(1)}, f32[112,128]{1,0:T(8,128)S(1)}, u32[]{:S(2)}, u32[]{:S(2)}) %collective-permute-start.10) | collective-permute-done | bytes 57376 | tf_op jit(solution)/shard_map/ppermute | solution.py:527
  61.5 2.2 %restore.5.chip = f32[32,2048]{1,0:T(8,128)S(1)} custom-call(s32[16,128]{1,0:T(8,128)S(1)} %bitcast.26, f32[32,2048]{1,0:T(8,128)S(1)} %collective-permute-done.7.chip.source), custom_call_target="tpu_custom_call" | custom-call | tf_op jit(solution)/shard_map/restore/pallas_call | solution.py:479
  63.8 3.4 %collective-permute-done.11 = f32[112,128]{1,0:T(8,128)S(1)} collective-permute-done((f32[112,128]{1,0:T(8,128)S(1)}, f32[112,128]{1,0:T(8,128)S(1)}, u32[]{:S(2)}, u32[]{:S(2)}) %collective-permute-start.11) | collective-permute-done | bytes 57376 | tf_op jit(solution)/shard_map/ppermute | solution.py:527
  67.3 2.2 %restore.6.both = f32[32,2048]{1,0:T(8,128)S(1)} custom-call(s32[16,128]{1,0:T(8,128)S(1)} %bitcast.27, f32[32,2048]{1,0:T(8,128)S(1)} %collective-permute-done.9.both.source), custom_call_target="tpu_custom_call" | custom-call | tf_op jit(solution)/shard_map/restore/pallas_call | solution.py:479
  69.5 1.9 %collective-permute-done.12 = f32[112,128]{1,0:T(8,128)S(1)} collective-permute-done((f32[112,128]{1,0:T(8,128)S(1)}, f32[112,128]{1,0:T(8,128)S(1)}, u32[]{:S(2)}, u32[]{:S(2)}) %collective-permute-start.12) | collective-permute-done | bytes 57376 | tf_op jit(solution)/shard_map/ppermute | solution.py:527
  71.9 2.2 %restore.7.own = f32[32,2048]{1,0:T(8,128)S(1)} custom-call(s32[16,128]{1,0:T(8,128)S(1)} %bitcast.28, f32[32,2048]{1,0:T(8,128)S(1)} %finish.1.own.source), custom_call_target="tpu_custom_call" | custom-call | tf_op jit(solution)/shard_map/restore/pallas_call | solution.py:479
  74.1 3.1 %collective-permute-done.13 = f32[112,128]{1,0:T(8,128)S(1)} collective-permute-done((f32[112,128]{1,0:T(8,128)S(1)}, f32[112,128]{1,0:T(8,128)S(1)}, u32[]{:S(2)}, u32[]{:S(2)}) %collective-permute-start.13) | collective-permute-done | bytes 57376 | tf_op jit(solution)/shard_map/ppermute | solution.py:527
  79.9 3.1 %collective-permute-done.14 = f32[112,128]{1,0:T(8,128)S(1)} collective-permute-done((f32[112,128]{1,0:T(8,128)S(1)}, f32[112,128]{1,0:T(8,128)S(1)}, u32[]{:S(2)}, u32[]{:S(2)}) %collective-permute-start.14) | collective-permute-done | bytes 57376 | tf_op jit(solution)/shard_map/ppermute | solution.py:527
  83.6 6.2 %solve.1.mixing = f32[32,128]{1,0:T(8,128)S(1)} custom-call(f32[112,128]{1,0:T(8,128)S(1)} %add.25.packed), custom_call_target="tpu_custom_call" | custom-call | tf_op jit(solution)/shard_map/solve/pallas_call | solution.py:565
  89.8 2.7 %update.1 = f32[256,2048]{1,0:T(8,128)} custom-call(s32[1]{0:T(128)} %bitcast.g.g_ref, f32[32,128]{1,0:T(8,128)S(1)} %solve.1.mixing, f32[3,32,2048]{2,1,0:T(8,128)S(1)} %get-tuple-element.133.theta_a.refs_0_, f32[3,32,2048]{2,1,0:T(8,128)S(1)} %collective-permute-done.16.refs_1_, f32[3,32,2048]{2,1,0:T(8,128)S(1)} %hold.1.refs_2_, ...), custom_call_target="tpu_custom_call" | custom-call | tf_op jit(solution)/shard_map/update/pallas_call | solution.py:571
  (46 shorter events, 14.2 us)
Async XLA Ops:
  3.3 15.7 %collective-permute-start = (f32[32,2048]{1,0:T(8,128)S(1)}, f32[32,2048]{1,0:T(8,128)S(1)}, u32[]{:S(2)}, u32[]{:S(2)}) collective-permute-start(f32[32,2048]{1,0:T(8,128)S(1)} %get-tuple-element.72), channel_id=1, source_target_pairs={{0,1},{1,0},{2,3},{3,2},{4,5},{5,4},{6,7},{7,6},{8,9},{9,8},{10,11... | collective-permute-start | bytes 786440 | tf_op jit(solution)/shard_map/ppermute | solution.py:404
  4.2 14.8 %collective-permute-start.1 = (f32[32,2048]{1,0:T(8,128)S(1)}, f32[32,2048]{1,0:T(8,128)S(1)}, u32[]{:S(2)}, u32[]{:S(2)}) collective-permute-start(f32[32,2048]{1,0:T(8,128)S(1)} %get-tuple-element.73), channel_id=1, source_target_pairs={{1,2},{2,1},{3,4},{4,3},{5,6},{6,5},{7,8},{8,7},{9,10},{10,9},{11,... | collective-permute-start | bytes 786440 | tf_op jit(solution)/shard_map/ppermute | solution.py:405
  10.5 41.3 %collective-permute-start.6 = (f32[3,32,2048]{2,1,0:T(8,128)S(1)}, f32[3,32,2048]{2,1,0:T(8,128)}, u32[]{:S(2)}, u32[]{:S(2)}) collective-permute-start(f32[3,32,2048]{2,1,0:T(8,128)S(1)} %get-tuple-element.133.theta_a.refs_0_), channel_id=1, source_target_pairs={{0,64},{32,96},{64,0},{96,32},{1,65},{33,97},{65,1},{97,33},{2,66}... | collective-permute-start | bytes 2359304 | tf_op jit(solution)/shard_map/ppermute | solution.py:418
  11.6 3.2 %slice-start = ((s32[2048,8]{0,1:T(8,128)}), s32[2048,1]{0,1:T(1,128)S(1)}, s32[]{:S(2)}) async-start(s32[2048,8]{0,1:T(8,128)} %param.7), calls=%async_computation | async-start | bytes 16384 | tf_op jit(solution)/shard_map/slice | solution.py:420
  19.5 13.5 %collective-permute-start.2 = (f32[32,2048]{1,0:T(8,128)S(1)}, f32[32,2048]{1,0:T(8,128)S(1)}, u32[]{:S(2)}, u32[]{:S(2)}) collective-permute-start(f32[32,2048]{1,0:T(8,128)S(1)} %get-tuple-element.79), channel_id=1, source_target_pairs={{0,1},{1,0},{2,3},{3,2},{4,5},{5,4},{6,7},{7,6},{8,9},{9,8},{10,11... | collective-permute-start | bytes 786440 | tf_op jit(solution)/shard_map/ppermute | solution.py:404
  19.6 13.9 %collective-permute-start.3 = (f32[32,2048]{1,0:T(8,128)S(1)}, f32[32,2048]{1,0:T(8,128)S(1)}, u32[]{:S(2)}, u32[]{:S(2)}) collective-permute-start(f32[32,2048]{1,0:T(8,128)S(1)} %get-tuple-element.80), channel_id=1, source_target_pairs={{1,2},{2,1},{3,4},{4,3},{5,6},{6,5},{7,8},{8,7},{9,10},{10,9},{11,... | collective-permute-start | bytes 786440 | tf_op jit(solution)/shard_map/ppermute | solution.py:405
  24.7 13.2 %collective-permute-start.4 = (f32[32,2048]{1,0:T(8,128)S(1)}, f32[32,2048]{1,0:T(8,128)S(1)}, u32[]{:S(2)}, u32[]{:S(2)}) collective-permute-start(f32[32,2048]{1,0:T(8,128)S(1)} %get-tuple-element.96), channel_id=1, source_target_pairs={{1,0},{2,1},{3,2},{4,3},{5,4},{6,5},{7,6},{8,7},{9,8},{10,9},{11,1... | collective-permute-start | bytes 786440 | tf_op jit(solution)/shard_map/ppermute | solution.py:449
  32.9 7.9 %copy-start.1 = (f32[2048]{0:T(1024)S(1)}, f32[2048]{0:T(1024)}, u32[]{:S(2)}) copy-start(f32[2048]{0:T(1024)} %param.9) | copy-start | bytes 24580
  39.7 12.1 %collective-permute-start.7 = (f32[32,2048]{1,0:T(8,128)S(1)}, f32[32,2048]{1,0:T(8,128)S(1)}, u32[]{:S(2)}, u32[]{:S(2)}) collective-permute-start(f32[32,2048]{1,0:T(8,128)S(1)} %finish.1.own.source), channel_id=1, source_target_pairs={{0,64},{32,96},{64,0},{96,32},{1,65},{33,97},{65,1},{97,33},{2,66}... | collective-permute-start | bytes 786440 | tf_op jit(solution)/shard_map/ppermute | solution.py:483
  40.8 11.0 %collective-permute-start.5 = (f32[32,2048]{1,0:T(8,128)S(1)}, f32[32,2048]{1,0:T(8,128)S(1)}, u32[]{:S(2)}, u32[]{:S(2)}) collective-permute-start(f32[32,2048]{1,0:T(8,128)S(1)} %finish.1.own.source), channel_id=1, source_target_pairs={{0,32},{32,0},{64,96},{96,64},{1,33},{33,1},{65,97},{97,65},{2,34}... | collective-permute-start | bytes 786440 | tf_op jit(solution)/shard_map/ppermute | solution.py:484
  40.8 1.2 %copy-start = (f32[128,2048]{1,0:T(8,128)S(1)}, f32[128,2048]{1,0:T(8,128)}, u32[]{:S(2)}) copy-start(f32[128,2048]{1,0:T(8,128)} %source) | copy-start | bytes 3145732
  51.8 31.2 %collective-permute-start.15 = (f32[5,32,2048]{2,1,0:T(8,128)S(1)}, f32[5,32,2048]{2,1,0:T(8,128)S(1)}, u32[]{:S(2)}, u32[]{:S(2)}) collective-permute-start(f32[5,32,2048]{2,1,0:T(8,128)S(1)} %get-tuple-element.131.theta_b.refs_4_), channel_id=1, source_target_pairs={{0,64},{32,96},{64,0},{96,32},{1,65},{33,97},{65,1},{97,33},{2,66}... | collective-permute-start | bytes 3932168 | tf_op jit(solution)/shard_map/ppermute | solution.py:510
  52.8 25.9 %collective-permute-start.8 = (f32[3,32,2048]{2,1,0:T(8,128)}, f32[3,32,2048]{2,1,0:T(8,128)S(1)}, u32[]{:S(2)}, u32[]{:S(2)}) collective-permute-start(f32[3,32,2048]{2,1,0:T(8,128)} %collective-permute-done.6.source), channel_id=1, source_target_pairs={{0,32},{32,0},{64,96},{96,64},{1,33},{33,1},{65,97},{97,65},{2,34}... | collective-permute-start | bytes 2359304 | tf_op jit(solution)/shard_map/ppermute | solution.py:511
  52.8 2.9 %collective-permute-start.9 = (f32[32,2048]{1,0:T(8,128)S(1)}, f32[32,2048]{1,0:T(8,128)S(1)}, u32[]{:S(2)}, u32[]{:S(2)}) collective-permute-start(f32[32,2048]{1,0:T(8,128)S(1)} %collective-permute-done.7.chip.source), channel_id=1, source_target_pairs={{0,32},{32,0},{64,96},{96,64},{1,33},{33,1},{65,97},{97,65},{2,34}... | collective-permute-start | bytes 786440 | tf_op jit(solution)/shard_map/ppermute | solution.py:508
  57.2 4.2 %collective-permute-start.10 = (f32[112,128]{1,0:T(8,128)S(1)}, f32[112,128]{1,0:T(8,128)S(1)}, u32[]{:S(2)}, u32[]{:S(2)}) collective-permute-start(f32[112,128]{1,0:T(8,128)S(1)} %product.1), channel_id=1, source_target_pairs={{0,1},{1,0},{2,3},{3,2},{4,5},{5,4},{6,7},{7,6},{8,9},{9,8},{10,11... | collective-permute-start | bytes 172040 | tf_op jit(solution)/shard_map/ppermute | solution.py:527
  61.4 5.8 %collective-permute-start.11 = (f32[112,128]{1,0:T(8,128)S(1)}, f32[112,128]{1,0:T(8,128)S(1)}, u32[]{:S(2)}, u32[]{:S(2)}) collective-permute-start(f32[112,128]{1,0:T(8,128)S(1)} %add.21), channel_id=1, source_target_pairs={{0,2},{1,3},{2,0},{3,1},{4,6},{5,7},{6,4},{7,5},{8,10},{9,11},{10,... | collective-permute-start | bytes 172040 | tf_op jit(solution)/shard_map/ppermute | solution.py:527
  67.2 4.3 %collective-permute-start.12 = (f32[112,128]{1,0:T(8,128)S(1)}, f32[112,128]{1,0:T(8,128)S(1)}, u32[]{:S(2)}, u32[]{:S(2)}) collective-permute-start(f32[112,128]{1,0:T(8,128)S(1)} %add.22), channel_id=1, source_target_pairs={{0,8},{1,9},{2,10},{3,11},{4,12},{5,13},{6,14},{7,15},{8,0},{9,1},... | collective-permute-start | bytes 172040 | tf_op jit(solution)/shard_map/ppermute | solution.py:527
  71.5 5.8 %collective-permute-start.13 = (f32[112,128]{1,0:T(8,128)S(1)}, f32[112,128]{1,0:T(8,128)S(1)}, u32[]{:S(2)}, u32[]{:S(2)}) collective-permute-start(f32[112,128]{1,0:T(8,128)S(1)} %add.23), channel_id=1, source_target_pairs={{0,16},{1,17},{2,18},{3,19},{4,20},{5,21},{6,22},{7,23},{8,24},{9,... | collective-permute-start | bytes 172040 | tf_op jit(solution)/shard_map/ppermute | solution.py:527
  77.2 5.8 %collective-permute-start.14 = (f32[112,128]{1,0:T(8,128)S(1)}, f32[112,128]{1,0:T(8,128)S(1)}, u32[]{:S(2)}, u32[]{:S(2)}) collective-permute-start(f32[112,128]{1,0:T(8,128)S(1)} %add.24), channel_id=1, source_target_pairs={{0,4},{1,5},{2,6},{3,7},{4,0},{5,1},{6,2},{7,3},{8,12},{9,13},{10,... | collective-permute-start | bytes 172040 | tf_op jit(solution)/shard_map/ppermute | solution.py:527
  77.7 12.1 %collective-permute-start.17 = (f32[5,32,2048]{2,1,0:T(8,128)S(1)}, f32[5,32,2048]{2,1,0:T(8,128)S(1)}, u32[]{:S(2)}, u32[]{:S(2)}) collective-permute-start(f32[5,32,2048]{2,1,0:T(8,128)S(1)} %get-tuple-element.131.theta_b.refs_4_), channel_id=1, source_target_pairs={{0,32},{32,0},{64,96},{96,64},{1,33},{33,1},{65,97},{97,65},{2,34}... | collective-permute-start | bytes 3932168 | tf_op jit(solution)/shard_map/ppermute | solution.py:487
  83.0 6.8 %collective-permute-start.18 = (f32[5,32,2048]{2,1,0:T(8,128)S(1)}, f32[5,32,2048]{2,1,0:T(8,128)S(1)}, u32[]{:S(2)}, u32[]{:S(2)}) collective-permute-start(f32[5,32,2048]{2,1,0:T(8,128)S(1)} %collective-permute-done.15.refs_6_), channel_id=1, source_target_pairs={{0,32},{32,0},{64,96},{96,64},{1,33},{33,1},{65,97},{97,65},{2,34}... | collective-permute-start | bytes 3932168 | tf_op jit(solution)/shard_map/ppermute | solution.py:564
  83.1 6.7 %collective-permute-start.16 = (f32[3,32,2048]{2,1,0:T(8,128)S(1)}, f32[3,32,2048]{2,1,0:T(8,128)S(1)}, u32[]{:S(2)}, u32[]{:S(2)}) collective-permute-start(f32[3,32,2048]{2,1,0:T(8,128)S(1)} %get-tuple-element.133.theta_a.refs_0_), channel_id=1, source_target_pairs={{0,32},{32,0},{64,96},{96,64},{1,33},{33,1},{65,97},{97,65},{2,34}... | collective-permute-start | bytes 2359304 | tf_op jit(solution)/shard_map/ppermute | solution.py:486
